TPU v7x, 32 devices: a whole 2x2x4 slice. The times are simulated.
32 devices in a mesh: beam: 8 (over z, y), fft: 4 (over x, core).
Axes of the slice: x: 2, y: 2, z: 4, core: 2. Of those that a mesh axis runs over, the one named last changes fastest.
Arguments:
- sky_model: bfloat16 [128, 512, 512], P('beam', 'fft'), may hold values from -6 to 6
- footprint: int32 [8, 64], replicated, may hold values from 0 to 127, as said below
- profile: float32 [8, 8, 2, 4096], P('beam'), may hold values from 0.25 to 1
- chan_block: int32 [8], P('beam'), may hold values from 0 to 7
- sub_strip: int32 [8, 128, 1], P('beam'), may hold values from 0 to 3; in each aligned block of 32 rows (0 to 31, 32 to 63, ..., all dimensions but the last counted through in order) at most 16 rows name the same one
- sub_row: int32 [8, 128], P('beam'), may hold values from 0 to 4064
- sub_col: int32 [8, 128], P('beam'), may hold values from 0 to 992
- offsets: float32 [8, 128, 2, 256], P('beam'), may hold values from 2 to 29
- sub_base: int32 [8, 128], P('beam'), may hold values from 0 to 629
- gain_table: float32 [2, 630], replicated, may hold values from -3 to 3
Outputs:
- visibilities: float32 [8, 128, 2, 256], P('beam', 'fft')
Inputs may be any that keep to these rules, and one draw needn't show every extreme that they name: `footprint`: each beam's list names 64 distinct sky tiles; entry i * 8 + j is the tile at tile row i and tile column j of the beam's image. At most 8 entries of one list lie in one block of 16 consecutive tile numbers, and every list reaches that. `sub_strip`: in each aligned block of 32 subgrids of a beam, at most 16 lie in one strip; some block reaches it.
All inputs are finite; a program needn't handle non-finite values.
Results may differ from a plain program's by a relative error of at most 0.0045.
Values may be sent and summed in bfloat16 or wider, within the bound.
No kernel may reach another device: no remote copies, remote signals or barrier semaphores. Data moves between devices by JAX's collectives and lax.ppermute only.
A program may use at most 192 MiB of HBM per device.

v0:
```python
import math

import jax
import jax.numpy as jnp
from jax import lax
from jax.sharding import PartitionSpec as P

FT = 8
SG = 32


kernel_width = 1.5
highest = lax.Precision.HIGHEST


def dft_tables(size_out, size_in, period):
    product = (
        jnp.arange(size_out, dtype=jnp.int32)[:, None]
        * jnp.arange(size_in, dtype=jnp.int32)[None, :]
        % period
    )
    angle = product.astype(jnp.float32) * (2.0 * math.pi / period)
    return (jnp.cos(angle), -jnp.sin(angle))


def complex_table(cos_t, sin_t):
    upper_half = jnp.concatenate([cos_t, sin_t], axis=1)
    lower_half = jnp.concatenate([-sin_t, cos_t], axis=1)
    return jnp.concatenate([upper_half, lower_half], axis=0)


def split_table(table):
    upper = table.astype(jnp.bfloat16)
    rest = table - upper.astype(jnp.float32)
    middle = rest.astype(jnp.bfloat16)
    lower = (rest - middle.astype(jnp.float32)).astype(jnp.bfloat16)
    return (upper, middle, lower)


def bf16_times_table(folded, table):
    pieces = split_table(table)
    total = jnp.einsum("pqv,pk->kqv", folded, pieces[0], preferred_element_type=jnp.float32)
    total = total + jnp.einsum("pqv,pk->kqv", folded, pieces[1], preferred_element_type=jnp.float32)
    return total + jnp.einsum("pqv,pk->kqv", folded, pieces[2], preferred_element_type=jnp.float32)


def split_length(length):
    outer_len = 1 << (length.bit_length() - 1) // 2
    return (outer_len, length // outer_len)


def transform_rows(real_in):
    row_count, length = real_in.shape
    outer_len, inner_len = split_length(length)
    folded = real_in.reshape(row_count, outer_len, inner_len)
    cos_one, sin_one = dft_tables(outer_len, outer_len, outer_len)
    both = jnp.einsum(
        "rpq,pk->rkq", folded, jnp.concatenate([cos_one, sin_one], axis=1), precision=highest
    )
    part_re = both[:, :outer_len]
    part_im = both[:, outer_len:]
    turn_cos, turn_sin = dft_tables(outer_len, inner_len, length)
    turned_re = part_re * turn_cos[None] - part_im * turn_sin[None]
    turned_im = part_re * turn_sin[None] + part_im * turn_cos[None]
    cos_two, sin_two = dft_tables(inner_len, inner_len, inner_len)
    stacked = jnp.concatenate([turned_re, turned_im], axis=2)
    result = jnp.einsum("rkq,qm->rmk", stacked, complex_table(cos_two, sin_two), precision=highest)
    out_re = result[:, :inner_len]
    out_im = result[:, inner_len:]
    return (out_re.reshape(row_count, length), out_im.reshape(row_count, length))


def transform_columns(field_re, field_im):
    length, col_count = field_re.shape
    outer_len, inner_len = split_length(length)
    stacked_in = jnp.concatenate(
        [
            field_re.reshape(outer_len, inner_len, col_count),
            field_im.reshape(outer_len, inner_len, col_count),
        ],
        axis=0,
    )
    cos_one, sin_one = dft_tables(outer_len, outer_len, outer_len)
    both = bf16_times_table(stacked_in, complex_table(cos_one, sin_one))
    part_re = both[:outer_len]
    part_im = both[outer_len:]
    turn_cos, turn_sin = dft_tables(outer_len, inner_len, length)
    turned_re = part_re * turn_cos[:, :, None] - part_im * turn_sin[:, :, None]
    turned_im = part_re * turn_sin[:, :, None] + part_im * turn_cos[:, :, None]
    cos_two, sin_two = dft_tables(inner_len, inner_len, inner_len)
    stacked = jnp.concatenate([turned_re, turned_im], axis=1)
    result = jnp.einsum("kqv,qm->mkv", stacked, complex_table(cos_two, sin_two), precision=highest)
    out_re = result[:inner_len]
    out_im = result[inner_len:]
    return (out_re.reshape(length, col_count), out_im.reshape(length, col_count))


def order_within(labels, label_count):
    hot_table = (
        labels[:, :, None] == jnp.arange(label_count, dtype=jnp.int32)[None, None, :]
    ).astype(jnp.int32)
    return jnp.sum((jnp.cumsum(hot_table, axis=1) - 1) * hot_table, axis=2)


def cut_blocks(field, first_rows, first_cols):

    def cut_one(row_at, col_at):
        return lax.dynamic_slice(field, (row_at, col_at), (SG, SG))

    return jax.vmap(cut_one)(first_rows, first_cols)


def degrid_blocks(cut_re, cut_im, sample_pos, base_ids, gain_table):
    places = jnp.arange(SG, dtype=jnp.float32)
    weight_u = jnp.exp(
        -jnp.square((places[None, None, :] - sample_pos[:, 0, :, None]) / kernel_width)
    )
    weight_v = jnp.exp(
        -jnp.square((places[None, None, :] - sample_pos[:, 1, :, None]) / kernel_width)
    )
    inner_re = jnp.einsum("bna,bac->bnc", weight_u, cut_re, precision=highest)
    inner_im = jnp.einsum("bna,bac->bnc", weight_u, cut_im, precision=highest)
    summed_re = jnp.sum(inner_re * weight_v, axis=-1)
    summed_im = jnp.sum(inner_im * weight_v, axis=-1)
    base_hot = (
        base_ids[:, None] == jnp.arange(gain_table.shape[1], dtype=jnp.int32)[None, :]
    ).astype(jnp.float32)
    picked_gain = jnp.dot(base_hot, gain_table.T, precision=highest)
    gain_re = picked_gain[:, 0:1]
    gain_im = picked_gain[:, 1:2]
    out_re = gain_re * summed_re - gain_im * summed_im
    out_im = gain_re * summed_im + gain_im * summed_re
    return jnp.stack([out_re, out_im], axis=1)


def local(
    sky_model,
    footprint,
    profile,
    chan_block,
    sub_strip,
    sub_row,
    sub_col,
    offsets,
    sub_base,
    gain_table,
):
    fft_count = lax.axis_size("fft")
    my_beam = lax.axis_index("beam")
    my_fft = lax.axis_index("fft")
    tiles_dev, tile_rows, tile_side = sky_model.shape
    gathered = lax.all_gather(sky_model, "beam", axis=0, tiled=True)
    fetched = jnp.take(
        gathered, lax.dynamic_index_in_dim(footprint, my_beam, 0, keepdims=False), axis=0
    )
    image_side = FT * tile_side
    arranged = (
        fetched.reshape(FT, FT, tile_rows, tile_side)
        .transpose(0, 2, 1, 3)
        .reshape(FT * tile_rows, image_side)
    )
    channel_pick = (jnp.arange(profile.shape[1], dtype=jnp.int32) == chan_block[0]).astype(
        jnp.float32
    )
    chosen_prof = jnp.einsum("c,cax->ax", channel_pick, profile[0], precision=highest)
    prof_rows = lax.dynamic_slice_in_dim(
        chosen_prof[0].reshape(FT, tile_side), my_fft * tile_rows, tile_rows, 1
    ).reshape(-1)
    sky_image = arranged.astype(jnp.float32) * prof_rows[:, None] * chosen_prof[1][None, :]
    norm_scale = 1.0 / math.sqrt(image_side)
    spec_re, spec_im = transform_rows(sky_image)
    spec_re = (spec_re * norm_scale).astype(jnp.bfloat16).reshape(FT, tile_rows, image_side)
    spec_im = (spec_im * norm_scale).astype(jnp.bfloat16).reshape(FT, tile_rows, image_side)
    moved_re, moved_im = (
        lax.all_to_all(spec_re, "fft", split_axis=2, concat_axis=1, tiled=True),
        lax.all_to_all(spec_im, "fft", split_axis=2, concat_axis=1, tiled=True),
    )
    strip_cols = moved_re.shape[2]
    grid_re, grid_im = transform_columns(
        moved_re.reshape(image_side, strip_cols), moved_im.reshape(image_side, strip_cols)
    )
    grid_re = grid_re * norm_scale
    grid_im = grid_im * norm_scale
    strip_of = sub_strip[0, :, 0]
    first_rows = sub_row[0]
    first_cols = sub_col[0]
    base_ids = sub_base[0]
    sample_pos = offsets[0]
    sub_total = strip_of.shape[0]
    sub_dev = sub_total // fft_count
    pair_cap = sub_dev // 2
    strip_blocks = strip_of.reshape(fft_count, sub_dev)
    strip_order = order_within(strip_blocks, fft_count)
    slot_hits = (
        (strip_blocks == my_fft)[:, :, None]
        & (strip_order[:, :, None] == jnp.arange(pair_cap, dtype=jnp.int32)[None, None, :])
    ).astype(jnp.int32)
    slot_local = jnp.sum(slot_hits * jnp.arange(sub_dev, dtype=jnp.int32)[None, :, None], axis=1)
    send_ids = (slot_local + jnp.arange(fft_count, dtype=jnp.int32)[:, None] * sub_dev).reshape(-1)
    my_strips = lax.dynamic_index_in_dim(strip_blocks, my_fft, 0, keepdims=False)
    my_orders = lax.dynamic_index_in_dim(strip_order, my_fft, 0, keepdims=False)
    pick_slot = my_strips * pair_cap + my_orders
    sent_re = cut_blocks(grid_re, jnp.take(first_rows, send_ids), jnp.take(first_cols, send_ids))
    sent_im = cut_blocks(grid_im, jnp.take(first_rows, send_ids), jnp.take(first_cols, send_ids))
    slot_values = degrid_blocks(
        sent_re,
        sent_im,
        jnp.take(sample_pos, send_ids, axis=0),
        jnp.take(base_ids, send_ids),
        gain_table,
    )
    came_back = lax.all_to_all(slot_values, "fft", split_axis=0, concat_axis=0, tiled=True)
    predicted = jnp.take(came_back, pick_slot, axis=0)
    return predicted[None]


def solution(mesh):
    return jax.shard_map(
        local,
        mesh=mesh,
        in_specs=(
            P("beam", "fft", None),
            P(),
            P("beam", None, None, None),
            P("beam"),
            P("beam", None, None),
            P("beam", None),
            P("beam", None),
            P("beam", None, None, None),
            P("beam", None),
            P(),
        ),
        out_specs=P("beam", "fft", None, None),
        check_vma=False,
    )
```

profile of v0, /device:TPU:1, one launch (start us, length us, event | category | flops | bytes accessed | tf_op | source)
XLA Modules:
  0.0 1308.4 jit_solution(2222570117738291984)
XLA Ops:
  11.9 226.9 %all-gather.2.cloned.1.call-done = bf16[128,128,512]{2,1,0:T(8,128)(2,1)} async-done(((bf16[16,128,512]{2,1,0:T(8,128)(2,1)}), bf16[128,128,512]{2,1,0:T(8,128)(2,1)}) %all-gather.2.cloned.1.call-update) | async-done | bytes 16777232 | tf_op jit(solution)/shard_map/all_gather | solution.py:152
  238.8 11.3 gather_fusion.1
  250.1 12.9 copy.73
  263.0 10.3 convert_bitcast_fusion
  273.3 18.0 %reshape.425 = f32[1024,64,64]{0,2,1:T(8,128)} reshape(f32[8,128,8,512]{1,0,3,2:T(8,128)} %convert_bitcast_fusion) | data formatting | bytes 33554432 | tf_op jit(solution)/shard_map/convert_element_type | solution.py:169
  291.3 6.8 multiply_multiply_fusion
  298.1 37.9 %fusion.8 = f32[1024,128,64]{0,1,2:T(8,128)} fusion(f32[1024,64,64]{0,2,1:T(8,128)S(1)} %multiply_multiply_fusion, f32[64,64]{1,0:T(8,128)S(1)} %get-tuple-element.67, f32[64,64]{1,0:T(8,128)S(1)} %get-tuple-element.66), kind=kOutput, calls=%fused_computation.31 | convolution fusion | flops 6442459136 | bytes 50364416 | tf_op jit(solution)/shard_map/rpq,pk->rkq/dot_general | solution.py:57
  336.0 17.6 %multiply_subtract_fusion.1 = (f32[1024,64,64]{0,1,2:T(8,128)S(1)}, f32[1024,64,64]{0,1,2:T(8,128)}) fusion(f32[1024,128,64]{0,1,2:T(8,128)} %fusion.8, f32[64,64]{0,1:T(8,128)S(1)} %copy.76, f32[64,64]{0,1:T(8,128)S(1)} %copy.75), kind=kLoop, calls=%fused_computation.29 | loop fusion | flops 25165824 | bytes 67141632 | tf_op jit(solution)/shard_map/sub | solution.py:63
  353.7 18.8 %pad_maximum_fusion = f32[1024,64,128]{0,1,2:T(8,128)} fusion(f32[1024,64,64]{0,1,2:T(8,128)} %get-tuple-element.51, f32[1024,64,64]{0,1,2:T(8,128)S(1)} %get-tuple-element.50), kind=kLoop, calls=%fused_computation.10 | loop fusion | flops 8388608 | bytes 67108864 | tf_op jit(solution)/shard_map/concatenate | solution.py:66
  372.5 58.6 %fusion.11 = f32[1024,128,64]{0,1,2:T(8,128)} fusion(f32[1024,64,128]{0,1,2:T(8,128)} %pad_maximum_fusion, f32[64,64]{1,0:T(8,128)S(1)} %get-tuple-element.66, f32[64,64]{1,0:T(8,128)S(1)} %fusion.49, f32[64,64]{1,0:T(8,128)S(1)} %get-tuple-element.67), kind=kOutput, calls=%fused_computation.32 | convolution fusion | flops 12884951040 | bytes 67158016 | tf_op jit(solution)/shard_map/rkq,qm->rmk/dot_general | solution.py:67
  431.1 17.0 %fusion.4 = (bf16[1024,64,64]{0,1,2:T(8,128)(2,1)}, bf16[1024,64,64]{0,1,2:T(8,128)(2,1)}) fusion(f32[1024,128,64]{0,1,2:T(8,128)} %fusion.11), kind=kLoop, calls=%fused_computation.20 | loop fusion | flops 16777216 | bytes 50331648 | tf_op jit(solution)/shard_map/convert_element_type | solution.py:173
  448.1 11.3 copy.79
  459.4 8.8 copy.112
  468.2 6.9 all-to-all-start
  475.1 11.3 copy.81
  486.5 8.8 copy.113
  495.3 72.1 %all-to-all-done = bf16[8,128,4096]{1,0,2:T(8,128)(2,1)} async-done(((bf16[8,128,4096]{1,0,2:T(8,128)(2,1)}), bf16[8,128,4096]{1,0,2:T(8,128)(2,1)}, u32[]{:S(2)}, u32[]{:S(2)}) %all-to-all-start) | async-done | bytes 8388640 | tf_op jit(solution)/shard_map/all_to_all | solution.py:175
  567.4 6.8 all-to-all-start.1
  583.4 12.2 copy.80
  595.6 11.4 copy_dynamic-update-slice_fusion.1
  607.0 59.6 %all-to-all-done.1 = bf16[8,128,4096]{1,0,2:T(8,128)(2,1)} async-done(((bf16[8,128,4096]{1,0,2:T(8,128)(2,1)}), bf16[8,128,4096]{1,0,2:T(8,128)(2,1)}, u32[]{:S(2)}, u32[]{:S(2)}) %all-to-all-start.1) | async-done | bytes 8388640 | tf_op jit(solution)/shard_map/all_to_all | solution.py:176
  666.6 23.4 %copy.82 = bf16[8,128,4,1024]{3,1,2,0:T(8,128)(2,1)} copy(bf16[8,128,4,1024]{1,0,3,2:T(8,128)(2,1)} %bitcast.23) | data formatting | bytes 16777216 | tf_op jit(solution)/shard_map/all_to_all | solution.py:176
  690.0 11.3 copy_dynamic-update-slice_fusion
  701.3 21.5 %fusion.29 = f32[128,64,1024]{2,0,1:T(8,128)} fusion(bf16[128,64,1024]{2,0,1:T(8,128)(2,1)} %copy_dynamic-update-slice_fusion, f32[64,64]{1,0:T(8,128)S(1)} %get-tuple-element.66, f32[64,64]{1,0:T(8,128)S(1)} %fusion.49, f32[64,64]{1,0:T(8,128)S(1)} %get-tuple-element.67), kind=kOutput, calls=%fused_computation.73 | convolution fusion | flops 2147598336 | bytes 50380800 | tf_op jit(solution)/shard_map/pqv,pk->kqv/dot_general | solution.py:43
  722.8 21.5 %fusion.31 = f32[128,64,1024]{2,0,1:T(8,128)} fusion(bf16[128,64,1024]{2,0,1:T(8,128)(2,1)} %copy_dynamic-update-slice_fusion, f32[64,64]{1,0:T(8,128)S(1)} %get-tuple-element.66, f32[64,64]{1,0:T(8,128)S(1)} %fusion.49, f32[64,64]{1,0:T(8,128)S(1)} %get-tuple-element.67), kind=kOutput, calls=%fused_computation.74 | convolution fusion | flops 2147614720 | bytes 50380800 | tf_op jit(solution)/shard_map/pqv,pk->kqv/dot_general | solution.py:42
  744.2 38.8 %add_add_fusion = f32[128,64,1024]{2,0,1:T(8,128)} fusion(f32[128,64,1024]{2,0,1:T(8,128)} %fusion.31, f32[128,64,1024]{2,0,1:T(8,128)} %fusion.29, bf16[128,64,1024]{2,0,1:T(8,128)(2,1)} %copy_dynamic-update-slice_fusion, f32[64,64]{1,0:T(8,128)S(1)} %get-tuple-element.66, f32[64,64]{1,0:T(8,128)S(1)} %fusion.49, f32[64,64]{1,0:T(8,128)S(1)} %get-tuple-element.67), kind=kOutput, calls=%fused_computation.16 | convolution fusion | flops 2164424704 | bytes 117489664 | tf_op jit(solution)/shard_map/pqv,pk->kqv/dot_general | solution.py:44
  783.1 17.7 %multiply_subtract_fusion = (f32[64,64,1024]{2,0,1:T(8,128)S(1)}, f32[64,64,1024]{2,0,1:T(8,128)}) fusion(f32[128,64,1024]{2,0,1:T(8,128)} %add_add_fusion, f32[64,64]{0,1:T(8,128)S(1)} %copy-done.8, f32[64,64]{0,1:T(8,128)S(1)} %copy-done.6), kind=kLoop, calls=%fused_computation.27 | loop fusion | flops 25165824 | bytes 67141632 | tf_op jit(solution)/shard_map/sub | solution.py:88
  800.8 18.8 %pad_maximum_fusion.1 = f32[64,128,1024]{2,0,1:T(8,128)} fusion(f32[64,64,1024]{2,0,1:T(8,128)} %get-tuple-element.49, f32[64,64,1024]{2,0,1:T(8,128)S(1)} %get-tuple-element.48), kind=kLoop, calls=%fused_computation.11 | loop fusion | flops 8388608 | bytes 67108864 | tf_op jit(solution)/shard_map/concatenate | solution.py:91
  819.6 58.6 %fusion = f32[128,64,1024]{2,0,1:T(8,128)} fusion(f32[64,128,1024]{2,0,1:T(8,128)} %pad_maximum_fusion.1, f32[64,64]{1,0:T(8,128)S(1)} %get-tuple-element.66, f32[64,64]{1,0:T(8,128)S(1)} %fusion.49, f32[64,64]{1,0:T(8,128)S(1)} %get-tuple-element.67), kind=kOutput, calls=%fused_computation.12 | convolution fusion | flops 12884951040 | bytes 67158016 | tf_op jit(solution)/shard_map/kqv,qm->mkv/dot_general | solution.py:92
  878.3 17.2 %slice_multiply_fusion.1 = (f32[64,64,1024]{2,0,1:T(8,128)S(1)}, f32[64,64,1024]{2,0,1:T(8,128)}) fusion(f32[128,64,1024]{2,0,1:T(8,128)} %fusion), kind=kLoop, calls=%fused_computation.18 | loop fusion | flops 8388608 | bytes 67108864 | tf_op jit(solution)/shard_map/mul | solution.py:182
  895.5 19.1 %copy.92 = f32[64,64,1024]{2,1,0:T(8,128)} copy(f32[64,64,1024]{2,0,1:T(8,128)S(1)} %get-tuple-element.52) | data formatting | bytes 33554432 | tf_op jit(solution)/shard_map/mul | solution.py:182
  914.7 176.6 %while.2 = (s32[]{:T(128)}, f32[4096,1024]{1,0:T(8,128)}, s32[64,2]{0,1:T(2,128)S(1)}, f32[64,32,32]{2,1,0:T(8,128)S(1)}, s32[]{:T(128)}) while((s32[]{:T(128)}, f32[4096,1024]{1,0:T(8,128)}, s32[64,2]{0,1:T(2,128)S(1)}, f32[64,32,32]{2,1,0:T(8,128)S(1)}, s32[]{:T(128)}) %tuple.57), condition=%wide.while_cond, body=%wide.while_body.sunk | while | flops 2 | bytes 20589 | solution.py:108
  918.1 2.1 bitcast_dynamic-update-slice_fusion.4
  920.9 2.1 bitcast_dynamic-update-slice_fusion.4
  923.6 2.1 bitcast_dynamic-update-slice_fusion.4
  926.4 2.1 bitcast_dynamic-update-slice_fusion.4
  929.2 2.1 bitcast_dynamic-update-slice_fusion.4
  940.2 2.1 bitcast_dynamic-update-slice_fusion.4
  945.8 2.1 bitcast_dynamic-update-slice_fusion.4
  951.3 2.1 bitcast_dynamic-update-slice_fusion.4
  970.6 2.1 bitcast_dynamic-update-slice_fusion.4
  976.1 2.1 bitcast_dynamic-update-slice_fusion.4
  981.6 2.1 bitcast_dynamic-update-slice_fusion.4
  1003.7 2.1 bitcast_dynamic-update-slice_fusion.4
  1009.2 2.1 bitcast_dynamic-update-slice_fusion.4
  1028.5 2.1 bitcast_dynamic-update-slice_fusion.4
  1050.6 2.1 bitcast_dynamic-update-slice_fusion.4
  1056.1 2.1 bitcast_dynamic-update-slice_fusion.4
  1086.4 2.1 bitcast_dynamic-update-slice_fusion.4
  1091.4 17.8 %copy.94 = f32[64,64,1024]{2,1,0:T(8,128)} copy(f32[64,64,1024]{2,0,1:T(8,128)} %get-tuple-element.53) | data formatting | bytes 33554432 | tf_op jit(solution)/shard_map/mul | solution.py:183
  1109.3 176.8 %while.3 = (s32[]{:T(128)}, f32[4096,1024]{1,0:T(8,128)}, s32[64,2]{0,1:T(2,128)S(1)}, f32[64,32,32]{2,1,0:T(8,128)S(1)}, s32[]{:T(128)}) while((s32[]{:T(128)}, f32[4096,1024]{1,0:T(8,128)}, s32[64,2]{0,1:T(2,128)S(1)}, f32[64,32,32]{2,1,0:T(8,128)S(1)}, s32[]{:T(128)}) %tuple.58), condition=%wide.while_cond.1, body=%wide.while_body.1.sunk | while | flops 2 | bytes 20589 | solution.py:108
  1143.1 2.1 bitcast_dynamic-update-slice_fusion.5
  1148.6 2.1 bitcast_dynamic-update-slice_fusion.5
  1167.9 2.1 bitcast_dynamic-update-slice_fusion.5
  1173.4 2.1 bitcast_dynamic-update-slice_fusion.5
  1178.9 2.1 bitcast_dynamic-update-slice_fusion.5
  1184.5 2.1 bitcast_dynamic-update-slice_fusion.5
  1206.5 2.1 bitcast_dynamic-update-slice_fusion.5
  1256.1 2.1 bitcast_dynamic-update-slice_fusion.5
  1283.7 2.1 bitcast_dynamic-update-slice_fusion.5
  1286.1 2.8 multiply_reduce_fusion.1
  1288.8 2.8 multiply_reduce_fusion
  1292.6 3.7 all-to-all-start.2
  1296.4 3.6 all-to-all-done.2
  (451 shorter events, 314.1 us)
Async XLA Ops:
  6.5 572.2 %copy-start = (f32[1,128,2,256]{3,2,1,0:T(2,128)S(1)}, f32[1,128,2,256]{3,2,1,0:T(2,128)}, u32[]{:S(2)}) copy-start(f32[1,128,2,256]{3,2,1,0:T(2,128)} %param.19) | copy-start | bytes 786436
  6.5 232.3 %all-gather.2.cloned.1.call-start = ((), (), s32[]{:S(2)}) async-start(), calls=%async_computation.3 | async-start | bytes 18874368 | tf_op jit(solution)/shard_map/all_gather | solution.py:152
  10.6 325.5 %copy-start.5 = (f32[64,64]{0,1:T(8,128)}, f32[64,64]{0,1:T(8,128)S(1)}, u32[]{:S(2)}) copy-start(f32[64,64]{0,1:T(8,128)S(1)} %copy.75) | copy-start | bytes 49156
  10.8 325.2 %copy-start.7 = (f32[64,64]{0,1:T(8,128)}, f32[64,64]{0,1:T(8,128)S(1)}, u32[]{:S(2)}) copy-start(f32[64,64]{0,1:T(8,128)S(1)} %copy.76) | copy-start | bytes 49156
  468.2 99.2 %all-to-all-start = ((bf16[8,128,4096]{1,0,2:T(8,128)(2,1)}), bf16[8,128,4096]{1,0,2:T(8,128)(2,1)}, u32[]{:S(2)}, u32[]{:S(2)}) async-start(bf16[8,128,4096]{1,0,2:T(8,128)(2,1)} %bitcast.125), calls=%async_computation | async-start | bytes 16777216 | tf_op jit(solution)/shard_map/all_to_all | solution.py:175
  486.4 88.3 %copy-start.17 = (s32[1,128,1]{1,2,0:T(1,128)S(1)}, s32[1,128,1]{1,2,0:T(1,128)}, u32[]{:S(2)}) copy-start(s32[1,128,1]{1,2,0:T(1,128)} %param.16) | copy-start | bytes 1540
  486.4 89.9 %copy-start.2 = (s32[1,128]{1,0:T(1,128)S(1)}, s32[1,128]{1,0:T(1,128)}, u32[]{:S(2)}) copy-start(s32[1,128]{1,0:T(1,128)} %param.20) | copy-start | bytes 1540
  486.4 90.7 %copy-start.3 = (s32[1,128]{1,0:T(1,128)S(1)}, s32[1,128]{1,0:T(1,128)}, u32[]{:S(2)}) copy-start(s32[1,128]{1,0:T(1,128)} %param.17) | copy-start | bytes 1540
  486.4 91.5 %copy-start.4 = (s32[1,128]{1,0:T(1,128)S(1)}, s32[1,128]{1,0:T(1,128)}, u32[]{:S(2)}) copy-start(s32[1,128]{1,0:T(1,128)} %param.18) | copy-start | bytes 1540
  486.4 96.1 %copy-start.16 = (f32[2,630]{1,0:T(2,128)S(1)}, f32[2,630]{1,0:T(2,128)}, u32[]{:S(2)}) copy-start(f32[2,630]{1,0:T(2,128)} %param.21) | copy-start | bytes 15124
  567.4 99.1 %all-to-all-start.1 = ((bf16[8,128,4096]{1,0,2:T(8,128)(2,1)}), bf16[8,128,4096]{1,0,2:T(8,128)(2,1)}, u32[]{:S(2)}, u32[]{:S(2)}) async-start(bf16[8,128,4096]{1,0,2:T(8,128)(2,1)} %bitcast.124), calls=%async_computation.1 | async-start | bytes 16777216 | tf_op jit(solution)/shard_map/all_to_all | solution.py:176
  744.2 38.9 %copy-start.6 = (f32[64,64]{0,1:T(8,128)S(1)}, f32[64,64]{0,1:T(8,128)}, u32[]{:S(2)}) copy-start(f32[64,64]{0,1:T(8,128)} %copy-done.5) | copy-start | bytes 49156
  744.2 38.9 %copy-start.8 = (f32[64,64]{0,1:T(8,128)S(1)}, f32[64,64]{0,1:T(8,128)}, u32[]{:S(2)}) copy-start(f32[64,64]{0,1:T(8,128)} %copy-done.7) | copy-start | bytes 49156
  895.5 19.3 %copy-start.9 = (s32[64,2]{0,1:T(2,128)S(1)}, s32[64,2]{0,1:T(2,128)}, u32[]{:S(2)}) copy-start(s32[64,2]{0,1:T(2,128)} %pad_add_fusion) | copy-start | bytes 1540
  1091.3 210.0 %copy-start.1 = (f32[1,128,2,256]{3,2,1,0:T(2,128)S(1)}, f32[1,128,2,256]{3,2,1,0:T(2,128)}, u32[]{:S(2)}) copy-start(f32[1,128,2,256]{3,2,1,0:T(2,128)} %param.19) | copy-start | bytes 786436
  1091.3 194.7 %copy-start.10 = (f32[64,1,256]{2,0,1:T(8,128)S(1)}, f32[64,1,256]{2,0,1:T(8,128)}, u32[]{:S(2)}) copy-start(f32[64,1,256]{2,0,1:T(8,128)} %copy.131) | copy-start | bytes 196612
  1091.3 194.7 %copy-start.11 = (f32[64,1,256]{2,0,1:T(8,128)S(1)}, f32[64,1,256]{2,0,1:T(8,128)}, u32[]{:S(2)}) copy-start(f32[64,1,256]{2,0,1:T(8,128)} %copy.132) | copy-start | bytes 196612
  1091.3 200.3 %copy-start.13 = (f32[64]{0:T(128)S(1)}, f32[64]{0:T(128)}, u32[]{:S(2)}) copy-start(f32[64]{0:T(128)} %get-tuple-element.60) | copy-start | bytes 772
  1091.3 200.3 %copy-start.14 = (f32[64]{0:T(128)S(1)}, f32[64]{0:T(128)}, u32[]{:S(2)}) copy-start(f32[64]{0:T(128)} %get-tuple-element.61) | copy-start | bytes 772
  1091.4 205.0 %copy-start.15 = (s32[32]{0:T(128)S(1)}, s32[32]{0:T(128)}, u32[]{:S(2)}) copy-start(s32[32]{0:T(128)} %fusion.60) | copy-start | bytes 388
  1091.4 209.3 %copy-start.12 = (pred[32]{0:T(512)(128)(4,1)S(1)}, pred[32]{0:T(512)(128)(4,1)}, u32[]{:S(2)}) copy-start(pred[32]{0:T(512)(128)(4,1)} %get-tuple-element.40) | copy-start | bytes 100
  1292.6 7.3 all-to-all-start.2
Sparse Core Ops, SparseCore 0:
  9.5 229.2 all-gather.1
where the time goes:
time: 1330 us; the launch traced here: 1310 us
  local copies, waits for them, and re-layouts  539 us (41%)
  waiting for transfers between devices  363 us (27%)
  matrix products  244 us (18%)
  other arithmetic  130 us (10%)
  starting transfers between devices  17.4 us (1%)
  between operations  14.6 us (1%)
    gather x384, local copies, waits for them, and re-layouts  353 us
    all_gather x1, waiting for transfers between devices, local(): gathered = lax.all_gather(sky_model, 'beam', axis=0, tiled=True)  227 us
    all_to_all x1, waiting for transfers between devices, local(): lax.all_to_all(spec_re, 'fft', split_axis=2, concat_axis=1, tiled=True)  72.1 us
    all_to_all x1, waiting for transfers between devices, local(): lax.all_to_all(spec_im, 'fft', split_axis=2, concat_axis=1, tiled=True)  59.6 us
    dot_general x1, matrix products, transform_rows(): jnp.einsum('rkq,qm->rmk', stacked, complex_table(cos_two, sin_two), preci...  58.6 us
    dot_general x1, matrix products, transform_columns(): jnp.einsum('kqv,qm->mkv', stacked, complex_table(cos_two, sin_two), preci...  58.6 us
    dot_general x1, matrix products, bf16_times_table(): jnp.einsum('pqv,pk->kqv', folded, pieces[2], preferred_element_type=jnp.f...  38.8 us
    dot_general x1, matrix products, transform_rows(): jnp.einsum('rpq,pk->rkq', folded, jnp.concatenate([cos_one, sin_one], axi...  37.9 us
  transfers between devices with their start and end apart: 4, of which 4 were waited for; matrix products, arithmetic and copies ran while one was open for 4% of the time, Pallas kernels for 0%

commit v1 on v0

v1 whole, which is shorter than its diff:
```python
import functools
import math

import jax
import jax.numpy as jnp
import ml_dtypes
import numpy as np
from jax import lax
from jax.experimental import pallas as pl
from jax.experimental.pallas import tpu as pltpu
from jax.sharding import PartitionSpec as P

FT = 8
SG = 32
CAP = 8
LANES = 128

kernel_width = 1.5
highest = lax.Precision.HIGHEST
f32 = jnp.float32
bf16 = jnp.bfloat16


def round_up(number, unit):
    return -(-number // unit) * unit


def phase_table(rows, cols, period):
    residue = np.arange(rows)[:, None] * np.arange(cols)[None, :] % period
    angle = residue * (2.0 * math.pi / period)
    return np.cos(angle), -np.sin(angle)


def unit_phase(residue, period):
    angle = residue.astype(f32) * (2.0 * math.pi / period)
    return jnp.cos(angle), -jnp.sin(angle)


def window_kernel(
    tix_ref, r0_ref, c0_ref,
    own_ref, oth_ref, p1_ref, p0_ref, tcos_ref, tsin_ref,
    lr0_ref, li0_ref, lr1_ref, li1_ref, ar_ref, ai_ref, br_ref, bi_ref,
    g_ref, rs_ref, *, chunk,
):
    q = pl.program_id(0)
    v_rows = rs_ref.shape[2]
    chunks = v_rows // chunk

    def one_tile(k, carry):
        t = tix_ref[q, k]
        scale = p1_ref[0, pl.ds(k, 1), :]
        own = (own_ref[t].astype(f32) * scale).astype(bf16)
        oth = (oth_ref[t].astype(f32) * scale).astype(bf16)
        both = jnp.concatenate([own, oth], axis=0)
        row_scale = p0_ref[0, pl.ds(k, 1), :]

        def one_chunk(i, inner):
            at = pl.multiple_of(i * chunk, chunk)
            for c, table in enumerate((tcos_ref, tsin_ref)):
                got = lax.dot_general(
                    table[pl.ds(at, chunk), :], both, (((1,), (1,)), ((), ())),
                    preferred_element_type=f32,
                ) * row_scale
                for h in range(2):
                    rs_ref[(h * 2 + c), k, pl.ds(at, chunk), :] = got[:, h * LANES:(h + 1) * LANES]
            return inner

        return lax.fori_loop(0, chunks, one_chunk, carry)

    lax.fori_loop(0, CAP, one_tile, 0)

    lane = lax.broadcasted_iota(jnp.int32, (2 * SG, LANES), 1)
    is_low = (lane // SG) == 1

    def one_sub(s, carry):
        r0 = r0_ref[q, s]
        c0 = c0_ref[q, s]
        rows = []
        for k in range(CAP):
            rows.append(jnp.concatenate(
                [rs_ref[j, k, pl.ds(c0, SG), :].astype(bf16) for j in range(4)], axis=1))
        windows = jnp.concatenate(rows, axis=0)
        lr0 = lr0_ref[pl.ds(r0, SG), :].astype(bf16)
        li0 = li0_ref[pl.ds(r0, SG), :].astype(bf16)
        lr1 = lr1_ref[pl.ds(r0, SG), :].astype(bf16)
        li1 = li1_ref[pl.ds(r0, SG), :].astype(bf16)
        left = jnp.concatenate([
            jnp.concatenate([lr0, -li0, lr1, -li1], axis=1),
            jnp.concatenate([li0, lr0, li1, lr1], axis=1),
        ], axis=0)
        out = lax.dot_general(left, windows, (((1,), (1,)), ((), ())), preferred_element_type=f32)
        r8 = lax.rem(r0, 8)
        c8 = lax.rem(c0, 8)
        ar, ai = ar_ref[0, r8], ai_ref[0, r8]
        br, bi = br_ref[0, c8], bi_ref[0, c8]
        fr = ar * br - ai * bi
        fi = ar * bi + ai * br
        re_parts, im_parts = [], []
        for a in range(SG // 8):
            re = out[a * 8:(a + 1) * 8]
            im = out[SG + a * 8:SG + (a + 1) * 8]
            re_parts.append(re * fr - im * fi)
            im_parts.append(re * fi + im * fr)
        full = jnp.concatenate(re_parts + im_parts, axis=0)
        half = full[:, :LANES] + full[:, LANES:]
        half = half + pltpu.roll(half, 2 * SG, 1)
        half = half + pltpu.roll(half, SG, 1)
        high = half.astype(bf16)
        low = half - high.astype(f32)
        g_ref[0, s] = jnp.where(is_low, low, half).astype(bf16)
        return carry

    lax.fori_loop(0, r0_ref.shape[1], one_sub, 0)


def degrid_kernel(g_ref, off_ref, out_ref, acc_ref):
    subs = g_ref.shape[1]
    samples = off_ref.shape[3]
    places = lax.broadcasted_iota(jnp.int32, (SG, samples), 0).astype(f32)
    factor = -math.log2(math.e) / kernel_width**2
    blank = jnp.zeros((LANES - 3 * SG, samples), bf16)

    def one_sub(s, carry):
        tu = places - off_ref[0, s, 0:1, :]
        tv = places - off_ref[0, s, 1:2, :]
        wu = jnp.exp2(tu * tu * factor)
        wv = jnp.exp2(tv * tv * factor)
        wv_high = wv.astype(bf16)
        wv_low = (wv - wv_high.astype(f32)).astype(bf16)
        right = jnp.concatenate([wv_high, wv_high, wv_low, blank], axis=0)
        inner = jnp.dot(g_ref[0, s], right, preferred_element_type=f32)
        re = jnp.sum(inner[:SG] * wu, axis=0, keepdims=True)
        im = jnp.sum(inner[SG:] * wu, axis=0, keepdims=True)
        acc_ref[pl.ds(s, 1), :] = jnp.concatenate([re, im], axis=1)
        return carry

    lax.fori_loop(0, subs, one_sub, 0, unroll=4)
    out_ref[0, 0, 0] = acc_ref[...].astype(out_ref.dtype)


def local(
    sky_model, footprint, profile, chan_block, sub_strip, sub_row, sub_col,
    offsets, sub_base, gain_table,
):
    axes = ("beam", "fft")
    beams = lax.axis_size("beam")
    ffts = lax.axis_size("fft")
    my_beam = lax.axis_index("beam")
    my_fft = lax.axis_index("fft")
    my_core = my_fft % 2
    quads = beams // 2
    pairs = ffts // 2
    tiles_dev, tile_rows, tile_side = sky_model.shape
    image_side = FT * tile_side
    half_side = image_side // 2
    subs = sub_row.shape[1]
    sub_dev = subs // ffts
    samples = offsets.shape[3]
    strip_cols = image_side // ffts

    def turn(step):
        out = []
        for b in range(beams):
            for f in range(ffts):
                target = (2 * ((b // 2 - step) % quads) + f % 2) * ffts + 2 * (f // 2) + b % 2
                out.append((b * ffts + f, target))
        return out

    oth_sky = lax.ppermute(sky_model, "fft", [(f, f ^ 1) for f in range(ffts)])

    channel_pick = (jnp.arange(profile.shape[1], dtype=jnp.int32) == chan_block[0]).astype(f32)
    chosen = jnp.sum(profile[0] * channel_pick[:, None, None], axis=0)
    col_at = sub_strip[0, :, 0] * strip_cols + sub_col[0]
    mirrored = col_at >= half_side
    r0_mine = jnp.where(mirrored, (image_side - (SG - 1) - sub_row[0]) % image_side, sub_row[0])
    c0_mine = jnp.where(mirrored, image_side - (SG - 1) - col_at, col_at)
    off_mine = jnp.where(mirrored[:, None, None], (SG - 1) - offsets[0], offsets[0])
    small = jnp.concatenate([chosen.reshape(-1), r0_mine.astype(f32), c0_mine.astype(f32)]).reshape(-1, LANES)
    steps = [(my_beam // 2 + t) % quads for t in range(quads)]
    smalls = jnp.stack([lax.ppermute(small, axes, turn(t)) for t in range(quads)]).reshape(quads, -1)
    offs = jnp.stack([lax.ppermute(off_mine, axes, turn(t)) for t in range(quads)])
    beam_ids = jnp.stack([2 * s + my_core for s in steps])
    prof = smalls[:, :2 * image_side].reshape(quads, 2, image_side)
    r0_all = smalls[:, 2 * image_side:2 * image_side + subs].astype(jnp.int32)
    c0_all = smalls[:, 2 * image_side + subs:].astype(jnp.int32)

    lists = jnp.take(footprint, beam_ids, axis=0)
    hits = (lists // tiles_dev == my_beam).astype(jnp.int32)
    order = jnp.cumsum(hits, axis=1) - 1
    slots = hits[:, :, None] * (order[:, :, None] == jnp.arange(CAP, dtype=jnp.int32)[None, None, :])
    tix = jnp.sum(slots * (lists % tiles_dev)[:, :, None], axis=1)
    place = jnp.sum(slots * jnp.arange(FT * FT, dtype=jnp.int32)[None, :, None], axis=1)
    valid = jnp.sum(slots, axis=1).astype(f32)
    tile_i, tile_j = place // FT, place % FT
    eights = jnp.arange(FT, dtype=jnp.int32)
    pick_i = (tile_i[:, :, None] == eights).astype(f32) * valid[:, :, None]
    pick_j = (tile_j[:, :, None] == eights).astype(f32)
    prof_u = prof[:, 0].reshape(quads, FT, ffts, tile_rows)
    fft_ids = jnp.stack([my_fft, my_fft + 1 - 2 * my_core])
    prof_u = jnp.take(prof_u, fft_ids, axis=2)
    prof_u = jnp.pad(prof_u, ((0, 0), (0, 0), (0, 0), (0, LANES - tile_rows))).reshape(quads, FT, 2 * LANES)
    p0 = jnp.sum(pick_i[:, :, :, None] * prof_u[:, None], axis=2)
    p1 = jnp.sum(pick_j[:, :, :, None] * prof[:, 1].reshape(quads, 1, FT, tile_side), axis=2)

    lane_e = jnp.arange(CAP * SG, dtype=jnp.int32) % SG
    lane_i = jnp.repeat(tile_i, SG, axis=1)
    lane_j = jnp.repeat(tile_j, SG, axis=1)
    ar, ai = unit_phase(
        lane_i[:, None, None, :] * (eights[:, None] + eights[None, :])[None, :, :, None] % FT, FT)
    br, bi = unit_phase(
        lane_j[:, None, :] * (eights[None, :, None] + lane_e[None, None, :]) % FT, FT)
    br = jnp.broadcast_to(br[:, :, None, :], ar.shape)
    bi = jnp.broadcast_to(bi[:, :, None, :], ai.shape)

    chunk = 344
    v_rows = 6 * chunk
    t_cos, t_sin = phase_table(v_rows, tile_side, image_side)
    t_cos, t_sin = jnp.asarray(t_cos.astype(ml_dtypes.bfloat16)), jnp.asarray(t_sin.astype(ml_dtypes.bfloat16))
    u_rows = image_side + SG
    u_cos, u_sin = phase_table(u_rows, LANES, image_side)
    u_cos, u_sin = jnp.asarray(u_cos.astype(np.float32)), jnp.asarray(u_sin.astype(np.float32))
    shift_r, shift_i = unit_phase(
        fft_ids[:, None] * tile_rows * jnp.arange(u_rows, dtype=jnp.int32)[None, :] % image_side, image_side)
    left = []
    for h in range(2):
        sr, si = shift_r[h][:, None], shift_i[h][:, None]
        left += [u_cos * sr - u_sin * si, u_cos * si + u_sin * sr]

    pad_rows = ((0, 0), (0, LANES - tile_rows), (0, 0))
    own_sky, oth_sky = (jnp.pad(s, pad_rows) if tile_rows < LANES else s for s in (sky_model, oth_sky))

    whole = lambda a: pl.BlockSpec(a.shape, lambda q, *_: (0,) * a.ndim, pipeline_mode=pl.Buffered(1))
    per_beam = lambda a: pl.BlockSpec((1,) + a.shape[1:], lambda q, *_: (q,) + (0,) * (a.ndim - 1))
    fixed = [own_sky, oth_sky]
    operands = (own_sky, oth_sky, p1, p0, t_cos, t_sin, *left, ar, ai, br, bi)
    specs = [whole(own_sky), whole(oth_sky), per_beam(p1), per_beam(p0), whole(t_cos), whole(t_sin)]
    specs += [whole(x) for x in left] + [per_beam(x) for x in (ar, ai, br, bi)]
    cuts = pl.pallas_call(
        functools.partial(window_kernel, chunk=chunk),
        out_shape=jax.ShapeDtypeStruct((quads, subs, 2 * SG, LANES), bf16),
        grid_spec=pltpu.PrefetchScalarGridSpec(
            num_scalar_prefetch=3, grid=(quads,), in_specs=specs,
            out_specs=pl.BlockSpec((1, subs, 2 * SG, LANES), lambda q, *_: (q, 0, 0, 0)),
            scratch_shapes=[pltpu.VMEM((4, CAP, v_rows, LANES), f32)],
        ),
        compiler_params=pltpu.CompilerParams(vmem_limit_bytes=63 << 20),
        name="windows",
    )(tix, r0_all, c0_all, *operands)

    partial = pl.pallas_call(
        degrid_kernel,
        grid=(quads, ffts),
        in_specs=[
            pl.BlockSpec((1, sub_dev, 2 * SG, LANES), lambda q, f: (q, f, 0, 0)),
            pl.BlockSpec((1, sub_dev, 2, samples), lambda q, f: (q, f, 0, 0)),
        ],
        out_specs=pl.BlockSpec((1, 1, 1, sub_dev, 2 * samples), lambda q, f: (q, f % 2, f // 2, 0, 0)),
        out_shape=jax.ShapeDtypeStruct((quads, 2, pairs, sub_dev, 2 * samples), bf16),
        scratch_shapes=[pltpu.VMEM((sub_dev, 2 * samples), f32)],
        compiler_params=pltpu.CompilerParams(vmem_limit_bytes=32 << 20),
        name="degrid",
    )(cuts, offs)

    partial = jnp.roll(partial, my_beam // 2, axis=0)
    groups = [[b * ffts + 2 * x + c for b in range(beams) for x in range(pairs)] for c in range(2)]
    parts = partial.reshape(beams * pairs, sub_dev, 2 * samples)
    came = lax.all_to_all(parts, axes, 0, 0, tiled=True, axis_index_groups=groups)
    total = jnp.sum(came.astype(f32), axis=0)
    total = lax.ppermute(total, axes, turn(0)) * (1.0 / image_side)
    total = total.reshape(sub_dev, 2, samples)

    mine = lambda a: lax.dynamic_slice_in_dim(a, my_fft * sub_dev, sub_dev, 0)
    base_hot = (mine(sub_base[0])[:, None] == jnp.arange(gain_table.shape[1], dtype=jnp.int32)[None, :]).astype(f32)
    gains = jnp.dot(base_hot, gain_table.T, precision=highest)
    g0, g1 = gains[:, 0:1], gains[:, 1:2]
    re = total[:, 0]
    im = jnp.where(mine(mirrored)[:, None], -total[:, 1], total[:, 1])
    return jnp.stack([g0 * re - g1 * im, g0 * im + g1 * re], axis=1)[None]


def solution(mesh):
    return jax.shard_map(
        local,
        mesh=mesh,
        in_specs=(
            P("beam", "fft", None), P(), P("beam", None, None, None), P("beam"),
            P("beam", None, None), P("beam", None), P("beam", None),
            P("beam", None, None, None), P("beam", None), P(),
        ),
        out_specs=P("beam", "fft", None, None),
        check_vma=False,
    )
```

time: 1330 us -> 387 us (0.29); the launches traced: 1310 us -> 387 us
  local copies, waits for them, and re-layouts: 539 us -> 9.93 us
  waiting for transfers between devices: 363 us -> 31.1 us
  Pallas kernels: 0 us -> 296 us
  matrix products: 244 us -> 0.18 us
  other arithmetic: 130 us -> 20.4 us
  between operations: 14.6 us -> 1.16 us
    gather x391 -> x2, local copies, waits for them, and re-layouts: 381 us -> 1.8 us  [the longest x1 1.25 us: local(): lists = jnp.take(footprint, beam_ids, axis=0)]
    pallas_call x0 -> x2, Pallas kernels: none -> 296 us  [the longest x1 270 us: local(): pl.pallas_call(functools.partial(window_kernel, chunk=chunk), out_shape=j...]
    dot_general x10 -> x1, matrix products: 244 us -> 0.18 us  [local(): gains = jnp.dot(base_hot, gain_table.T, precision=highest)]
    all_gather x1 -> x0, waiting for transfers between devices: 227 us -> none  [local(): gathered = lax.all_gather(sky_model, 'beam', axis=0, tiled=True)]
    all_to_all x3 -> x1, waiting for transfers between devices: 135 us -> 12 us  [local(): lax.all_to_all(parts, axes, 0, 0, tiled=True, axis_index_groups=groups)]
    convert_element_type x3 -> x0, local copies, waits for them, and re-layouts: 40.6 us -> none  [the longest x1 18 us: local(): arranged.astype(jnp.float32) * prof_rows[:, None] * chosen_prof[1][None, :]]
    concatenate x3 -> x1, other arithmetic: 38.2 us -> 0.99 us  [local(): partial = jnp.roll(partial, my_beam // 2, axis=0)]
    mul x4 -> x2, local copies, waits for them, and re-layouts: 37 us -> 0.16 us  [the longest x1 0.08 us: local(): lane_i[:, None, None, :]]
  transfers between devices with their start and end apart: 4 -> 11, of which waited for: 4 -> 3; matrix products, arithmetic and copies ran while one was open for 4% -> 5% of each run, Pallas kernels for 0% -> 0%
where the time goes in v1:
time: 387 us
  Pallas kernels  296 us (76%)
  waiting for transfers between devices  31.1 us (8%)
  starting transfers between devices  28.3 us (7%)
  other arithmetic  20.4 us (5%)
  local copies, waits for them, and re-layouts  9.93 us (3%)
    pallas_call x1, Pallas kernels, local(): pl.pallas_call(functools.partial(window_kernel, chunk=chunk), out_shape=j...  270 us
    pallas_call x1, Pallas kernels, local(): pl.pallas_call(degrid_kernel, grid=(quads, ffts), in_specs=[pl.BlockSpec(...  25.9 us
    ppermute x4, waiting for transfers between devices, local(): lax.ppermute(off_mine, axes, turn(t))  17.2 us
    all_to_all x1, waiting for transfers between devices, local(): lax.all_to_all(parts, axes, 0, 0, tiled=True, axis_index_groups=groups)  12 us
    ppermute x4, starting transfers between devices, local(): lax.ppermute(small, axes, turn(t))  9.43 us
    ppermute x4, starting transfers between devices, local(): lax.ppermute(off_mine, axes, turn(t))  9.15 us
  transfers between devices with their start and end apart: 11, of which 3 were waited for; matrix products, arithmetic and copies ran while one was open for 5% of the time, Pallas kernels for 0%

profile of v1, /device:TPU:1, one launch (start us, length us, event | category | flops | bytes accessed | tf_op | source)
XLA Modules:
  0.0 386.7 jit_solution(16369426082540256297)
XLA Ops:
  0.8 1.1 fusion.4
  2.0 0.7 fusion.30
  2.7 5.7 %collective-permute-start.1 = (f32[66,128]{1,0:T(8,128)S(1)}, f32[66,128]{1,0:T(8,128)S(1)}, u32[]{:S(2)}, u32[]{:S(2)}) collective-permute-start(f32[66,128]{1,0:T(8,128)S(1)} %maximum_bitcast_fusion.1), channel_id=1, source_target_pairs={{0,24},{1,28},{2,26},{3,30},{4,25},{5,29},{6,27},{7,31},{8,0},{9,4... | collective-permute-start | bytes 101384 | tf_op jit(solution)/shard_map/ppermute | solution.py:180
  8.4 1.9 collective-permute-start
  10.3 0.1 collective-permute-start.3
  10.4 1.7 collective-permute-start.2
  12.1 0.1 broadcast_multiply_fusion.1
  12.2 0.1 compare_and_fusion
  12.3 0.7 broadcast_compare_fusion.2
  13.0 0.6 fusion.14
  13.7 0.1 fusion.28
  13.8 1.2 gather_fusion
  15.0 0.1 compare_and_fusion.1
  15.1 0.1 fusion.23
  15.2 0.2 reduce_window_sum.11
  15.4 0.1 add_select_fusion.4
  15.5 0.9 select_reduce_fusion
  16.4 0.1 fusion.18
  16.5 0.1 fusion.19
  16.5 0.1 broadcast_in_dim.53
  16.6 0.1 mul.334
  16.7 0.1 broadcast_in_dim.54
  16.8 0.1 mul.340
  16.9 0.2 slice_reduce_fusion.1
  17.0 0.1 fusion.29
  17.1 1.9 sine_negate_fusion
  19.0 0.1 sine_negate_fusion.2
  19.2 1.2 subtract_select_fusion
  20.4 7.2 %multiply_add_fusion = (f32[4128,128]{1,0:T(8,128)}, f32[4128,128]{1,0:T(8,128)}, f32[4128,128]{1,0:T(8,128)}, f32[4128,128]{1,0:T(8,128)}) fusion(f32[4128,128]{1,0:T(8,128)} %constant.248.clone, f32[4128,128]{1,0:T(8,128)S(1)} %copy-done.3, f32[4128]{0:T(1024)S(1)} %get-tuple-element.7, f32[4128]{0:T(1024)S(1)} %get-tuple-element.39, ...), kind=kLoop, calls=%fused_computation.2 | loop fusion | flops 6340608 | bytes 12747264 | tf_op jit(solution)/shard_map/add | solution.py:227
  27.5 0.1 broadcast_bitcast_fusion
  27.6 3.5 collective-permute-start.5
  31.2 2.9 collective-permute-start.6
  34.1 0.0 collective-permute-done.3
  34.1 2.7 collective-permute-start.7
  36.9 0.1 collective-permute-start.8
  37.0 0.1 pad_maximum_fusion.1
  37.1 0.1 reshape.592
  37.3 0.1 reshape_squeeze.4
  37.4 0.6 gather_fusion.1
  37.9 0.2 slice_reduce_fusion
  38.1 0.6 maximum_convert_fusion
  38.7 0.7 multiply_reduce_fusion.1.p0_ref
  39.5 0.8 multiply_reduce_fusion.p1_ref
  40.3 17.2 %collective-permute-done.7 = f32[128,2,256]{2,1,0:T(2,128)S(1)} collective-permute-done((f32[128,2,256]{2,1,0:T(2,128)S(1)}, f32[128,2,256]{2,1,0:T(2,128)S(1)}, u32[]{:S(2)}, u32[]{:S(2)}) %collective-permute-start.7) | collective-permute-done | bytes 262176 | tf_op jit(solution)/shard_map/ppermute | solution.py:181
  57.5 0.0 collective-permute-done.8
  57.5 1.5 pad_maximum_fusion.off_ref
  59.0 0.7 broadcast_in_dim.58.br_ref
  59.7 0.7 broadcast_in_dim.94.bi_ref
  60.5 269.8 %windows.1.g_ref = bf16[4,128,64,128]{3,2,1,0:T(8,128)(2,1)} custom-call(s32[4,8]{1,0:T(4,128)} %get-tuple-element.11.tix_ref, s32[4,128]{1,0:T(4,128)} %get-tuple-element.19.r0_ref, s32[4,128]{1,0:T(4,128)} %get-tuple-element.18.c0_ref, bf16[16,128,512]{2,1,0:T(8,128)(2,1)} %own_ref.1, bf16[16,128,512]{2,1,0:T(8,128)(2,1)} %collective-permute-done.4.oth_ref, ...), custom_call_target="tpu_custom_call" | custom-call | tf_op jit(solution)/shard_map/windows/pallas_call | solution.py:238
  330.3 3.4 copy-done.1
  333.7 1.2 copy-done.2
  334.9 25.9 %degrid.1 = bf16[4,2,2,32,512]{4,3,2,1,0:T(8,128)(2,1)S(1)} custom-call(bf16[4,128,64,128]{3,2,1,0:T(8,128)(2,1)S(1)} %copy-done.1, f32[4,128,2,256]{3,2,1,0:T(2,128)S(1)} %copy-done.2), custom_call_target="tpu_custom_call" | custom-call | tf_op jit(solution)/shard_map/degrid/pallas_call | solution.py:250
  360.7 1.0 fusion
  361.7 3.6 all-to-all-start
  365.3 0.1 fusion.25
  365.4 0.2 fusion.6
  365.6 12.0 %all-to-all-done = bf16[16,32,512]{2,1,0:T(8,128)(2,1)S(1)} async-done(((bf16[16,32,512]{2,1,0:T(8,128)(2,1)}), bf16[16,32,512]{2,1,0:T(8,128)(2,1)S(1)}, u32[]{:S(2)}, u32[]{:S(2)}) %all-to-all-start) | async-done | bytes 524320 | tf_op jit(solution)/shard_map/all_to_all | solution.py:267
  377.6 0.1 convert_reduce_fusion
  377.7 6.2 %collective-permute-start.9 = (f32[32,512]{1,0:T(8,128)S(1)}, f32[32,512]{1,0:T(8,128)S(1)}, u32[]{:S(2)}, u32[]{:S(2)}) collective-permute-start(f32[32,512]{1,0:T(8,128)S(1)} %convert_reduce_fusion), channel_id=1, source_target_pairs={{0,0},{1,4},{2,2},{3,6},{4,1},{5,5},{6,3},{7,7},{8,8},{9,12},{10,1... | collective-permute-start | bytes 196616 | tf_op jit(solution)/shard_map/ppermute | solution.py:269
  383.9 0.1 dynamic_slice.12
  384.0 1.8 collective-permute-done.9
  385.8 0.1 fusion.31
  385.9 0.1 multiply_subtract_fusion.2
  386.0 0.7 copy.30
  (37 shorter events, 0.3 us)
Async XLA Ops:
  0.0 365.4 %copy-start = (f32[2,630]{1,0:T(2,128)S(1)}, f32[2,630]{1,0:T(2,128)}, u32[]{:S(2)}) copy-start(f32[2,630]{1,0:T(2,128)} %param.23) | copy-start | bytes 15124
  0.0 20.4 %copy-start.3 = (f32[4128,128]{1,0:T(8,128)S(1)}, f32[4128,128]{1,0:T(8,128)}, u32[]{:S(2)}) copy-start(f32[4128,128]{1,0:T(8,128)} %constant.247.clone) | copy-start | bytes 6340612
  2.7 24.9 %collective-permute-start.1 = (f32[66,128]{1,0:T(8,128)S(1)}, f32[66,128]{1,0:T(8,128)S(1)}, u32[]{:S(2)}, u32[]{:S(2)}) collective-permute-start(f32[66,128]{1,0:T(8,128)S(1)} %maximum_bitcast_fusion.1), channel_id=1, source_target_pairs={{0,24},{1,28},{2,26},{3,30},{4,25},{5,29},{6,27},{7,31},{8,0},{9,4... | collective-permute-start | bytes 101384 | tf_op jit(solution)/shard_map/ppermute | solution.py:180
  8.4 22.8 %collective-permute-start = (f32[66,128]{1,0:T(8,128)S(1)}, f32[66,128]{1,0:T(8,128)S(1)}, u32[]{:S(2)}, u32[]{:S(2)}) collective-permute-start(f32[66,128]{1,0:T(8,128)S(1)} %maximum_bitcast_fusion.1), channel_id=1, source_target_pairs={{0,0},{1,4},{2,2},{3,6},{4,1},{5,5},{6,3},{7,7},{8,8},{9,12},{10,1... | collective-permute-start | bytes 101384 | tf_op jit(solution)/shard_map/ppermute | solution.py:180
  10.3 23.8 %collective-permute-start.3 = (f32[66,128]{1,0:T(8,128)S(1)}, f32[66,128]{1,0:T(8,128)S(1)}, u32[]{:S(2)}, u32[]{:S(2)}) collective-permute-start(f32[66,128]{1,0:T(8,128)S(1)} %maximum_bitcast_fusion.1), channel_id=1, source_target_pairs={{0,8},{1,12},{2,10},{3,14},{4,9},{5,13},{6,11},{7,15},{8,16},{9,20... | collective-permute-start | bytes 101384 | tf_op jit(solution)/shard_map/ppermute | solution.py:180
  10.4 26.5 %collective-permute-start.2 = (f32[66,128]{1,0:T(8,128)S(1)}, f32[66,128]{1,0:T(8,128)S(1)}, u32[]{:S(2)}, u32[]{:S(2)}) collective-permute-start(f32[66,128]{1,0:T(8,128)S(1)} %maximum_bitcast_fusion.1), channel_id=1, source_target_pairs={{0,16},{1,20},{2,18},{3,22},{4,17},{5,21},{6,19},{7,23},{8,24},{9,... | collective-permute-start | bytes 101384 | tf_op jit(solution)/shard_map/ppermute | solution.py:180
  12.1 46.9 %collective-permute-start.4 = (bf16[16,128,512]{2,1,0:T(8,128)(2,1)}, bf16[16,128,512]{2,1,0:T(8,128)(2,1)}, u32[]{:S(2)}, u32[]{:S(2)}) collective-permute-start(bf16[16,128,512]{2,1,0:T(8,128)(2,1)} %own_ref.1), channel_id=1, source_target_pairs={{0,1},{1,0},{2,3},{3,2},{4,5},{5,4},{6,7},{7,6},{8,9},{9,8},{10,11... | collective-permute-start | bytes 6291464 | tf_op jit(solution)/shard_map/ppermute | solution.py:169
  27.6 12.7 %collective-permute-start.5 = (f32[128,2,256]{2,1,0:T(2,128)S(1)}, f32[128,2,256]{2,1,0:T(2,128)S(1)}, u32[]{:S(2)}, u32[]{:S(2)}) collective-permute-start(f32[128,2,256]{2,1,0:T(2,128)S(1)} %subtract_select_fusion), channel_id=1, source_target_pairs={{0,0},{1,4},{2,2},{3,6},{4,1},{5,5},{6,3},{7,7},{8,8},{9,12},{10,1... | collective-permute-start | bytes 786440 | tf_op jit(solution)/shard_map/ppermute | solution.py:181
  31.2 9.1 %collective-permute-start.6 = (f32[128,2,256]{2,1,0:T(2,128)S(1)}, f32[128,2,256]{2,1,0:T(2,128)S(1)}, u32[]{:S(2)}, u32[]{:S(2)}) collective-permute-start(f32[128,2,256]{2,1,0:T(2,128)S(1)} %subtract_select_fusion), channel_id=1, source_target_pairs={{0,24},{1,28},{2,26},{3,30},{4,25},{5,29},{6,27},{7,31},{8,0},{9,4... | collective-permute-start | bytes 786440 | tf_op jit(solution)/shard_map/ppermute | solution.py:181
  34.1 23.4 %collective-permute-start.7 = (f32[128,2,256]{2,1,0:T(2,128)S(1)}, f32[128,2,256]{2,1,0:T(2,128)S(1)}, u32[]{:S(2)}, u32[]{:S(2)}) collective-permute-start(f32[128,2,256]{2,1,0:T(2,128)S(1)} %subtract_select_fusion), channel_id=1, source_target_pairs={{0,16},{1,20},{2,18},{3,22},{4,17},{5,21},{6,19},{7,23},{8,24},{9,... | collective-permute-start | bytes 786440 | tf_op jit(solution)/shard_map/ppermute | solution.py:181
  36.9 20.7 %collective-permute-start.8 = (f32[128,2,256]{2,1,0:T(2,128)S(1)}, f32[128,2,256]{2,1,0:T(2,128)S(1)}, u32[]{:S(2)}, u32[]{:S(2)}) collective-permute-start(f32[128,2,256]{2,1,0:T(2,128)S(1)} %subtract_select_fusion), channel_id=1, source_target_pairs={{0,8},{1,12},{2,10},{3,14},{4,9},{5,13},{6,11},{7,15},{8,16},{9,20... | collective-permute-start | bytes 786440 | tf_op jit(solution)/shard_map/ppermute | solution.py:181
  330.3 3.4 copy-start.1
  333.6 1.2 copy-start.2
  334.9 30.4 %copy-start.4 = (s32[1,128]{1,0:T(1,128)S(1)}, s32[1,128]{1,0:T(1,128)}, u32[]{:S(2)}) copy-start(s32[1,128]{1,0:T(1,128)} %param.22) | copy-start | bytes 1540
  361.7 15.9 %all-to-all-start = ((bf16[16,32,512]{2,1,0:T(8,128)(2,1)}), bf16[16,32,512]{2,1,0:T(8,128)(2,1)S(1)}, u32[]{:S(2)}, u32[]{:S(2)}) async-start(bf16[16,32,512]{2,1,0:T(8,128)(2,1)} %bitcast.31), calls=%async_computation | async-start | bytes 1048576 | tf_op jit(solution)/shard_map/all_to_all | solution.py:267
  377.7 8.1 %collective-permute-start.9 = (f32[32,512]{1,0:T(8,128)S(1)}, f32[32,512]{1,0:T(8,128)S(1)}, u32[]{:S(2)}, u32[]{:S(2)}) collective-permute-start(f32[32,512]{1,0:T(8,128)S(1)} %convert_reduce_fusion), channel_id=1, source_target_pairs={{0,0},{1,4},{2,2},{3,6},{4,1},{5,5},{6,3},{7,7},{8,8},{9,12},{10,1... | collective-permute-start | bytes 196616 | tf_op jit(solution)/shard_map/ppermute | solution.py:269

commit v2 on v1

--- a/solution.py
+++ b/solution.py
@@ -3,8 +3,6 @@
 
 import jax
 import jax.numpy as jnp
-import ml_dtypes
-import numpy as np
 from jax import lax
 from jax.experimental import pallas as pl
 from jax.experimental.pallas import tpu as pltpu
@@ -25,74 +23,75 @@
     return -(-number // unit) * unit
 
 
-def phase_table(rows, cols, period):
-    residue = np.arange(rows)[:, None] * np.arange(cols)[None, :] % period
-    angle = residue * (2.0 * math.pi / period)
-    return np.cos(angle), -np.sin(angle)
-
-
 def unit_phase(residue, period):
     angle = residue.astype(f32) * (2.0 * math.pi / period)
     return jnp.cos(angle), -jnp.sin(angle)
 
 
+def split_phase(coarse, fine, width, step, offset, period):
+    col = step * jnp.arange(width, dtype=jnp.int32) + offset
+    cr, ci = unit_phase(fine * jnp.arange(coarse, dtype=jnp.int32)[:, None] * col % period, period)
+    fr, fi = unit_phase(jnp.arange(fine, dtype=jnp.int32)[:, None] * col % period, period)
+    cr, ci, fr, fi = cr[:, None], ci[:, None], fr[None], fi[None]
+    return (
+        (cr * fr - ci * fi).reshape(coarse * fine, width),
+        (cr * fi + ci * fr).reshape(coarse * fine, width),
+    )
+
+
 def window_kernel(
-    tix_ref, r0_ref, c0_ref,
-    own_ref, oth_ref, p1_ref, p0_ref, tcos_ref, tsin_ref,
-    lr0_ref, li0_ref, lr1_ref, li1_ref, ar_ref, ai_ref, br_ref, bi_ref,
-    g_ref, rs_ref, *, chunk,
+    tix_ref, r0_ref, c0_ref, wr_ref, wi_ref,
+    own_hi_ref, own_lo_ref, oth_hi_ref, oth_lo_ref, p1_hi_ref, p1_lo_ref, p0_ref,
+    tcos_ref, tsin_ref, lr0_ref, li0_ref, lr1_ref, li1_ref,
+    ar_ref, ai_ref, br_ref, bi_ref,
+    g_ref, rs_ref, *, unroll,
 ):
     q = pl.program_id(0)
-    v_rows = rs_ref.shape[2]
-    chunks = v_rows // chunk
 
     def one_tile(k, carry):
         t = tix_ref[q, k]
-        scale = p1_ref[0, pl.ds(k, 1), :]
-        own = (own_ref[t].astype(f32) * scale).astype(bf16)
-        oth = (oth_ref[t].astype(f32) * scale).astype(bf16)
-        both = jnp.concatenate([own, oth], axis=0)
+        scale_hi = p1_hi_ref[0, pl.ds(k, 1), :]
+        scale_lo = p1_lo_ref[0, pl.ds(k, 1), :]
+        even, odd = [], []
+        for hi_ref, lo_ref in ((own_hi_ref, own_lo_ref), (oth_hi_ref, oth_lo_ref)):
+            hi = hi_ref[t].astype(f32) * scale_hi
+            lo = lo_ref[t].astype(f32) * scale_lo
+            even.append((hi + lo).astype(bf16))
+            odd.append((hi - lo).astype(bf16))
         row_scale = p0_ref[0, pl.ds(k, 1), :]
-
-        def one_chunk(i, inner):
-            at = pl.multiple_of(i * chunk, chunk)
-            for c, table in enumerate((tcos_ref, tsin_ref)):
-                got = lax.dot_general(
-                    table[pl.ds(at, chunk), :], both, (((1,), (1,)), ((), ())),
-                    preferred_element_type=f32,
-                ) * row_scale
-                for h in range(2):
-                    rs_ref[(h * 2 + c), k, pl.ds(at, chunk), :] = got[:, h * LANES:(h + 1) * LANES]
-            return inner
-
-        return lax.fori_loop(0, chunks, one_chunk, carry)
+        for c, (table, halves) in enumerate(((tcos_ref, even), (tsin_ref, odd))):
+            got = lax.dot_general(
+                table[...], jnp.concatenate(halves, axis=0), (((1,), (1,)), ((), ())),
+                preferred_element_type=f32,
+            ) * row_scale
+            for h in range(2):
+                rs_ref[h * 2 + c, k] = got[:, h * LANES:(h + 1) * LANES]
+        return carry
 
     lax.fori_loop(0, CAP, one_tile, 0)
 
     lane = lax.broadcasted_iota(jnp.int32, (2 * SG, LANES), 1)
     is_low = (lane // SG) == 1
 
-    def one_sub(s, carry):
+    def one_sub(s):
         r0 = r0_ref[q, s]
         c0 = c0_ref[q, s]
-        rows = []
-        for k in range(CAP):
-            rows.append(jnp.concatenate(
-                [rs_ref[j, k, pl.ds(c0, SG), :].astype(bf16) for j in range(4)], axis=1))
-        windows = jnp.concatenate(rows, axis=0)
-        lr0 = lr0_ref[pl.ds(r0, SG), :].astype(bf16)
-        li0 = li0_ref[pl.ds(r0, SG), :].astype(bf16)
-        lr1 = lr1_ref[pl.ds(r0, SG), :].astype(bf16)
-        li1 = li1_ref[pl.ds(r0, SG), :].astype(bf16)
+        windows = jnp.concatenate([
+            jnp.concatenate([rs_ref[j, k, pl.ds(c0, SG), :].astype(bf16) for j in range(4)], axis=1)
+            for k in range(CAP)
+        ], axis=0)
+        lr0, li0, lr1, li1 = (
+            ref[pl.ds(r0, SG), :].astype(bf16) for ref in (lr0_ref, li0_ref, lr1_ref, li1_ref))
         left = jnp.concatenate([
             jnp.concatenate([lr0, -li0, lr1, -li1], axis=1),
             jnp.concatenate([li0, lr0, li1, lr1], axis=1),
         ], axis=0)
         out = lax.dot_general(left, windows, (((1,), (1,)), ((), ())), preferred_element_type=f32)
-        r8 = lax.rem(r0, 8)
-        c8 = lax.rem(c0, 8)
+        r8, c8 = lax.rem(r0, 8), lax.rem(c0, 8)
         ar, ai = ar_ref[0, r8], ai_ref[0, r8]
         br, bi = br_ref[0, c8], bi_ref[0, c8]
+        wr, wi = wr_ref[q, s], wi_ref[q, s]
+        br, bi = br * wr - bi * wi, br * wi + bi * wr
         fr = ar * br - ai * bi
         fi = ar * bi + ai * br
         re_parts, im_parts = [], []
@@ -108,19 +107,23 @@
         high = half.astype(bf16)
         low = half - high.astype(f32)
         g_ref[0, s] = jnp.where(is_low, low, half).astype(bf16)
+
+    def some_subs(i, carry):
+        for u in range(unroll):
+            one_sub(i * unroll + u)
         return carry
 
-    lax.fori_loop(0, r0_ref.shape[1], one_sub, 0)
-
-
-def degrid_kernel(g_ref, off_ref, out_ref, acc_ref):
+    lax.fori_loop(0, r0_ref.shape[1] // unroll, some_subs, 0)
+
+
+def degrid_kernel(turn_ref, g_ref, off_ref, out_ref, acc_ref, *, unroll):
     subs = g_ref.shape[1]
     samples = off_ref.shape[3]
     places = lax.broadcasted_iota(jnp.int32, (SG, samples), 0).astype(f32)
     factor = -math.log2(math.e) / kernel_width**2
     blank = jnp.zeros((LANES - 3 * SG, samples), bf16)
 
-    def one_sub(s, carry):
+    def one_sub(s):
         tu = places - off_ref[0, s, 0:1, :]
         tv = places - off_ref[0, s, 1:2, :]
         wu = jnp.exp2(tu * tu * factor)
@@ -132,9 +135,13 @@
         re = jnp.sum(inner[:SG] * wu, axis=0, keepdims=True)
         im = jnp.sum(inner[SG:] * wu, axis=0, keepdims=True)
         acc_ref[pl.ds(s, 1), :] = jnp.concatenate([re, im], axis=1)
+
+    def some_subs(i, carry):
+        for u in range(unroll):
+            one_sub(i * unroll + u)
         return carry
 
-    lax.fori_loop(0, subs, one_sub, 0, unroll=4)
+    lax.fori_loop(0, subs // unroll, some_subs, 0)
     out_ref[0, 0, 0] = acc_ref[...].astype(out_ref.dtype)
 
 
@@ -178,7 +185,8 @@
     small = jnp.concatenate([chosen.reshape(-1), r0_mine.astype(f32), c0_mine.astype(f32)]).reshape(-1, LANES)
     steps = [(my_beam // 2 + t) % quads for t in range(quads)]
     smalls = jnp.stack([lax.ppermute(small, axes, turn(t)) for t in range(quads)]).reshape(quads, -1)
-    offs = jnp.stack([lax.ppermute(off_mine, axes, turn(t)) for t in range(quads)])
+    smalls, off_mine = lax.optimization_barrier((smalls, off_mine))
+    offs = [lax.ppermute(off_mine, axes, turn(t)) for t in range(quads)]
     beam_ids = jnp.stack([2 * s + my_core for s in steps])
     prof = smalls[:, :2 * image_side].reshape(quads, 2, image_side)
     r0_all = smalls[:, 2 * image_side:2 * image_side + subs].astype(jnp.int32)
@@ -207,61 +215,77 @@
     lane_j = jnp.repeat(tile_j, SG, axis=1)
     ar, ai = unit_phase(
         lane_i[:, None, None, :] * (eights[:, None] + eights[None, :])[None, :, :, None] % FT, FT)
+    middle = 2 * image_side
     br, bi = unit_phase(
-        lane_j[:, None, :] * (eights[None, :, None] + lane_e[None, None, :]) % FT, FT)
+        (middle // FT * lane_j[:, None, :] * (eights[None, :, None] + lane_e[None, None, :])
+         + (tile_side - 1) * lane_e[None, None, :]) % middle, middle)
+    wr, wi = unit_phase((tile_side - 1) * c0_all % middle, middle)
     br = jnp.broadcast_to(br[:, :, None, :], ar.shape)
     bi = jnp.broadcast_to(bi[:, :, None, :], ai.shape)
 
-    chunk = 344
-    v_rows = 6 * chunk
-    t_cos, t_sin = phase_table(v_rows, tile_side, image_side)
-    t_cos, t_sin = jnp.asarray(t_cos.astype(ml_dtypes.bfloat16)), jnp.asarray(t_sin.astype(ml_dtypes.bfloat16))
-    u_rows = image_side + SG
-    u_cos, u_sin = phase_table(u_rows, LANES, image_side)
-    u_cos, u_sin = jnp.asarray(u_cos.astype(np.float32)), jnp.asarray(u_sin.astype(np.float32))
-    shift_r, shift_i = unit_phase(
-        fft_ids[:, None] * tile_rows * jnp.arange(u_rows, dtype=jnp.int32)[None, :] % image_side, image_side)
+    side_half = tile_side // 2
+    t_cos, t_sin = split_phase(129, 16, side_half, 2, 1, 2 * image_side)
+    t_cos, t_sin = t_cos.astype(bf16), t_sin.astype(bf16)
+    v_rows = t_cos.shape[0]
     left = []
     for h in range(2):
-        sr, si = shift_r[h][:, None], shift_i[h][:, None]
-        left += [u_cos * sr - u_sin * si, u_cos * si + u_sin * sr]
-
-    pad_rows = ((0, 0), (0, LANES - tile_rows), (0, 0))
-    own_sky, oth_sky = (jnp.pad(s, pad_rows) if tile_rows < LANES else s for s in (sky_model, oth_sky))
+        coarse, fine = (image_side + SG) // SG, SG
+        col = fft_ids[h] * tile_rows + jnp.arange(LANES, dtype=jnp.int32)
+        cr, ci = unit_phase(fine * jnp.arange(coarse, dtype=jnp.int32)[:, None] * col % image_side, image_side)
+        fr, fi = unit_phase(jnp.arange(fine, dtype=jnp.int32)[:, None] * col % image_side, image_side)
+        cr, ci, fr, fi = cr[:, None], ci[:, None], fr[None], fi[None]
+        left += [(cr * fr - ci * fi).reshape(-1, LANES), (cr * fi + ci * fr).reshape(-1, LANES)]
+
+    flip = jnp.arange(side_half)[:, None] + jnp.arange(side_half)[None, :] == side_half - 1
+    halves = []
+    for sky in (sky_model, oth_sky):
+        if tile_rows < LANES:
+            sky = jnp.pad(sky, ((0, 0), (0, LANES - tile_rows), (0, 0)))
+        low = jnp.einsum("trx,xy->try", sky[:, :, :side_half], flip.astype(bf16), preferred_element_type=f32)
+        halves += [sky[:, :, side_half:], low.astype(bf16)]
+    p1_lo = jnp.flip(p1[:, :, :side_half], axis=2)
+    p1_hi = p1[:, :, side_half:]
 
     whole = lambda a: pl.BlockSpec(a.shape, lambda q, *_: (0,) * a.ndim, pipeline_mode=pl.Buffered(1))
     per_beam = lambda a: pl.BlockSpec((1,) + a.shape[1:], lambda q, *_: (q,) + (0,) * (a.ndim - 1))
-    fixed = [own_sky, oth_sky]
-    operands = (own_sky, oth_sky, p1, p0, t_cos, t_sin, *left, ar, ai, br, bi)
-    specs = [whole(own_sky), whole(oth_sky), per_beam(p1), per_beam(p0), whole(t_cos), whole(t_sin)]
-    specs += [whole(x) for x in left] + [per_beam(x) for x in (ar, ai, br, bi)]
+    tables = [t_cos, t_sin, *left]
+    slabs, phases = [p1_hi, p1_lo, p0], [ar, ai, br, bi]
+    operands = halves + slabs + tables + phases
+    specs = [whole(x) for x in halves] + [per_beam(x) for x in slabs]
+    specs += [whole(x) for x in tables] + [per_beam(x) for x in phases]
     cuts = pl.pallas_call(
-        functools.partial(window_kernel, chunk=chunk),
+        functools.partial(window_kernel, unroll=16),
         out_shape=jax.ShapeDtypeStruct((quads, subs, 2 * SG, LANES), bf16),
         grid_spec=pltpu.PrefetchScalarGridSpec(
-            num_scalar_prefetch=3, grid=(quads,), in_specs=specs,
+            num_scalar_prefetch=5, grid=(quads,), in_specs=specs,
             out_specs=pl.BlockSpec((1, subs, 2 * SG, LANES), lambda q, *_: (q, 0, 0, 0)),
             scratch_shapes=[pltpu.VMEM((4, CAP, v_rows, LANES), f32)],
         ),
         compiler_params=pltpu.CompilerParams(vmem_limit_bytes=63 << 20),
         name="windows",
-    )(tix, r0_all, c0_all, *operands)
-
+    )(tix, r0_all, c0_all, wr, wi, *operands)
+
+    offs, cuts = lax.optimization_barrier((offs, cuts))
+    offs = jnp.stack(offs)
+    home = (my_beam // 2).astype(jnp.int32).reshape(1)
     partial = pl.pallas_call(
-        degrid_kernel,
-        grid=(quads, ffts),
-        in_specs=[
-            pl.BlockSpec((1, sub_dev, 2 * SG, LANES), lambda q, f: (q, f, 0, 0)),
-            pl.BlockSpec((1, sub_dev, 2, samples), lambda q, f: (q, f, 0, 0)),
-        ],
-        out_specs=pl.BlockSpec((1, 1, 1, sub_dev, 2 * samples), lambda q, f: (q, f % 2, f // 2, 0, 0)),
+        functools.partial(degrid_kernel, unroll=8),
+        grid_spec=pltpu.PrefetchScalarGridSpec(
+            num_scalar_prefetch=1, grid=(quads, ffts),
+            in_specs=[
+                pl.BlockSpec((1, sub_dev, 2 * SG, LANES), lambda q, f, _: (q, f, 0, 0)),
+                pl.BlockSpec((1, sub_dev, 2, samples), lambda q, f, _: (q, f, 0, 0)),
+            ],
+            out_specs=pl.BlockSpec(
+                (1, 1, 1, sub_dev, 2 * samples),
+                lambda q, f, home: (lax.rem(q + home[0], quads), lax.rem(f, 2), f // 2, 0, 0)),
+            scratch_shapes=[pltpu.VMEM((sub_dev, 2 * samples), f32)],
+        ),
         out_shape=jax.ShapeDtypeStruct((quads, 2, pairs, sub_dev, 2 * samples), bf16),
-        scratch_shapes=[pltpu.VMEM((sub_dev, 2 * samples), f32)],
         compiler_params=pltpu.CompilerParams(vmem_limit_bytes=32 << 20),
         name="degrid",
-    )(cuts, offs)
-
-    partial = jnp.roll(partial, my_beam // 2, axis=0)
+    )(home, cuts, offs)
+
     groups = [[b * ffts + 2 * x + c for b in range(beams) for x in range(pairs)] for c in range(2)]
     parts = partial.reshape(beams * pairs, sub_dev, 2 * samples)
     came = lax.all_to_all(parts, axes, 0, 0, tiled=True, axis_index_groups=groups)

time: 387 us -> 182 us (0.47)
  Pallas kernels: 296 us -> 103 us
  waiting for transfers between devices: 31.1 us -> 13.2 us
  matrix products: 0.18 us -> 5.56 us
    pallas_call x2, Pallas kernels: 296 us -> 103 us  [the longest x1 85.7 us: local(): pl.pallas_call(functools.partial(window_kernel, unroll=16), out_shape=jax...]
    ppermute x4, waiting for transfers between devices: 17.2 us -> 0.01 us  [local(): offs = [lax.ppermute(off_mine, axes, turn(t)) for t in range(quads)]]
    dot_general x0 -> x2, matrix products: none -> 5.38 us  [local(): jnp.einsum('trx,xy->try', sky[:, :, :side_half], flip.astype(bf16), prefe...]
  transfers between devices with their start and end apart: 11 -> 11, of which waited for: 3 -> 2; matrix products, arithmetic and copies ran while one was open for 5% -> 15% of each run, Pallas kernels for 0% -> 47%
where the time goes in v2:
time: 182 us
  Pallas kernels  103 us (57%)
  starting transfers between devices  28.9 us (16%)
  other arithmetic  17.4 us (10%)
  waiting for transfers between devices  13.2 us (7%)
  local copies, waits for them, and re-layouts  12.6 us (7%)
  matrix products  5.56 us (3%)
    pallas_call x1, Pallas kernels, local(): pl.pallas_call(functools.partial(window_kernel, unroll=16), out_shape=jax...  85.7 us
    pallas_call x1, Pallas kernels, local(): pl.pallas_call(functools.partial(degrid_kernel, unroll=8), grid_spec=pltp...  17.2 us
    all_to_all x1, waiting for transfers between devices, local(): lax.all_to_all(parts, axes, 0, 0, tiled=True, axis_index_groups=groups)  11.4 us
    ppermute x4, starting transfers between devices, local(): lax.ppermute(small, axes, turn(t))  10.2 us
    ppermute x1, starting transfers between devices, local(): total = lax.ppermute(total, axes, turn(0)) * (1.0 / image_side)  6.92 us
    ppermute x4, starting transfers between devices, local(): offs = [lax.ppermute(off_mine, axes, turn(t)) for t in range(quads)]  6.54 us
    dot_general x2, matrix products, local(): jnp.einsum('trx,xy->try', sky[:, :, :side_half], flip.astype(bf16), prefe...  5.38 us
    all_to_all x1, starting transfers between devices, local(): lax.all_to_all(parts, axes, 0, 0, tiled=True, axis_index_groups=groups)  5.19 us
  transfers between devices with their start and end apart: 11, of which 2 were waited for; matrix products, arithmetic and copies ran while one was open for 15% of the time, Pallas kernels for 47%

profile of v2, /device:TPU:1, one launch (start us, length us, event | category | flops | bytes accessed | tf_op | source)
XLA Modules:
  0.0 181.6 jit_solution(16267905950478122822)
XLA Ops:
  0.7 1.1 fusion.7
  1.9 0.7 fusion.69
  2.6 3.7 %collective-permute-start.3 = (f32[66,128]{1,0:T(8,128)S(1)}, f32[66,128]{1,0:T(8,128)S(1)}, u32[]{:S(2)}, u32[]{:S(2)}) collective-permute-start(f32[66,128]{1,0:T(8,128)S(1)} %maximum_bitcast_fusion.1), channel_id=1, source_target_pairs={{0,8},{1,12},{2,10},{3,14},{4,9},{5,13},{6,11},{7,15},{8,16},{9,20... | collective-permute-start | bytes 101384 | tf_op jit(solution)/shard_map/ppermute | solution.py:187
  6.3 2.0 %collective-permute-start.2 = (f32[66,128]{1,0:T(8,128)S(1)}, f32[66,128]{1,0:T(8,128)S(1)}, u32[]{:S(2)}, u32[]{:S(2)}) collective-permute-start(f32[66,128]{1,0:T(8,128)S(1)} %maximum_bitcast_fusion.1), channel_id=1, source_target_pairs={{0,16},{1,20},{2,18},{3,22},{4,17},{5,21},{6,19},{7,23},{8,24},{9,... | collective-permute-start | bytes 101384 | tf_op jit(solution)/shard_map/ppermute | solution.py:187
  8.3 2.6 %collective-permute-start.1 = (f32[66,128]{1,0:T(8,128)S(1)}, f32[66,128]{1,0:T(8,128)S(1)}, u32[]{:S(2)}, u32[]{:S(2)}) collective-permute-start(f32[66,128]{1,0:T(8,128)S(1)} %maximum_bitcast_fusion.1), channel_id=1, source_target_pairs={{0,24},{1,28},{2,26},{3,30},{4,25},{5,29},{6,27},{7,31},{8,0},{9,4... | collective-permute-start | bytes 101384 | tf_op jit(solution)/shard_map/ppermute | solution.py:187
  10.8 1.9 %collective-permute-start = (f32[66,128]{1,0:T(8,128)S(1)}, f32[66,128]{1,0:T(8,128)S(1)}, u32[]{:S(2)}, u32[]{:S(2)}) collective-permute-start(f32[66,128]{1,0:T(8,128)S(1)} %maximum_bitcast_fusion.1), channel_id=1, source_target_pairs={{0,0},{1,4},{2,2},{3,6},{4,1},{5,5},{6,3},{7,7},{8,8},{9,12},{10,1... | collective-permute-start | bytes 101384 | tf_op jit(solution)/shard_map/ppermute | solution.py:187
  12.8 0.1 collective-permute-start.8
  12.9 0.7 broadcast_compare_fusion.2
  13.7 2.7 %fusion.own_lo_ref = bf16[16,128,256]{2,1,0:T(8,128)(2,1)} fusion(bf16[16,128,512]{2,1,0:T(8,128)(2,1)} %param.10), kind=kOutput, calls=%fused_computation.10 | convolution fusion | flops 269090816 | bytes 2097152 | tf_op jit(solution)/shard_map/trx,xy->try/dot_general | solution.py:244
  16.3 0.1 fusion.54
  16.4 0.1 fusion.55
  16.5 0.6 fusion.26
  17.2 0.1 fusion.67
  17.3 0.6 gather_fusion
  17.8 0.1 compare_and_fusion.1
  17.9 0.1 fusion.63
  18.0 0.2 reduce_window_sum.11
  18.3 0.1 add_select_fusion.11
  18.3 0.9 select_reduce_fusion
  19.2 0.1 compare_and_fusion
  19.3 0.1 broadcast_bitcast_fusion
  19.5 0.1 fusion.53
  19.6 0.1 mul.725
  19.8 0.1 mul.733
  19.8 0.1 fusion.56
  19.9 0.6 fusion.24
  20.6 0.1 fusion.68
  20.7 0.2 subtract_select_fusion
  20.9 1.9 %sine_negate_fusion = (f32[4,8,8,256]{3,2,1,0:T(8,128)}, f32[4,8,8,256]{3,2,1,0:T(8,128)}) fusion(s32[8,8]{1,0:T(8,128)S(1)} %iota_add_fusion.1, s32[4,256]{1,0:T(4,128)S(1)} %mul.725), kind=kLoop, calls=%fused_computation.28 | loop fusion | flops 983040 | bytes 528640 | tf_op jit(solution)/shard_map/neg | solution.py:28
  22.8 0.1 sine_negate_fusion.4
  23.0 2.0 %add_convert_fusion = (bf16[129,16,256]{2,1,0:T(8,128)(2,1)}, bf16[129,16,256]{2,1,0:T(8,128)(2,1)}) fusion(f32[16,256]{1,0:T(8,128)S(1)} %get-tuple-element.56, f32[129,256]{1,0:T(8,128)S(1)} %get-tuple-element.45, f32[16,256]{1,0:T(8,128)S(1)} %get-tuple-element.55, f32[129,256]{1,0:T(8,128)S(1)} %get-tuple-element.44), kind=kLoop, calls=%fused_computation.6 | loop fusion | flops 4227072 | bytes 2410496 | tf_op jit(solution)/shard_map/convert_element_type | solution.py:228
  24.9 3.8 %multiply_add_fusion = (f32[129,32,128]{2,1,0:T(8,128)}, f32[129,32,128]{2,1,0:T(8,128)}, f32[129,32,128]{2,1,0:T(8,128)}, f32[129,32,128]{2,1,0:T(8,128)}) fusion(f32[32,128]{1,0:T(8,128)S(1)} %get-tuple-element.60, f32[129,128]{1,0:T(8,128)S(1)} %get-tuple-element.48, f32[32,128]{1,0:T(8,128)S(1)} %get-tuple-element.59, ...), kind=kLoop, calls=%fused_computation.2 | loop fusion | flops 6340608 | bytes 8783872 | tf_op jit(solution)/shard_map/add | solution.py:237
  28.7 1.1 slice.54.own_hi_ref
  30.0 0.1 pad_maximum_fusion.1
  30.2 3.6 %collective-permute-start.4 = (f32[128,2,256]{2,1,0:T(2,128)S(1)}, f32[128,2,256]{2,1,0:T(2,128)S(1)}, u32[]{:S(2)}, u32[]{:S(2)}) collective-permute-start(f32[128,2,256]{2,1,0:T(2,128)S(1)} %subtract_select_fusion), channel_id=1, source_target_pairs={{0,0},{1,4},{2,2},{3,6},{4,1},{5,5},{6,3},{7,7},{8,8},{9,12},{10,1... | collective-permute-start | bytes 786440 | tf_op jit(solution)/shard_map/ppermute | solution.py:189
  33.8 0.2 collective-permute-start.5
  34.0 2.7 %collective-permute-start.6 = (f32[128,2,256]{2,1,0:T(2,128)S(1)}, f32[128,2,256]{2,1,0:T(2,128)}, u32[]{:S(2)}, u32[]{:S(2)}) collective-permute-start(f32[128,2,256]{2,1,0:T(2,128)S(1)} %subtract_select_fusion), channel_id=1, source_target_pairs={{0,16},{1,20},{2,18},{3,22},{4,17},{5,21},{6,19},{7,23},{8,24},{9,... | collective-permute-start | bytes 786440 | tf_op jit(solution)/shard_map/ppermute | solution.py:189
  36.7 0.1 collective-permute-start.7
  36.7 0.1 reshape.1005
  37.0 0.2 slice_reduce_fusion
  37.2 0.2 multiply_reduce_fusion
  37.4 0.6 fusion.74
  38.1 0.8 rev.4.p1_lo_ref
  38.8 0.5 gather_fusion.1
  39.4 0.7 multiply_reduce_fusion.1.p0_ref
  40.1 0.7 sine_negate_fusion.8
  40.8 2.3 %slice.71.oth_hi_ref = bf16[16,128,256]{2,1,0:T(8,128)(2,1)} slice(bf16[16,128,512]{2,1,0:T(8,128)(2,1)} %collective-permute-done.8), slice={[0:16], [0:128], [256:512]} | slice | bytes 2097152 | tf_op jit(solution)/shard_map/slice | solution.py:245
  43.1 2.7 %fusion.1.oth_lo_ref = bf16[16,128,256]{2,1,0:T(8,128)(2,1)} fusion(bf16[16,128,512]{2,1,0:T(8,128)(2,1)} %collective-permute-done.8), kind=kOutput, calls=%fused_computation.11 | convolution fusion | flops 269090816 | bytes 2097152 | tf_op jit(solution)/shard_map/trx,xy->try/dot_general | solution.py:244
  45.8 0.7 broadcast_in_dim.56.br_ref
  46.5 0.7 broadcast_in_dim.57.bi_ref
  47.2 85.7 %windows.1.g_ref = bf16[4,128,64,128]{3,2,1,0:T(8,128)(2,1)} custom-call(s32[4,8]{1,0:T(4,128)} %get-tuple-element.21.tix_ref, s32[4,128]{1,0:T(4,128)} %get-tuple-element.33.r0_ref, s32[4,128]{1,0:T(4,128)} %get-tuple-element.32.c0_ref, f32[4,128]{1,0:T(4,128)} %get-tuple-element.31.wr_ref, f32[4,128]{1,0:T(4,128)} %get-tuple-element.30.wi_ref, ...), custom_call_target="tpu_custom_call" | custom-call | tf_op jit(solution)/shard_map/windows/pallas_call | solution.py:256
  132.9 1.5 pad_maximum_fusion.off_ref
  134.4 3.4 %copy-done.1 = bf16[4,128,64,128]{3,2,1,0:T(8,128)(2,1)S(1)} copy-done((bf16[4,128,64,128]{3,2,1,0:T(8,128)(2,1)S(1)}, bf16[4,128,64,128]{3,2,1,0:T(8,128)(2,1)}, u32[]{:S(2)}) %copy-start.1) | copy-done | bytes 8388632
  137.8 17.2 %degrid.1 = bf16[4,2,2,32,512]{4,3,2,1,0:T(8,128)(2,1)} custom-call(s32[1]{0:T(128)} %bitcast.2.turn_ref, bf16[4,128,64,128]{3,2,1,0:T(8,128)(2,1)S(1)} %copy-done.1, f32[4,128,2,256]{3,2,1,0:T(2,128)S(1)} %pad_maximum_fusion.off_ref), custom_call_target="tpu_custom_call" | custom-call | tf_op jit(solution)/shard_map/degrid/pallas_call | solution.py:271
  155.0 5.2 %all-to-all-start = ((bf16[16,32,512]{2,1,0:T(8,128)(2,1)}), bf16[16,32,512]{2,1,0:T(8,128)(2,1)S(1)}, u32[]{:S(2)}, u32[]{:S(2)}) async-start(bf16[16,32,512]{2,1,0:T(8,128)(2,1)} %bitcast.41), calls=%async_computation | async-start | bytes 1048576 | tf_op jit(solution)/shard_map/all_to_all | solution.py:291
  160.2 0.1 dynamic-slice_bitcast_fusion
  160.2 0.2 fusion.17
  160.4 11.4 %all-to-all-done = bf16[16,32,512]{2,1,0:T(8,128)(2,1)S(1)} async-done(((bf16[16,32,512]{2,1,0:T(8,128)(2,1)}), bf16[16,32,512]{2,1,0:T(8,128)(2,1)S(1)}, u32[]{:S(2)}, u32[]{:S(2)}) %all-to-all-start) | async-done | bytes 524320 | tf_op jit(solution)/shard_map/all_to_all | solution.py:291
  171.8 0.1 convert_reduce_fusion
  171.9 6.9 %collective-permute-start.9 = (f32[32,512]{1,0:T(8,128)S(1)}, f32[32,512]{1,0:T(8,128)S(1)}, u32[]{:S(2)}, u32[]{:S(2)}) collective-permute-start(f32[32,512]{1,0:T(8,128)S(1)} %convert_reduce_fusion), channel_id=1, source_target_pairs={{0,0},{1,4},{2,2},{3,6},{4,1},{5,5},{6,3},{7,7},{8,8},{9,12},{10,1... | collective-permute-start | bytes 196616 | tf_op jit(solution)/shard_map/ppermute | solution.py:293
  178.8 0.1 dynamic_slice.7
  178.9 1.8 %collective-permute-done.9 = f32[32,512]{1,0:T(8,128)S(1)} collective-permute-done((f32[32,512]{1,0:T(8,128)S(1)}, f32[32,512]{1,0:T(8,128)S(1)}, u32[]{:S(2)}, u32[]{:S(2)}) %collective-permute-start.9) | collective-permute-done | bytes 65568 | tf_op jit(solution)/shard_map/ppermute | solution.py:293
  180.9 0.1 multiply_subtract_fusion.2
  181.0 0.7 copy.38
  (54 shorter events, 0.7 us)
Async XLA Ops:
  0.0 160.2 %copy-start = (f32[2,630]{1,0:T(2,128)S(1)}, f32[2,630]{1,0:T(2,128)}, u32[]{:S(2)}) copy-start(f32[2,630]{1,0:T(2,128)} %param.19) | copy-start | bytes 15124
  0.0 17.3 %copy-start.4 = (s32[8,64]{1,0:T(8,128)S(1)}, s32[8,64]{1,0:T(8,128)}, u32[]{:S(2)}) copy-start(s32[8,64]{1,0:T(8,128)} %param.11) | copy-start | bytes 6148
  0.0 20.6 %copy-start.3 = (f32[1,128,2,256]{3,2,1,0:T(2,128)S(1)}, f32[1,128,2,256]{3,2,1,0:T(2,128)}, u32[]{:S(2)}) copy-start(f32[1,128,2,256]{3,2,1,0:T(2,128)} %param.17) | copy-start | bytes 786436
  2.6 27.2 %collective-permute-start.3 = (f32[66,128]{1,0:T(8,128)S(1)}, f32[66,128]{1,0:T(8,128)S(1)}, u32[]{:S(2)}, u32[]{:S(2)}) collective-permute-start(f32[66,128]{1,0:T(8,128)S(1)} %maximum_bitcast_fusion.1), channel_id=1, source_target_pairs={{0,8},{1,12},{2,10},{3,14},{4,9},{5,13},{6,11},{7,15},{8,16},{9,20... | collective-permute-start | bytes 101384 | tf_op jit(solution)/shard_map/ppermute | solution.py:187
  6.3 23.6 %collective-permute-start.2 = (f32[66,128]{1,0:T(8,128)S(1)}, f32[66,128]{1,0:T(8,128)S(1)}, u32[]{:S(2)}, u32[]{:S(2)}) collective-permute-start(f32[66,128]{1,0:T(8,128)S(1)} %maximum_bitcast_fusion.1), channel_id=1, source_target_pairs={{0,16},{1,20},{2,18},{3,22},{4,17},{5,21},{6,19},{7,23},{8,24},{9,... | collective-permute-start | bytes 101384 | tf_op jit(solution)/shard_map/ppermute | solution.py:187
  8.3 21.7 %collective-permute-start.1 = (f32[66,128]{1,0:T(8,128)S(1)}, f32[66,128]{1,0:T(8,128)S(1)}, u32[]{:S(2)}, u32[]{:S(2)}) collective-permute-start(f32[66,128]{1,0:T(8,128)S(1)} %maximum_bitcast_fusion.1), channel_id=1, source_target_pairs={{0,24},{1,28},{2,26},{3,30},{4,25},{5,29},{6,27},{7,31},{8,0},{9,4... | collective-permute-start | bytes 101384 | tf_op jit(solution)/shard_map/ppermute | solution.py:187
  10.8 19.1 %collective-permute-start = (f32[66,128]{1,0:T(8,128)S(1)}, f32[66,128]{1,0:T(8,128)S(1)}, u32[]{:S(2)}, u32[]{:S(2)}) collective-permute-start(f32[66,128]{1,0:T(8,128)S(1)} %maximum_bitcast_fusion.1), channel_id=1, source_target_pairs={{0,0},{1,4},{2,2},{3,6},{4,1},{5,5},{6,3},{7,7},{8,8},{9,12},{10,1... | collective-permute-start | bytes 101384 | tf_op jit(solution)/shard_map/ppermute | solution.py:187
  12.8 28.0 %collective-permute-start.8 = (bf16[16,128,512]{2,1,0:T(8,128)(2,1)}, bf16[16,128,512]{2,1,0:T(8,128)(2,1)}, u32[]{:S(2)}, u32[]{:S(2)}) collective-permute-start(bf16[16,128,512]{2,1,0:T(8,128)(2,1)} %param.10), channel_id=1, source_target_pairs={{0,1},{1,0},{2,3},{3,2},{4,5},{5,4},{6,7},{7,6},{8,9},{9,8},{10,11... | collective-permute-start | bytes 6291464 | tf_op jit(solution)/shard_map/ppermute | solution.py:176
  24.9 3.8 %copy-start.2 = (bf16[16,128,512]{2,1,0:T(8,128)(2,1)S(1)}, bf16[16,128,512]{2,1,0:T(8,128)(2,1)}, u32[]{:S(2)}) copy-start(bf16[16,128,512]{2,1,0:T(8,128)(2,1)} %param.10) | copy-start | bytes 6291460
  30.2 102.7 %collective-permute-start.4 = (f32[128,2,256]{2,1,0:T(2,128)S(1)}, f32[128,2,256]{2,1,0:T(2,128)S(1)}, u32[]{:S(2)}, u32[]{:S(2)}) collective-permute-start(f32[128,2,256]{2,1,0:T(2,128)S(1)} %subtract_select_fusion), channel_id=1, source_target_pairs={{0,0},{1,4},{2,2},{3,6},{4,1},{5,5},{6,3},{7,7},{8,8},{9,12},{10,1... | collective-permute-start | bytes 786440 | tf_op jit(solution)/shard_map/ppermute | solution.py:189
  33.8 99.1 %collective-permute-start.5 = (f32[128,2,256]{2,1,0:T(2,128)S(1)}, f32[128,2,256]{2,1,0:T(2,128)S(1)}, u32[]{:S(2)}, u32[]{:S(2)}) collective-permute-start(f32[128,2,256]{2,1,0:T(2,128)S(1)} %subtract_select_fusion), channel_id=1, source_target_pairs={{0,24},{1,28},{2,26},{3,30},{4,25},{5,29},{6,27},{7,31},{8,0},{9,4... | collective-permute-start | bytes 786440 | tf_op jit(solution)/shard_map/ppermute | solution.py:189
  34.0 98.9 %collective-permute-start.6 = (f32[128,2,256]{2,1,0:T(2,128)S(1)}, f32[128,2,256]{2,1,0:T(2,128)}, u32[]{:S(2)}, u32[]{:S(2)}) collective-permute-start(f32[128,2,256]{2,1,0:T(2,128)S(1)} %subtract_select_fusion), channel_id=1, source_target_pairs={{0,16},{1,20},{2,18},{3,22},{4,17},{5,21},{6,19},{7,23},{8,24},{9,... | collective-permute-start | bytes 786440 | tf_op jit(solution)/shard_map/ppermute | solution.py:189
  36.7 96.3 %collective-permute-start.7 = (f32[128,2,256]{2,1,0:T(2,128)S(1)}, f32[128,2,256]{2,1,0:T(2,128)}, u32[]{:S(2)}, u32[]{:S(2)}) collective-permute-start(f32[128,2,256]{2,1,0:T(2,128)S(1)} %subtract_select_fusion), channel_id=1, source_target_pairs={{0,8},{1,12},{2,10},{3,14},{4,9},{5,13},{6,11},{7,15},{8,16},{9,20... | collective-permute-start | bytes 786440 | tf_op jit(solution)/shard_map/ppermute | solution.py:189
  134.4 3.4 %copy-start.1 = (bf16[4,128,64,128]{3,2,1,0:T(8,128)(2,1)S(1)}, bf16[4,128,64,128]{3,2,1,0:T(8,128)(2,1)}, u32[]{:S(2)}) copy-start(bf16[4,128,64,128]{3,2,1,0:T(8,128)(2,1)} %windows.1.g_ref) | copy-start | bytes 25165828
  137.8 22.4 %copy-start.5 = (s32[1,128]{1,0:T(1,128)S(1)}, s32[1,128]{1,0:T(1,128)}, u32[]{:S(2)}) copy-start(s32[1,128]{1,0:T(1,128)} %param.18) | copy-start | bytes 1540
  155.0 16.8 %all-to-all-start = ((bf16[16,32,512]{2,1,0:T(8,128)(2,1)}), bf16[16,32,512]{2,1,0:T(8,128)(2,1)S(1)}, u32[]{:S(2)}, u32[]{:S(2)}) async-start(bf16[16,32,512]{2,1,0:T(8,128)(2,1)} %bitcast.41), calls=%async_computation | async-start | bytes 1048576 | tf_op jit(solution)/shard_map/all_to_all | solution.py:291
  171.9 8.9 %collective-permute-start.9 = (f32[32,512]{1,0:T(8,128)S(1)}, f32[32,512]{1,0:T(8,128)S(1)}, u32[]{:S(2)}, u32[]{:S(2)}) collective-permute-start(f32[32,512]{1,0:T(8,128)S(1)} %convert_reduce_fusion), channel_id=1, source_target_pairs={{0,0},{1,4},{2,2},{3,6},{4,1},{5,5},{6,3},{7,7},{8,8},{9,12},{10,1... | collective-permute-start | bytes 196616 | tf_op jit(solution)/shard_map/ppermute | solution.py:293

commit v3 on v2

--- a/solution.py
+++ b/solution.py
@@ -28,47 +28,65 @@
     return jnp.cos(angle), -jnp.sin(angle)
 
 
-def split_phase(coarse, fine, width, step, offset, period):
-    col = step * jnp.arange(width, dtype=jnp.int32) + offset
+def split_phase(coarse, fine, col, period):
     cr, ci = unit_phase(fine * jnp.arange(coarse, dtype=jnp.int32)[:, None] * col % period, period)
     fr, fi = unit_phase(jnp.arange(fine, dtype=jnp.int32)[:, None] * col % period, period)
     cr, ci, fr, fi = cr[:, None], ci[:, None], fr[None], fi[None]
-    return (
-        (cr * fr - ci * fi).reshape(coarse * fine, width),
-        (cr * fi + ci * fr).reshape(coarse * fine, width),
-    )
+    return (cr * fr - ci * fi).reshape(-1, col.shape[0]), (cr * fi + ci * fr).reshape(-1, col.shape[0])
 
 
 def window_kernel(
-    tix_ref, r0_ref, c0_ref, wr_ref, wi_ref,
-    own_hi_ref, own_lo_ref, oth_hi_ref, oth_lo_ref, p1_hi_ref, p1_lo_ref, p0_ref,
+    ffts_ref, tix_ref, ti_ref, tj_ref, valid_ref, r0_ref, c0_ref, wr_ref, wi_ref,
+    own_ref, oth_ref, prof_ref, flip_ref,
     tcos_ref, tsin_ref, lr0_ref, li0_ref, lr1_ref, li1_ref,
     ar_ref, ai_ref, br_ref, bi_ref,
-    g_ref, rs_ref, *, unroll,
+    g_ref, rs_ref, low_ref, *, ffts, unroll,
 ):
     q = pl.program_id(0)
-
-    def one_tile(k, carry):
-        t = tix_ref[q, k]
-        scale_hi = p1_hi_ref[0, pl.ds(k, 1), :]
-        scale_lo = p1_lo_ref[0, pl.ds(k, 1), :]
-        even, odd = [], []
-        for hi_ref, lo_ref in ((own_hi_ref, own_lo_ref), (oth_hi_ref, oth_lo_ref)):
-            hi = hi_ref[t].astype(f32) * scale_hi
-            lo = lo_ref[t].astype(f32) * scale_lo
+    side = own_ref.shape[2]
+    half_side = side // 2
+    per_tile = side // LANES
+    per_half = per_tile // 2
+    first_v = FT * ffts
+
+    def prof_row(at):
+        return prof_ref[0, pl.ds(at, 1), :]
+
+    low_prof = jnp.concatenate(
+        [prof_ref[0, pl.ds(first_v + p, FT, stride=per_tile), :] for p in range(per_half)], axis=1)
+    low_ref[...] = jnp.dot(
+        low_prof, flip_ref[...].astype(f32), precision=highest, preferred_element_type=f32)
+
+    def some_tiles(step, carry):
+        even, odd, row_scales = [], [], []
+        for n in range(2):
+            k = step * 2 + n
+            t, i, j = tix_ref[q, k], ti_ref[q, k], tj_ref[q, k]
+            scale_hi = jnp.concatenate(
+                [prof_row(first_v + j * per_tile + p) for p in range(per_half, per_tile)], axis=1)
+            scale_lo = low_ref[pl.ds(j, 1), :]
+            lo = jnp.dot(
+                jnp.concatenate([own_ref[t, :, :half_side], oth_ref[t, :, :half_side]], axis=0),
+                flip_ref[...], preferred_element_type=f32) * scale_lo
+            hi = jnp.concatenate(
+                [own_ref[t, :, half_side:], oth_ref[t, :, half_side:]], axis=0).astype(f32) * scale_hi
             even.append((hi + lo).astype(bf16))
             odd.append((hi - lo).astype(bf16))
-        row_scale = p0_ref[0, pl.ds(k, 1), :]
-        for c, (table, halves) in enumerate(((tcos_ref, even), (tsin_ref, odd))):
+            for h in range(2):
+                row_scales.append(prof_row(i * ffts + ffts_ref[h]) * valid_ref[q, k])
+        row_scale = jnp.concatenate(row_scales, axis=1)
+        for c, (table, parts) in enumerate(((tcos_ref, even), (tsin_ref, odd))):
             got = lax.dot_general(
-                table[...], jnp.concatenate(halves, axis=0), (((1,), (1,)), ((), ())),
+                table[...], jnp.concatenate(parts, axis=0), (((1,), (1,)), ((), ())),
                 preferred_element_type=f32,
             ) * row_scale
-            for h in range(2):
-                rs_ref[h * 2 + c, k] = got[:, h * LANES:(h + 1) * LANES]
+            for n in range(2):
+                for h in range(2):
+                    at = (2 * n + h) * LANES
+                    rs_ref[h * 2 + c, step * 2 + n] = got[:, at:at + LANES]
         return carry
 
-    lax.fori_loop(0, CAP, one_tile, 0)
+    lax.fori_loop(0, CAP // 2, some_tiles, 0)
 
     lane = lax.broadcasted_iota(jnp.int32, (2 * SG, LANES), 1)
     is_low = (lane // SG) == 1
@@ -88,8 +106,10 @@
         ], axis=0)
         out = lax.dot_general(left, windows, (((1,), (1,)), ((), ())), preferred_element_type=f32)
         r8, c8 = lax.rem(r0, 8), lax.rem(c0, 8)
-        ar, ai = ar_ref[0, r8], ai_ref[0, r8]
-        br, bi = br_ref[0, c8], bi_ref[0, c8]
+        ar, ai = (
+            jnp.concatenate([ref[0, p, pl.ds(r8, 8), :] for p in range(2)], axis=1)
+            for ref in (ar_ref, ai_ref))
+        br, bi = br_ref[0, pl.ds(c8, 1), :], bi_ref[0, pl.ds(c8, 1), :]
         wr, wi = wr_ref[q, s], wi_ref[q, s]
         br, bi = br * wr - bi * wi, br * wi + bi * wr
         fr = ar * br - ai * bi
@@ -175,22 +195,23 @@
 
     oth_sky = lax.ppermute(sky_model, "fft", [(f, f ^ 1) for f in range(ffts)])
 
-    channel_pick = (jnp.arange(profile.shape[1], dtype=jnp.int32) == chan_block[0]).astype(f32)
-    chosen = jnp.sum(profile[0] * channel_pick[:, None, None], axis=0)
+    chosen = lax.dynamic_index_in_dim(profile[0], chan_block[0], 0, keepdims=False)
     col_at = sub_strip[0, :, 0] * strip_cols + sub_col[0]
     mirrored = col_at >= half_side
     r0_mine = jnp.where(mirrored, (image_side - (SG - 1) - sub_row[0]) % image_side, sub_row[0])
     c0_mine = jnp.where(mirrored, image_side - (SG - 1) - col_at, col_at)
     off_mine = jnp.where(mirrored[:, None, None], (SG - 1) - offsets[0], offsets[0])
-    small = jnp.concatenate([chosen.reshape(-1), r0_mine.astype(f32), c0_mine.astype(f32)]).reshape(-1, LANES)
-    steps = [(my_beam // 2 + t) % quads for t in range(quads)]
-    smalls = jnp.stack([lax.ppermute(small, axes, turn(t)) for t in range(quads)]).reshape(quads, -1)
-    smalls, off_mine = lax.optimization_barrier((smalls, off_mine))
+    prof_u = jnp.pad(chosen[0].reshape(FT * ffts, tile_rows), ((0, 0), (0, LANES - tile_rows)))
+    small = jnp.concatenate([
+        prof_u, chosen[1].reshape(-1, LANES),
+        r0_mine.astype(f32).reshape(-1, LANES), c0_mine.astype(f32).reshape(-1, LANES)])
+    smalls = jnp.stack([lax.ppermute(small, axes, turn(t)) for t in range(quads)])
     offs = [lax.ppermute(off_mine, axes, turn(t)) for t in range(quads)]
-    beam_ids = jnp.stack([2 * s + my_core for s in steps])
-    prof = smalls[:, :2 * image_side].reshape(quads, 2, image_side)
-    r0_all = smalls[:, 2 * image_side:2 * image_side + subs].astype(jnp.int32)
-    c0_all = smalls[:, 2 * image_side + subs:].astype(jnp.int32)
+    beam_ids = jnp.stack([2 * ((my_beam // 2 + t) % quads) + my_core for t in range(quads)])
+    prof_rows = FT * ffts + image_side // LANES
+    sub_rows = subs // LANES
+    r0_all = smalls[:, prof_rows:prof_rows + sub_rows].reshape(quads, subs).astype(jnp.int32)
+    c0_all = smalls[:, prof_rows + sub_rows:].reshape(quads, subs).astype(jnp.int32)
 
     lists = jnp.take(footprint, beam_ids, axis=0)
     hits = (lists // tiles_dev == my_beam).astype(jnp.int32)
@@ -200,70 +221,50 @@
     place = jnp.sum(slots * jnp.arange(FT * FT, dtype=jnp.int32)[None, :, None], axis=1)
     valid = jnp.sum(slots, axis=1).astype(f32)
     tile_i, tile_j = place // FT, place % FT
+    fft_ids = jnp.stack([my_fft, my_fft + 1 - 2 * my_core])
+
     eights = jnp.arange(FT, dtype=jnp.int32)
-    pick_i = (tile_i[:, :, None] == eights).astype(f32) * valid[:, :, None]
-    pick_j = (tile_j[:, :, None] == eights).astype(f32)
-    prof_u = prof[:, 0].reshape(quads, FT, ffts, tile_rows)
-    fft_ids = jnp.stack([my_fft, my_fft + 1 - 2 * my_core])
-    prof_u = jnp.take(prof_u, fft_ids, axis=2)
-    prof_u = jnp.pad(prof_u, ((0, 0), (0, 0), (0, 0), (0, LANES - tile_rows))).reshape(quads, FT, 2 * LANES)
-    p0 = jnp.sum(pick_i[:, :, :, None] * prof_u[:, None], axis=2)
-    p1 = jnp.sum(pick_j[:, :, :, None] * prof[:, 1].reshape(quads, 1, FT, tile_side), axis=2)
-
     lane_e = jnp.arange(CAP * SG, dtype=jnp.int32) % SG
-    lane_i = jnp.repeat(tile_i, SG, axis=1)
-    lane_j = jnp.repeat(tile_j, SG, axis=1)
-    ar, ai = unit_phase(
-        lane_i[:, None, None, :] * (eights[:, None] + eights[None, :])[None, :, :, None] % FT, FT)
+    lane_i = jnp.repeat(tile_i, SG, axis=1).reshape(quads, 2, 1, LANES)
+    lane_j = jnp.repeat(tile_j, SG, axis=1)[:, None, :]
+    ar, ai = unit_phase(lane_i * jnp.arange(16, dtype=jnp.int32)[:, None] % FT, FT)
     middle = 2 * image_side
     br, bi = unit_phase(
-        (middle // FT * lane_j[:, None, :] * (eights[None, :, None] + lane_e[None, None, :])
-         + (tile_side - 1) * lane_e[None, None, :]) % middle, middle)
+        (middle // FT * lane_j * (eights[:, None] + lane_e) + (tile_side - 1) * lane_e) % middle, middle)
     wr, wi = unit_phase((tile_side - 1) * c0_all % middle, middle)
-    br = jnp.broadcast_to(br[:, :, None, :], ar.shape)
-    bi = jnp.broadcast_to(bi[:, :, None, :], ai.shape)
 
     side_half = tile_side // 2
-    t_cos, t_sin = split_phase(129, 16, side_half, 2, 1, 2 * image_side)
+    t_cos, t_sin = split_phase(129, 16, 2 * jnp.arange(side_half, dtype=jnp.int32) + 1, middle)
     t_cos, t_sin = t_cos.astype(bf16), t_sin.astype(bf16)
     v_rows = t_cos.shape[0]
     left = []
     for h in range(2):
-        coarse, fine = (image_side + SG) // SG, SG
         col = fft_ids[h] * tile_rows + jnp.arange(LANES, dtype=jnp.int32)
-        cr, ci = unit_phase(fine * jnp.arange(coarse, dtype=jnp.int32)[:, None] * col % image_side, image_side)
-        fr, fi = unit_phase(jnp.arange(fine, dtype=jnp.int32)[:, None] * col % image_side, image_side)
-        cr, ci, fr, fi = cr[:, None], ci[:, None], fr[None], fi[None]
-        left += [(cr * fr - ci * fi).reshape(-1, LANES), (cr * fi + ci * fr).reshape(-1, LANES)]
-
-    flip = jnp.arange(side_half)[:, None] + jnp.arange(side_half)[None, :] == side_half - 1
-    halves = []
-    for sky in (sky_model, oth_sky):
-        if tile_rows < LANES:
-            sky = jnp.pad(sky, ((0, 0), (0, LANES - tile_rows), (0, 0)))
-        low = jnp.einsum("trx,xy->try", sky[:, :, :side_half], flip.astype(bf16), preferred_element_type=f32)
-        halves += [sky[:, :, side_half:], low.astype(bf16)]
-    p1_lo = jnp.flip(p1[:, :, :side_half], axis=2)
-    p1_hi = p1[:, :, side_half:]
+        left += split_phase((image_side + SG) // SG, SG, col, image_side)
+    place_z = jnp.arange(side_half, dtype=jnp.int32)
+    flip = (place_z[:, None] + place_z[None, :] == side_half - 1).astype(bf16)
+    if tile_rows < LANES:
+        pad_rows = ((0, 0), (0, LANES - tile_rows), (0, 0))
+        sky_model, oth_sky = jnp.pad(sky_model, pad_rows), jnp.pad(oth_sky, pad_rows)
 
     whole = lambda a: pl.BlockSpec(a.shape, lambda q, *_: (0,) * a.ndim, pipeline_mode=pl.Buffered(1))
     per_beam = lambda a: pl.BlockSpec((1,) + a.shape[1:], lambda q, *_: (q,) + (0,) * (a.ndim - 1))
-    tables = [t_cos, t_sin, *left]
-    slabs, phases = [p1_hi, p1_lo, p0], [ar, ai, br, bi]
-    operands = halves + slabs + tables + phases
-    specs = [whole(x) for x in halves] + [per_beam(x) for x in slabs]
-    specs += [whole(x) for x in tables] + [per_beam(x) for x in phases]
+    fixed = [flip, t_cos, t_sin, *left]
+    phases = [ar, ai, br, bi]
+    operands = [sky_model, oth_sky, smalls, *fixed, *phases]
+    specs = [whole(sky_model), whole(oth_sky), per_beam(smalls)]
+    specs += [whole(x) for x in fixed] + [per_beam(x) for x in phases]
     cuts = pl.pallas_call(
-        functools.partial(window_kernel, unroll=16),
+        functools.partial(window_kernel, ffts=ffts, unroll=16),
         out_shape=jax.ShapeDtypeStruct((quads, subs, 2 * SG, LANES), bf16),
         grid_spec=pltpu.PrefetchScalarGridSpec(
-            num_scalar_prefetch=5, grid=(quads,), in_specs=specs,
+            num_scalar_prefetch=9, grid=(quads,), in_specs=specs,
             out_specs=pl.BlockSpec((1, subs, 2 * SG, LANES), lambda q, *_: (q, 0, 0, 0)),
-            scratch_shapes=[pltpu.VMEM((4, CAP, v_rows, LANES), f32)],
+            scratch_shapes=[pltpu.VMEM((4, CAP, v_rows, LANES), f32), pltpu.VMEM((FT, side_half), f32)],
         ),
         compiler_params=pltpu.CompilerParams(vmem_limit_bytes=63 << 20),
         name="windows",
-    )(tix, r0_all, c0_all, wr, wi, *operands)
+    )(fft_ids, tix, tile_i, tile_j, valid, r0_all, c0_all, wr, wi, *operands)
 
     offs, cuts = lax.optimization_barrier((offs, cuts))
     offs = jnp.stack(offs)

time: 182 us -> 173 us (0.951)
  local copies, waits for them, and re-layouts: 12.6 us -> 6.75 us
  matrix products: 5.56 us -> 0.18 us
    dot_general x2 -> x0, matrix products: 5.38 us -> none  [local(): jnp.einsum('trx,xy->try', sky[:, :, :side_half], flip.astype(bf16), prefe...]
    slice x6 -> x1, local copies, waits for them, and re-layouts: 4.22 us -> 0.87 us  [local(): chosen[0].reshape(FT * ffts, tile_rows)]
    reduce_sum x3 -> x0, other arithmetic: 2.1 us -> none  [the longest x1 1.14 us: local(): chosen = jnp.sum(profile[0] * channel_pick[:, None, None], axis=0)]
    add x4 -> x3, other arithmetic: 3.82 us -> 3.84 us  [the longest x1 3.83 us: split_phase(): cr * fi + ci * fr]
  transfers between devices with their start and end apart: 11 -> 11, of which waited for: 2 -> 2; matrix products, arithmetic and copies ran while one was open for 15% -> 10% of each run, Pallas kernels for 47% -> 50%
where the time goes in v3:
time: 173 us; the launch traced here: 172 us
  Pallas kernels  103 us (60%)
  starting transfers between devices  29.9 us (17%)
  other arithmetic  18.6 us (11%)
  waiting for transfers between devices  13.1 us (8%)
  local copies, waits for them, and re-layouts  6.75 us (4%)
    pallas_call x1, Pallas kernels, local(): pl.pallas_call(functools.partial(window_kernel, ffts=ffts, unroll=16), ou...  85.7 us
    pallas_call x1, Pallas kernels, local(): pl.pallas_call(functools.partial(degrid_kernel, unroll=8), grid_spec=pltp...  17.1 us
    all_to_all x1, waiting for transfers between devices, local(): lax.all_to_all(parts, axes, 0, 0, tiled=True, axis_index_groups=groups)  11.2 us
    ppermute x4, starting transfers between devices, local(): lax.ppermute(small, axes, turn(t))  9.45 us
    ppermute x4, starting transfers between devices, local(): offs = [lax.ppermute(off_mine, axes, turn(t)) for t in range(quads)]  8.14 us
    ppermute x1, starting transfers between devices, local(): total = lax.ppermute(total, axes, turn(0)) * (1.0 / image_side)  7.07 us
    all_to_all x1, starting transfers between devices, local(): lax.all_to_all(parts, axes, 0, 0, tiled=True, axis_index_groups=groups)  5.19 us
    add x1, other arithmetic, split_phase(): cr * fi + ci * fr  3.83 us
  transfers between devices with their start and end apart: 11, of which 2 were waited for; matrix products, arithmetic and copies ran while one was open for 10% of the time, Pallas kernels for 50%

profile of v3, /device:TPU:1, one launch (start us, length us, event | category | flops | bytes accessed | tf_op | source)
XLA Modules:
  0.0 172.2 jit_solution(1256745292451184626)
XLA Ops:
  0.7 0.9 constant_dynamic-slice_fusion
  1.5 0.7 fusion.61
  2.3 4.5 %collective-permute-start.4 = (f32[66,128]{1,0:T(8,128)S(1)}, f32[66,128]{1,0:T(8,128)S(1)}, u32[]{:S(2)}, u32[]{:S(2)}) collective-permute-start(f32[66,128]{1,0:T(8,128)S(1)} %pad_maximum_fusion.2), channel_id=1, source_target_pairs={{0,0},{1,4},{2,2},{3,6},{4,1},{5,5},{6,3},{7,7},{8,8},{9,12},{10,1... | collective-permute-start | bytes 101384 | tf_op jit(solution)/shard_map/ppermute | solution.py:208
  6.8 3.1 %collective-permute-start.5 = (f32[66,128]{1,0:T(8,128)S(1)}, f32[66,128]{1,0:T(8,128)S(1)}, u32[]{:S(2)}, u32[]{:S(2)}) collective-permute-start(f32[66,128]{1,0:T(8,128)S(1)} %pad_maximum_fusion.2), channel_id=1, source_target_pairs={{0,24},{1,28},{2,26},{3,30},{4,25},{5,29},{6,27},{7,31},{8,0},{9,4... | collective-permute-start | bytes 101384 | tf_op jit(solution)/shard_map/ppermute | solution.py:208
  9.9 0.6 collective-permute-start.6
  10.5 1.2 collective-permute-start.7
  11.7 0.0 collective-permute-start.8
  11.8 0.7 fusion.flip_ref
  12.5 0.1 fusion.46
  12.5 0.1 fusion.47
  12.6 0.6 fusion.19
  13.3 0.1 fusion.59
  13.4 1.2 gather_fusion
  14.6 0.1 compare_and_fusion
  14.7 0.1 fusion.55
  14.8 0.2 reduce_window_sum.11
  15.1 0.1 add_select_fusion.11
  15.1 0.9 select_reduce_fusion
  16.0 0.6 broadcast_multiply_fusion.1
  16.6 0.1 broadcast_in_dim.32
  16.7 0.1 mul.667
  16.8 0.9 sine_negate_fusion.3
  17.7 0.1 broadcast_in_dim.33
  17.8 0.1 mul.675
  17.9 0.1 fusion.48
  18.0 0.8 sine_negate_fusion.4
  18.8 0.7 fusion.60
  19.4 0.6 fusion.11
  20.1 1.2 subtract_select_fusion
  21.2 1.9 %add_convert_fusion = (bf16[129,16,256]{2,1,0:T(8,128)(2,1)}, bf16[129,16,256]{2,1,0:T(8,128)(2,1)}) fusion(f32[16,256]{1,0:T(8,128)S(1)} %get-tuple-element.52, f32[129,256]{1,0:T(8,128)S(1)} %get-tuple-element.39, f32[16,256]{1,0:T(8,128)S(1)} %get-tuple-element.51, f32[129,256]{1,0:T(8,128)S(1)} %get-tuple-element.38), kind=kLoop, calls=%fused_computation.5 | loop fusion | flops 4227072 | bytes 2410496 | tf_op jit(solution)/shard_map/convert_element_type | solution.py:238
  23.2 3.8 %multiply_add_fusion = (f32[129,32,128]{2,1,0:T(8,128)}, f32[129,32,128]{2,1,0:T(8,128)}, f32[129,32,128]{2,1,0:T(8,128)}, f32[129,32,128]{2,1,0:T(8,128)}) fusion(f32[32,128]{1,0:T(8,128)S(1)} %get-tuple-element.56, f32[129,128]{1,0:T(8,128)S(1)} %get-tuple-element.44, f32[32,128]{1,0:T(8,128)S(1)} %get-tuple-element.55, ...), kind=kLoop, calls=%fused_computation.1 | loop fusion | flops 6340608 | bytes 8783872 | tf_op jit(solution)/shard_map/add | solution.py:35
  27.0 0.7 pad_add_fusion.ffts_ref
  27.7 0.6 convert_element_type.124.valid_ref
  28.3 0.0 collective-permute-done.4
  28.3 3.5 %collective-permute-start = (f32[128,2,256]{2,1,0:T(2,128)S(1)}, f32[128,2,256]{2,1,0:T(2,128)S(1)}, u32[]{:S(2)}, u32[]{:S(2)}) collective-permute-start(f32[128,2,256]{2,1,0:T(2,128)S(1)} %subtract_select_fusion), channel_id=1, source_target_pairs={{0,0},{1,4},{2,2},{3,6},{4,1},{5,5},{6,3},{7,7},{8,8},{9,12},{10,1... | collective-permute-start | bytes 786440 | tf_op jit(solution)/shard_map/ppermute | solution.py:209
  31.7 0.0 collective-permute-done.5
  31.7 2.9 %collective-permute-start.1 = (f32[128,2,256]{2,1,0:T(2,128)S(1)}, f32[128,2,256]{2,1,0:T(2,128)S(1)}, u32[]{:S(2)}, u32[]{:S(2)}) collective-permute-start(f32[128,2,256]{2,1,0:T(2,128)S(1)} %subtract_select_fusion), channel_id=1, source_target_pairs={{0,24},{1,28},{2,26},{3,30},{4,25},{5,29},{6,27},{7,31},{8,0},{9,4... | collective-permute-start | bytes 786440 | tf_op jit(solution)/shard_map/ppermute | solution.py:209
  34.6 0.0 collective-permute-done.6
  34.6 1.7 %collective-permute-start.2 = (f32[128,2,256]{2,1,0:T(2,128)S(1)}, f32[128,2,256]{2,1,0:T(2,128)}, u32[]{:S(2)}, u32[]{:S(2)}) collective-permute-start(f32[128,2,256]{2,1,0:T(2,128)S(1)} %subtract_select_fusion), channel_id=1, source_target_pairs={{0,16},{1,20},{2,18},{3,22},{4,17},{5,21},{6,19},{7,23},{8,24},{9,... | collective-permute-start | bytes 786440 | tf_op jit(solution)/shard_map/ppermute | solution.py:209
  36.3 0.0 collective-permute-done.7
  36.4 0.1 collective-permute-start.3
  36.5 0.6 slice_convert_fusion
  37.1 0.7 sine_negate_fusion.8
  37.7 0.0 collective-permute-done.8.oth_ref
  37.7 85.7 %windows.1.g_ref = bf16[4,128,64,128]{3,2,1,0:T(8,128)(2,1)} custom-call(s32[2]{0:T(128)} %pad_add_fusion.ffts_ref, s32[4,8]{1,0:T(4,128)} %get-tuple-element.17.tix_ref, s32[4,8]{1,0:T(4,128)} %copy-done.3, s32[4,8]{1,0:T(4,128)} %get-tuple-element.19.tj_ref, f32[4,8]{1,0:T(4,128)} %convert_element_type.124.valid_ref, s32[4,128]{1,0:T(4,128)} %bitcast.75, ...), custom_call_target="tpu_custom_call" | custom-call | tf_op jit(solution)/shard_map/windows/pallas_call | solution.py:257
  123.4 0.0 collective-permute-done
  123.4 0.0 collective-permute-done.1
  123.4 0.0 collective-permute-done.2
  123.5 0.0 collective-permute-done.3
  123.5 1.5 pad_maximum_fusion.off_ref
  125.0 3.4 %copy-done.1 = bf16[4,128,64,128]{3,2,1,0:T(8,128)(2,1)S(1)} copy-done((bf16[4,128,64,128]{3,2,1,0:T(8,128)(2,1)S(1)}, bf16[4,128,64,128]{3,2,1,0:T(8,128)(2,1)}, u32[]{:S(2)}) %copy-start.1) | copy-done | bytes 8388632
  128.4 17.1 %degrid.1 = bf16[4,2,2,32,512]{4,3,2,1,0:T(8,128)(2,1)} custom-call(s32[1]{0:T(128)} %bitcast.2.turn_ref, bf16[4,128,64,128]{3,2,1,0:T(8,128)(2,1)S(1)} %copy-done.1, f32[4,128,2,256]{3,2,1,0:T(2,128)S(1)} %pad_maximum_fusion.off_ref), custom_call_target="tpu_custom_call" | custom-call | tf_op jit(solution)/shard_map/degrid/pallas_call | solution.py:272
  145.5 5.2 %all-to-all-start = ((bf16[16,32,512]{2,1,0:T(8,128)(2,1)}), bf16[16,32,512]{2,1,0:T(8,128)(2,1)S(1)}, u32[]{:S(2)}, u32[]{:S(2)}) async-start(bf16[16,32,512]{2,1,0:T(8,128)(2,1)} %bitcast.37), calls=%async_computation | async-start | bytes 1048576 | tf_op jit(solution)/shard_map/all_to_all | solution.py:292
  150.7 0.0 copy-done.5
  150.7 0.1 fusion.56
  150.8 0.2 fusion.4
  151.0 11.2 %all-to-all-done = bf16[16,32,512]{2,1,0:T(8,128)(2,1)S(1)} async-done(((bf16[16,32,512]{2,1,0:T(8,128)(2,1)}), bf16[16,32,512]{2,1,0:T(8,128)(2,1)S(1)}, u32[]{:S(2)}, u32[]{:S(2)}) %all-to-all-start) | async-done | bytes 524320 | tf_op jit(solution)/shard_map/all_to_all | solution.py:292
  162.2 0.1 convert_reduce_fusion
  162.3 7.1 %collective-permute-start.9 = (f32[32,512]{1,0:T(8,128)S(1)}, f32[32,512]{1,0:T(8,128)S(1)}, u32[]{:S(2)}, u32[]{:S(2)}) collective-permute-start(f32[32,512]{1,0:T(8,128)S(1)} %convert_reduce_fusion), channel_id=1, source_target_pairs={{0,0},{1,4},{2,2},{3,6},{4,1},{5,5},{6,3},{7,7},{8,8},{9,12},{10,1... | collective-permute-start | bytes 196616 | tf_op jit(solution)/shard_map/ppermute | solution.py:294
  169.4 0.1 dynamic_slice.12
  169.5 1.8 %collective-permute-done.9 = f32[32,512]{1,0:T(8,128)S(1)} collective-permute-done((f32[32,512]{1,0:T(8,128)S(1)}, f32[32,512]{1,0:T(8,128)S(1)}, u32[]{:S(2)}, u32[]{:S(2)}) %collective-permute-start.9) | collective-permute-done | bytes 65568 | tf_op jit(solution)/shard_map/ppermute | solution.py:294
  171.4 0.1 fusion.63
  171.4 0.1 multiply_subtract_fusion.2
  171.5 0.7 copy.14
  (24 shorter events, 0.1 us)
Async XLA Ops:
  0.0 150.8 %copy-start = (f32[2,630]{1,0:T(2,128)S(1)}, f32[2,630]{1,0:T(2,128)}, u32[]{:S(2)}) copy-start(f32[2,630]{1,0:T(2,128)} %param.19) | copy-start | bytes 15124
  2.3 26.0 %collective-permute-start.4 = (f32[66,128]{1,0:T(8,128)S(1)}, f32[66,128]{1,0:T(8,128)S(1)}, u32[]{:S(2)}, u32[]{:S(2)}) collective-permute-start(f32[66,128]{1,0:T(8,128)S(1)} %pad_maximum_fusion.2), channel_id=1, source_target_pairs={{0,0},{1,4},{2,2},{3,6},{4,1},{5,5},{6,3},{7,7},{8,8},{9,12},{10,1... | collective-permute-start | bytes 101384 | tf_op jit(solution)/shard_map/ppermute | solution.py:208
  6.8 24.9 %collective-permute-start.5 = (f32[66,128]{1,0:T(8,128)S(1)}, f32[66,128]{1,0:T(8,128)S(1)}, u32[]{:S(2)}, u32[]{:S(2)}) collective-permute-start(f32[66,128]{1,0:T(8,128)S(1)} %pad_maximum_fusion.2), channel_id=1, source_target_pairs={{0,24},{1,28},{2,26},{3,30},{4,25},{5,29},{6,27},{7,31},{8,0},{9,4... | collective-permute-start | bytes 101384 | tf_op jit(solution)/shard_map/ppermute | solution.py:208
  9.9 24.7 %collective-permute-start.6 = (f32[66,128]{1,0:T(8,128)S(1)}, f32[66,128]{1,0:T(8,128)S(1)}, u32[]{:S(2)}, u32[]{:S(2)}) collective-permute-start(f32[66,128]{1,0:T(8,128)S(1)} %pad_maximum_fusion.2), channel_id=1, source_target_pairs={{0,16},{1,20},{2,18},{3,22},{4,17},{5,21},{6,19},{7,23},{8,24},{9,... | collective-permute-start | bytes 101384 | tf_op jit(solution)/shard_map/ppermute | solution.py:208
  10.5 25.8 %collective-permute-start.7 = (f32[66,128]{1,0:T(8,128)S(1)}, f32[66,128]{1,0:T(8,128)S(1)}, u32[]{:S(2)}, u32[]{:S(2)}) collective-permute-start(f32[66,128]{1,0:T(8,128)S(1)} %pad_maximum_fusion.2), channel_id=1, source_target_pairs={{0,8},{1,12},{2,10},{3,14},{4,9},{5,13},{6,11},{7,15},{8,16},{9,20... | collective-permute-start | bytes 101384 | tf_op jit(solution)/shard_map/ppermute | solution.py:208
  11.7 26.0 %collective-permute-start.8 = (bf16[16,128,512]{2,1,0:T(8,128)(2,1)}, bf16[16,128,512]{2,1,0:T(8,128)(2,1)}, u32[]{:S(2)}, u32[]{:S(2)}) collective-permute-start(bf16[16,128,512]{2,1,0:T(8,128)(2,1)} %own_ref.1), channel_id=1, source_target_pairs={{0,1},{1,0},{2,3},{3,2},{4,5},{5,4},{6,7},{7,6},{8,9},{9,8},{10,11... | collective-permute-start | bytes 6291464 | tf_op jit(solution)/shard_map/ppermute | solution.py:196
  16.6 10.4 %copy-start.3 = (s32[4,8]{1,0:T(4,128)}, s32[4,8]{1,0:T(4,128)S(1)}, u32[]{:S(2)}) copy-start(s32[4,8]{1,0:T(4,128)S(1)} %get-tuple-element.42.ti_ref) | copy-start | bytes 388
  28.3 95.2 %collective-permute-start = (f32[128,2,256]{2,1,0:T(2,128)S(1)}, f32[128,2,256]{2,1,0:T(2,128)S(1)}, u32[]{:S(2)}, u32[]{:S(2)}) collective-permute-start(f32[128,2,256]{2,1,0:T(2,128)S(1)} %subtract_select_fusion), channel_id=1, source_target_pairs={{0,0},{1,4},{2,2},{3,6},{4,1},{5,5},{6,3},{7,7},{8,8},{9,12},{10,1... | collective-permute-start | bytes 786440 | tf_op jit(solution)/shard_map/ppermute | solution.py:209
  31.7 91.7 %collective-permute-start.1 = (f32[128,2,256]{2,1,0:T(2,128)S(1)}, f32[128,2,256]{2,1,0:T(2,128)S(1)}, u32[]{:S(2)}, u32[]{:S(2)}) collective-permute-start(f32[128,2,256]{2,1,0:T(2,128)S(1)} %subtract_select_fusion), channel_id=1, source_target_pairs={{0,24},{1,28},{2,26},{3,30},{4,25},{5,29},{6,27},{7,31},{8,0},{9,4... | collective-permute-start | bytes 786440 | tf_op jit(solution)/shard_map/ppermute | solution.py:209
  34.6 88.8 %collective-permute-start.2 = (f32[128,2,256]{2,1,0:T(2,128)S(1)}, f32[128,2,256]{2,1,0:T(2,128)}, u32[]{:S(2)}, u32[]{:S(2)}) collective-permute-start(f32[128,2,256]{2,1,0:T(2,128)S(1)} %subtract_select_fusion), channel_id=1, source_target_pairs={{0,16},{1,20},{2,18},{3,22},{4,17},{5,21},{6,19},{7,23},{8,24},{9,... | collective-permute-start | bytes 786440 | tf_op jit(solution)/shard_map/ppermute | solution.py:209
  36.4 87.1 %collective-permute-start.3 = (f32[128,2,256]{2,1,0:T(2,128)S(1)}, f32[128,2,256]{2,1,0:T(2,128)}, u32[]{:S(2)}, u32[]{:S(2)}) collective-permute-start(f32[128,2,256]{2,1,0:T(2,128)S(1)} %subtract_select_fusion), channel_id=1, source_target_pairs={{0,8},{1,12},{2,10},{3,14},{4,9},{5,13},{6,11},{7,15},{8,16},{9,20... | collective-permute-start | bytes 786440 | tf_op jit(solution)/shard_map/ppermute | solution.py:209
  36.4 1.3 copy-start.2
  37.1 0.7 copy-start.4
  125.0 3.4 %copy-start.1 = (bf16[4,128,64,128]{3,2,1,0:T(8,128)(2,1)S(1)}, bf16[4,128,64,128]{3,2,1,0:T(8,128)(2,1)}, u32[]{:S(2)}) copy-start(bf16[4,128,64,128]{3,2,1,0:T(8,128)(2,1)} %windows.1.g_ref) | copy-start | bytes 25165828
  128.4 22.4 %copy-start.5 = (s32[1,128]{1,0:T(1,128)S(1)}, s32[1,128]{1,0:T(1,128)}, u32[]{:S(2)}) copy-start(s32[1,128]{1,0:T(1,128)} %param.18) | copy-start | bytes 1540
  145.5 16.7 %all-to-all-start = ((bf16[16,32,512]{2,1,0:T(8,128)(2,1)}), bf16[16,32,512]{2,1,0:T(8,128)(2,1)S(1)}, u32[]{:S(2)}, u32[]{:S(2)}) async-start(bf16[16,32,512]{2,1,0:T(8,128)(2,1)} %bitcast.37), calls=%async_computation | async-start | bytes 1048576 | tf_op jit(solution)/shard_map/all_to_all | solution.py:292
  162.3 9.0 %collective-permute-start.9 = (f32[32,512]{1,0:T(8,128)S(1)}, f32[32,512]{1,0:T(8,128)S(1)}, u32[]{:S(2)}, u32[]{:S(2)}) collective-permute-start(f32[32,512]{1,0:T(8,128)S(1)} %convert_reduce_fusion), channel_id=1, source_target_pairs={{0,0},{1,4},{2,2},{3,6},{4,1},{5,5},{6,3},{7,7},{8,8},{9,12},{10,1... | collective-permute-start | bytes 196616 | tf_op jit(solution)/shard_map/ppermute | solution.py:294

commit v4 on v3

v4 whole, which is shorter than its diff:
```python
import functools
import math

import jax
import jax.numpy as jnp
import numpy as np
from jax import lax
from jax.experimental import pallas as pl
from jax.experimental.pallas import tpu as pltpu
from jax.sharding import PartitionSpec as P

FT = 8
SG = 32
CAP = 8
LANES = 128
OFF_LEAST, OFF_MOST = 2.0, 29.0
OFF_STEP = (OFF_MOST - OFF_LEAST) / 65535.0

kernel_width = 1.5
highest = lax.Precision.HIGHEST
f32 = jnp.float32
bf16 = jnp.bfloat16


def phase_table(rows, cols, period):
    angle = np.asarray(rows * cols % period) * (2.0 * math.pi / period)
    return jnp.asarray(np.stack([np.cos(angle), -np.sin(angle)]).astype(np.float32))


def turn_by(xr, xi, yr, yi):
    return xr * yr - xi * yi, xr * yi + xi * yr


def window_kernel(
    lists_ref, r0_ref, c0_ref, wr_ref, wi_ref,
    own_ref, oth_ref, prof_ref, v_coarse_ref, v_fine_ref, u_coarse_ref, u_fine_ref, ea_ref, eb_ref,
    *rest, beams, ffts, quads, unroll,
):
    off_refs, rest = rest[:quads], rest[quads:]
    (out_ref, rs_ref, low_ref, flip_ref, tcos_ref, tsin_ref, left_ref,
     a_ref, b_ref, off_ref, acc_ref, slot_ref) = rest
    q = pl.program_id(0)
    my_beam = lax.axis_index("beam")
    my_fft = lax.axis_index("fft")
    my_core = lax.rem(my_fft, 2)
    fft_ids = (my_fft, my_fft + 1 - 2 * my_core)
    quad = lax.rem(my_beam // 2 + q, quads)
    beam = 2 * quad + my_core
    tiles_dev = own_ref.shape[0]
    half_side = own_ref.shape[2] // 2
    per_half = half_side // LANES
    per_tile = 2 * per_half
    first_v = FT * ffts
    fine_v, fine_u = v_fine_ref.shape[1], u_fine_ref.shape[2]

    @pl.when(q == 0)
    def _():
        row = lax.broadcasted_iota(jnp.int32, (half_side, half_side), 0)
        col = lax.broadcasted_iota(jnp.int32, (half_side, half_side), 1)
        flip_ref[...] = (row + col == half_side - 1).astype(f32).astype(bf16)

        def some_rows(i, carry):
            for n in range(3):
                a = i * 3 + n
                cos, sin = turn_by(
                    v_coarse_ref[0, pl.ds(a, 1), :], v_coarse_ref[1, pl.ds(a, 1), :],
                    v_fine_ref[0], v_fine_ref[1])
                at = pl.ds(pl.multiple_of(a * fine_v, fine_v), fine_v)
                tcos_ref[at, :] = cos.astype(bf16)
                tsin_ref[at, :] = sin.astype(bf16)
                at = pl.ds(pl.multiple_of(a * fine_u, fine_u), fine_u)
                for h, f in enumerate(fft_ids):
                    cos, sin = turn_by(
                        u_coarse_ref[0, f, pl.ds(a, 1), :], u_coarse_ref[1, f, pl.ds(a, 1), :],
                        u_fine_ref[0, f], u_fine_ref[1, f])
                    left_ref[2 * h, at, :] = cos
                    left_ref[2 * h + 1, at, :] = sin
            return carry

        lax.fori_loop(0, v_coarse_ref.shape[1] // 3, some_rows, 0)

    for k in range(CAP):
        for n in range(3):
            slot_ref[n, k] = 0

    def one_entry(p, found):
        tile = lists_ref[beam, p]
        hit = (tile // tiles_dev) == my_beam

        @pl.when(hit)
        def _():
            at = jnp.minimum(found, CAP - 1)
            slot_ref[0, at] = lax.rem(tile, tiles_dev)
            slot_ref[1, at] = p // FT
            slot_ref[2, at] = lax.rem(p, FT)

        return found + hit.astype(jnp.int32)

    found = lax.fori_loop(0, FT * FT, one_entry, 0, unroll=8)

    lane = lax.broadcasted_iota(jnp.int32, (16, LANES), 1)
    for part in range(2):
        for half in range(2):
            a_rows, b_rows = ea_ref[part, 0], eb_ref[part, 0]
            for n in range(CAP // 2):
                here = lane // SG == n
                k = half * (CAP // 2) + n
                a_rows = jnp.where(here, ea_ref[part, slot_ref[1, k]], a_rows)
                b_rows = jnp.where(here[:8], eb_ref[part, slot_ref[2, k]], b_rows)
            a_ref[part, half] = a_rows
            b_ref[part, half] = b_rows

    for t in range(quads):
        @pl.when(q == t)
        def _():
            code = off_refs[t][...].astype(jnp.int32).astype(f32)
            off_ref[...] = (code + 32768.0) * OFF_STEP + OFF_LEAST

    def prof_row(at):
        return prof_ref[0, pl.ds(at, 1), :]

    low_prof = jnp.concatenate(
        [prof_ref[0, pl.ds(first_v + p, FT, stride=per_tile), :] for p in range(per_half)], axis=1)
    low_ref[...] = jnp.dot(
        low_prof, flip_ref[...].astype(f32), precision=highest, preferred_element_type=f32)

    def some_tiles(step, carry):
        even, odd, row_scales = [], [], []
        for n in range(2):
            k = step * 2 + n
            t, i, j = slot_ref[0, k], slot_ref[1, k], slot_ref[2, k]
            valid = (k < found).astype(f32)
            scale_hi = jnp.concatenate(
                [prof_row(first_v + j * per_tile + p) for p in range(per_half, per_tile)], axis=1)
            scale_lo = low_ref[pl.ds(j, 1), :]
            lo = jnp.dot(
                jnp.concatenate([own_ref[t, :, :half_side], oth_ref[t, :, :half_side]], axis=0),
                flip_ref[...], preferred_element_type=f32) * scale_lo
            hi = jnp.concatenate(
                [own_ref[t, :, half_side:], oth_ref[t, :, half_side:]], axis=0).astype(f32) * scale_hi
            even.append((hi + lo).astype(bf16))
            odd.append((hi - lo).astype(bf16))
            for f in fft_ids:
                row_scales.append(prof_row(i * ffts + f) * valid)
        row_scale = jnp.concatenate(row_scales, axis=1)
        for c, (table, parts) in enumerate(((tcos_ref, even), (tsin_ref, odd))):
            got = lax.dot_general(
                table[...], jnp.concatenate(parts, axis=0), (((1,), (1,)), ((), ())),
                preferred_element_type=f32,
            ) * row_scale
            for n in range(2):
                for h in range(2):
                    at = (2 * n + h) * LANES
                    rs_ref[h * 2 + c, step * 2 + n] = got[:, at:at + LANES]
        return carry

    lax.fori_loop(0, CAP // 2, some_tiles, 0)

    samples = off_ref.shape[1]
    wide = lax.broadcasted_iota(jnp.int32, (2 * SG, LANES), 1)
    is_low = (wide // SG) == 1
    places = lax.broadcasted_iota(jnp.int32, (SG, samples), 0).astype(f32)
    factor = -math.log2(math.e) / kernel_width**2
    blank = jnp.zeros((LANES - 3 * SG, samples), bf16)

    def one_sub(s):
        r0 = r0_ref[q, s]
        code = c0_ref[q, s]
        mirrored = code >= 2 * FT * half_side
        c0 = jnp.where(mirrored, code - 2 * FT * half_side, code)
        windows = jnp.concatenate([
            jnp.concatenate([rs_ref[j, k, pl.ds(c0, SG), :].astype(bf16) for j in range(4)], axis=1)
            for k in range(CAP)
        ], axis=0)
        lr0, li0, lr1, li1 = (left_ref[n, pl.ds(r0, SG), :].astype(bf16) for n in range(4))
        left = jnp.concatenate([
            jnp.concatenate([lr0, -li0, lr1, -li1], axis=1),
            jnp.concatenate([li0, lr0, li1, lr1], axis=1),
        ], axis=0)
        out = lax.dot_general(left, windows, (((1,), (1,)), ((), ())), preferred_element_type=f32)
        r8, c8 = lax.rem(r0, 8), lax.rem(c0, 8)
        ar, ai = (
            jnp.concatenate([a_ref[part, half, pl.ds(r8, 8), :] for half in range(2)], axis=1)
            for part in range(2))
        br, bi = (
            jnp.concatenate([b_ref[part, half, pl.ds(c8, 1), :] for half in range(2)], axis=1)
            for part in range(2))
        br, bi = turn_by(br, bi, wr_ref[q, s], wi_ref[q, s])
        fr, fi = turn_by(ar, ai, br, bi)
        re_parts, im_parts = [], []
        for a in range(SG // 8):
            re, im = turn_by(out[a * 8:(a + 1) * 8], out[SG + a * 8:SG + (a + 1) * 8], fr, fi)
            re_parts.append(re)
            im_parts.append(im)
        full = jnp.concatenate(re_parts + im_parts, axis=0)
        half = full[:, :LANES] + full[:, LANES:]
        half = half + pltpu.roll(half, 2 * SG, 1)
        half = half + pltpu.roll(half, SG, 1)
        low = half - half.astype(bf16).astype(f32)
        cut = jnp.where(is_low, low, half).astype(bf16)

        base = jnp.where(mirrored, SG - 1.0, 0.0)
        way = jnp.where(mirrored, -1.0, 1.0)
        at = places * way + base
        tu = at - off_ref[pl.ds(2 * s, 1), :]
        tv = at - off_ref[pl.ds(2 * s + 1, 1), :]
        wu = jnp.exp2(tu * tu * factor)
        wv = jnp.exp2(tv * tv * factor)
        wv_high = wv.astype(bf16)
        wv_low = (wv - wv_high.astype(f32)).astype(bf16)
        right = jnp.concatenate([wv_high, wv_high, wv_low, blank], axis=0)
        inner = jnp.dot(cut, right, preferred_element_type=f32)
        re = jnp.sum(inner[:SG] * wu, axis=0, keepdims=True)
        im = jnp.sum(inner[SG:] * wu, axis=0, keepdims=True)
        acc_ref[pl.ds(s, 1), :] = jnp.concatenate([re, im], axis=1)

    def some_subs(i, carry):
        for u in range(unroll):
            one_sub(i * unroll + u)
        return carry

    subs = acc_ref.shape[0]
    lax.fori_loop(0, subs // unroll, some_subs, 0)
    sub_dev = subs // ffts
    for f in range(ffts):
        out_ref[quad, f % 2, f // 2] = acc_ref[f * sub_dev:(f + 1) * sub_dev].astype(out_ref.dtype)


def local(
    sky_model, footprint, profile, chan_block, sub_strip, sub_row, sub_col,
    offsets, sub_base, gain_table,
):
    axes = ("beam", "fft")
    beams = lax.axis_size("beam")
    ffts = lax.axis_size("fft")
    my_fft = lax.axis_index("fft")
    quads = beams // 2
    pairs = ffts // 2
    tiles_dev, tile_rows, tile_side = sky_model.shape
    image_side = FT * tile_side
    half_side = image_side // 2
    subs = sub_row.shape[1]
    sub_dev = subs // ffts
    samples = offsets.shape[3]
    strip_cols = image_side // ffts

    def turn(step):
        out = []
        for b in range(beams):
            for f in range(ffts):
                target = (2 * ((b // 2 - step) % quads) + f % 2) * ffts + 2 * (f // 2) + b % 2
                out.append((b * ffts + f, target))
        return out

    oth_sky = lax.ppermute(sky_model, "fft", [(f, f ^ 1) for f in range(ffts)])

    chosen = lax.dynamic_index_in_dim(profile[0], chan_block[0], 0, keepdims=False)
    col_at = sub_strip[0, :, 0] * strip_cols + sub_col[0]
    mirrored = col_at >= half_side
    r0_mine = jnp.where(mirrored, (image_side - (SG - 1) - sub_row[0]) % image_side, sub_row[0])
    c0_mine = jnp.where(mirrored, image_side - (SG - 1) - col_at, col_at)
    middle = 2 * image_side
    angle = ((tile_side - 1) * c0_mine % middle).astype(f32) * (2.0 * math.pi / middle)
    code_mine = jnp.where(mirrored, c0_mine + image_side, c0_mine)
    prof_u = jnp.pad(chosen[0].reshape(FT * ffts, tile_rows), ((0, 0), (0, LANES - tile_rows)))
    per_sub = [r0_mine.astype(f32), code_mine.astype(f32), jnp.cos(angle), -jnp.sin(angle)]
    small = jnp.concatenate(
        [prof_u, chosen[1].reshape(-1, LANES)] + [x.reshape(-1, LANES) for x in per_sub])
    smalls = jnp.stack([lax.ppermute(small, axes, turn(t)) for t in range(quads)])
    off_code = jnp.round((offsets[0].reshape(2 * subs, samples) - OFF_LEAST) * (1.0 / OFF_STEP)) - 32768.0
    off_code = off_code.astype(jnp.int16)
    offs = [lax.ppermute(off_code, axes, turn(t)) for t in range(quads)]
    sub_parts = smalls[:, FT * ffts + image_side // LANES:].reshape(quads, 4, subs)
    r0_all, c0_all = sub_parts[:, 0].astype(jnp.int32), sub_parts[:, 1].astype(jnp.int32)
    wr, wi = sub_parts[:, 2], sub_parts[:, 3]

    side_half = tile_side // 2
    coarse, fine_v, fine_u = 129, image_side // 256, SG
    v_col = 2 * np.arange(side_half) + 1
    v_coarse = phase_table(fine_v * np.arange(coarse)[:, None], v_col, middle)
    v_fine = phase_table(np.arange(fine_v)[:, None], v_col, middle)
    u_col = np.arange(ffts)[:, None, None] * tile_rows + np.arange(LANES)
    u_coarse = phase_table(fine_u * np.arange(coarse)[:, None], u_col, image_side)
    u_fine = phase_table(np.arange(fine_u)[:, None], u_col, image_side)
    lane_e = np.arange(LANES) % SG
    eights = np.arange(FT)[:, None, None]
    ea = phase_table(eights * np.arange(16)[:, None], np.ones(LANES, np.int64), FT)
    eb = phase_table(
        middle // FT * eights * (np.arange(8)[:, None] + lane_e) + (tile_side - 1) * lane_e, 1, middle)
    v_rows, u_rows = coarse * fine_v, coarse * fine_u
    if tile_rows < LANES:
        pad_rows = ((0, 0), (0, LANES - tile_rows), (0, 0))
        sky_model, oth_sky = jnp.pad(sky_model, pad_rows), jnp.pad(oth_sky, pad_rows)

    whole = lambda a: pl.BlockSpec(a.shape, lambda q, *_: (0,) * a.ndim, pipeline_mode=pl.Buffered(1))
    per_beam = lambda a: pl.BlockSpec((1,) + a.shape[1:], lambda q, *_: (q,) + (0,) * (a.ndim - 1))
    fixed = [v_coarse, v_fine, u_coarse, u_fine, ea, eb, *offs]
    out_shape = (quads, 2, pairs, sub_dev, 2 * samples)
    partial = pl.pallas_call(
        functools.partial(window_kernel, beams=beams, ffts=ffts, quads=quads, unroll=8),
        out_shape=jax.ShapeDtypeStruct(out_shape, bf16),
        grid_spec=pltpu.PrefetchScalarGridSpec(
            num_scalar_prefetch=5, grid=(quads,),
            in_specs=[whole(sky_model), whole(oth_sky), per_beam(smalls)] + [whole(x) for x in fixed],
            out_specs=pl.BlockSpec(out_shape, lambda q, *_: (0,) * len(out_shape)),
            scratch_shapes=[
                pltpu.VMEM((4, CAP, v_rows, LANES), f32),
                pltpu.VMEM((FT, side_half), f32),
                pltpu.VMEM((side_half, side_half), bf16),
                pltpu.VMEM((v_rows, side_half), bf16),
                pltpu.VMEM((v_rows, side_half), bf16),
                pltpu.VMEM((4, u_rows, LANES), f32),
                pltpu.VMEM((2, 2, 16, LANES), f32),
                pltpu.VMEM((2, 2, 8, LANES), f32),
                pltpu.VMEM((2 * subs, samples), f32),
                pltpu.VMEM((subs, 2 * samples), f32),
                pltpu.SMEM((3, CAP), jnp.int32),
            ],
        ),
        compiler_params=pltpu.CompilerParams(vmem_limit_bytes=63 << 20),
        name="windows",
    )(footprint, r0_all, c0_all, wr, wi, sky_model, oth_sky, smalls, *fixed)

    groups = [[b * ffts + 2 * x + c for b in range(beams) for x in range(pairs)] for c in range(2)]
    parts = partial.reshape(beams * pairs, sub_dev, 2 * samples)
    came = lax.all_to_all(parts, axes, 0, 0, tiled=True, axis_index_groups=groups)
    total = jnp.sum(came.astype(f32), axis=0)
    total = lax.ppermute(total, axes, turn(0)) * (1.0 / image_side)
    total = total.reshape(sub_dev, 2, samples)

    mine = lambda a: lax.dynamic_slice_in_dim(a, my_fft * sub_dev, sub_dev, 0)
    base_hot = (mine(sub_base[0])[:, None] == jnp.arange(gain_table.shape[1], dtype=jnp.int32)[None, :]).astype(f32)
    gains = jnp.dot(base_hot, gain_table.T, precision=highest)
    g0, g1 = gains[:, 0:1], gains[:, 1:2]
    re = total[:, 0]
    im = jnp.where(mine(mirrored)[:, None], -total[:, 1], total[:, 1])
    return jnp.stack([g0 * re - g1 * im, g0 * im + g1 * re], axis=1)[None]


def solution(mesh):
    return jax.shard_map(
        local,
        mesh=mesh,
        in_specs=(
            P("beam", "fft", None), P(), P("beam", None, None, None), P("beam"),
            P("beam", None, None), P("beam", None), P("beam", None),
            P("beam", None, None, None), P("beam", None), P(),
        ),
        out_specs=P("beam", "fft", None, None),
        check_vma=False,
    )
```

time: 173 us -> 297 us (1.72)
  Pallas kernels: 103 us -> 242 us
  other arithmetic: 18.6 us -> 3.54 us
  waiting for transfers between devices: 13.1 us -> 20.4 us
  local copies, waits for them, and re-layouts: 6.75 us -> 2.58 us
    pallas_call x2 -> x1, Pallas kernels: 103 us -> 242 us  [local(): pl.pallas_call(functools.partial(window_kernel, beams=beams, ffts=ffts, q...]
    ppermute x4, waiting for transfers between devices: 0.01 us -> 6.41 us  [local(): offs = [lax.ppermute(off_code, axes, turn(t)) for t in range(quads)]]
    convert_element_type x6 -> x1, other arithmetic: 4.62 us -> 0.7 us  [local(): code_mine.astype(f32)]
    add x5 -> x0, other arithmetic: 3.85 us -> none  [the longest x1 3.83 us: split_phase(): cr * fi + ci * fr]
  transfers between devices with their start and end apart: 11 -> 11, of which waited for: 2 -> 5; matrix products, arithmetic and copies ran while one was open for 10% -> 2% of each run, Pallas kernels for 50% -> 0%
where the time goes in v4:
time: 297 us
  Pallas kernels  242 us (81%)
  starting transfers between devices  27.2 us (9%)
  waiting for transfers between devices  20.4 us (7%)
  other arithmetic  3.54 us (1%)
    pallas_call x1, Pallas kernels, local(): pl.pallas_call(functools.partial(window_kernel, beams=beams, ffts=ffts, q...  242 us
    all_to_all x1, waiting for transfers between devices, local(): lax.all_to_all(parts, axes, 0, 0, tiled=True, axis_index_groups=groups)  12.1 us
    ppermute x4, starting transfers between devices, local(): lax.ppermute(small, axes, turn(t))  9.82 us
    ppermute x4, starting transfers between devices, local(): offs = [lax.ppermute(off_code, axes, turn(t)) for t in range(quads)]  7.66 us
    ppermute x4, waiting for transfers between devices, local(): offs = [lax.ppermute(off_code, axes, turn(t)) for t in range(quads)]  6.41 us
    ppermute x1, starting transfers between devices, local(): total = lax.ppermute(total, axes, turn(0)) * (1.0 / image_side)  6.04 us
  transfers between devices with their start and end apart: 11, of which 5 were waited for; matrix products, arithmetic and copies ran while one was open for 2% of the time, Pallas kernels for 0%

profile of v4, /device:TPU:1, one launch (start us, length us, event | category | flops | bytes accessed | tf_op | source)
XLA Modules:
  0.0 296.6 jit_solution(16923142003770015874)
XLA Ops:
  0.0 0.0 copy-start
  0.0 0.1 collective-permute-start.4
  0.7 0.7 sine_negate_fusion
  1.5 0.7 fusion.9
  2.2 0.9 constant_dynamic-slice_fusion.1
  3.1 4.5 %collective-permute-start = (f32[68,128]{1,0:T(8,128)S(1)}, f32[68,128]{1,0:T(8,128)S(1)}, u32[]{:S(2)}, u32[]{:S(2)}) collective-permute-start(f32[68,128]{1,0:T(8,128)S(1)} %concatenate.3), channel_id=1, source_target_pairs={{0,0},{1,4},{2,2},{3,6},{4,1},{5,5},{6,3},{7,7},{8,8},{9,12},{10,1... | collective-permute-start | bytes 104456 | tf_op jit(solution)/shard_map/ppermute | solution.py:269
  7.6 3.7 %collective-permute-start.1 = (f32[68,128]{1,0:T(8,128)S(1)}, f32[68,128]{1,0:T(8,128)S(1)}, u32[]{:S(2)}, u32[]{:S(2)}) collective-permute-start(f32[68,128]{1,0:T(8,128)S(1)} %concatenate.3), channel_id=1, source_target_pairs={{0,24},{1,28},{2,26},{3,30},{4,25},{5,29},{6,27},{7,31},{8,0},{9,4... | collective-permute-start | bytes 104456 | tf_op jit(solution)/shard_map/ppermute | solution.py:269
  11.3 0.0 collective-permute-start.2
  11.3 1.6 collective-permute-start.3
  12.9 1.3 add_convert_fusion
  14.2 0.1 sub.28
  14.3 0.0 collective-permute-done
  14.3 3.0 %collective-permute-start.5 = (s16[256,256]{1,0:T(8,128)(2,1)S(1)}, s16[256,256]{1,0:T(8,128)(2,1)S(1)}, u32[]{:S(2)}, u32[]{:S(2)}) collective-permute-start(s16[256,256]{1,0:T(8,128)(2,1)S(1)} %sub.28), channel_id=1, source_target_pairs={{0,0},{1,4},{2,2},{3,6},{4,1},{5,5},{6,3},{7,7},{8,8},{9,12},{10,1... | collective-permute-start | bytes 393224 | tf_op jit(solution)/shard_map/ppermute | solution.py:272
  17.3 0.0 collective-permute-done.1
  17.3 2.9 collective-permute-start.6
  20.2 0.0 collective-permute-done.2
  20.2 1.7 collective-permute-start.7
  22.0 0.0 collective-permute-done.3
  22.0 0.0 collective-permute-start.8
  22.0 0.0 copy-start.1
  22.0 0.6 fusion.11
  22.6 0.0 collective-permute-done.5.rest_0_
  22.6 0.0 copy-start.2
  22.6 1.3 collective-permute-done.6.rest_1_
  23.9 0.0 copy-start.3
  23.9 3.5 %collective-permute-done.7.rest_2_ = s16[256,256]{1,0:T(8,128)(2,1)S(1)} collective-permute-done((s16[256,256]{1,0:T(8,128)(2,1)S(1)}, s16[256,256]{1,0:T(8,128)(2,1)S(1)}, u32[]{:S(2)}, u32[]{:S(2)}) %collective-permute-start.7) | collective-permute-done | bytes 131104 | tf_op jit(solution)/shard_map/ppermute | solution.py:272
  27.4 0.0 copy-start.4
  27.4 1.6 collective-permute-done.8.rest_3_
  29.1 0.0 copy-start.5
  29.1 0.0 collective-permute-done.4.oth_ref
  29.1 0.0 copy-done.1
  29.1 0.0 copy-done.2
  29.1 0.0 copy-done.3
  29.1 0.0 copy-done.4
  29.1 0.6 copy-done.5
  29.7 0.0 copy-start.8
  29.7 0.0 copy-start.6
  29.7 0.0 copy-start.7
  29.7 241.9 %windows.1 = bf16[4,2,2,32,512]{4,3,2,1,0:T(8,128)(2,1)} custom-call(s32[8,64]{1,0:T(8,128)} %lists_ref.1, s32[4,128]{1,0:T(4,128)} %bitcast.49, s32[4,128]{1,0:T(4,128)} %bitcast.48, f32[4,128]{1,0:T(4,128)} %bitcast.47, f32[4,128]{1,0:T(4,128)} %bitcast.46, bf16[16,128,512]{2,1,0:T(8,128)(2,1)} %own_ref.1, ...), custom_call_target="tpu_custom_call" | custom-call | tf_op jit(solution)/shard_map/windows/pallas_call | solution.py:299
  271.6 3.6 %all-to-all-start = ((bf16[16,32,512]{2,1,0:T(8,128)(2,1)}), bf16[16,32,512]{2,1,0:T(8,128)(2,1)S(1)}, u32[]{:S(2)}, u32[]{:S(2)}) async-start(bf16[16,32,512]{2,1,0:T(8,128)(2,1)} %bitcast.39), calls=%async_computation | async-start | bytes 1048576 | tf_op jit(solution)/shard_map/all_to_all | solution.py:326
  275.2 0.0 copy-done.8
  275.2 0.1 fusion.2
  275.3 0.0 copy-done
  275.3 0.2 fusion
  275.4 12.1 %all-to-all-done = bf16[16,32,512]{2,1,0:T(8,128)(2,1)S(1)} async-done(((bf16[16,32,512]{2,1,0:T(8,128)(2,1)}), bf16[16,32,512]{2,1,0:T(8,128)(2,1)S(1)}, u32[]{:S(2)}, u32[]{:S(2)}) %all-to-all-start) | async-done | bytes 524320 | tf_op jit(solution)/shard_map/all_to_all | solution.py:326
  287.6 0.1 convert_reduce_fusion
  287.7 6.0 %collective-permute-start.9 = (f32[32,512]{1,0:T(8,128)S(1)}, f32[32,512]{1,0:T(8,128)S(1)}, u32[]{:S(2)}, u32[]{:S(2)}) collective-permute-start(f32[32,512]{1,0:T(8,128)S(1)} %convert_reduce_fusion), channel_id=1, source_target_pairs={{0,0},{1,4},{2,2},{3,6},{4,1},{5,5},{6,3},{7,7},{8,8},{9,12},{10,1... | collective-permute-start | bytes 196616 | tf_op jit(solution)/shard_map/ppermute | solution.py:328
  293.7 0.0 copy-done.6
  293.7 0.0 copy-done.7
  293.8 0.1 dynamic_slice.12
  293.8 1.8 collective-permute-done.9
  295.7 0.1 fusion.12
  295.8 0.1 multiply_subtract_fusion
  295.9 0.7 copy.20
  (8 shorter events, 0.2 us)
Async XLA Ops:
  0.0 275.3 %copy-start = (f32[2,630]{1,0:T(2,128)S(1)}, f32[2,630]{1,0:T(2,128)}, u32[]{:S(2)}) copy-start(f32[2,630]{1,0:T(2,128)} %param.25) | copy-start | bytes 15124
  0.0 29.1 %collective-permute-start.4 = (bf16[16,128,512]{2,1,0:T(8,128)(2,1)}, bf16[16,128,512]{2,1,0:T(8,128)(2,1)}, u32[]{:S(2)}, u32[]{:S(2)}) collective-permute-start(bf16[16,128,512]{2,1,0:T(8,128)(2,1)} %own_ref.1), channel_id=1, source_target_pairs={{0,1},{1,0},{2,3},{3,2},{4,5},{5,4},{6,7},{7,6},{8,9},{9,8},{10,11... | collective-permute-start | bytes 6291464 | tf_op jit(solution)/shard_map/ppermute | solution.py:255
  3.1 11.2 %collective-permute-start = (f32[68,128]{1,0:T(8,128)S(1)}, f32[68,128]{1,0:T(8,128)S(1)}, u32[]{:S(2)}, u32[]{:S(2)}) collective-permute-start(f32[68,128]{1,0:T(8,128)S(1)} %concatenate.3), channel_id=1, source_target_pairs={{0,0},{1,4},{2,2},{3,6},{4,1},{5,5},{6,3},{7,7},{8,8},{9,12},{10,1... | collective-permute-start | bytes 104456 | tf_op jit(solution)/shard_map/ppermute | solution.py:269
  7.6 9.7 %collective-permute-start.1 = (f32[68,128]{1,0:T(8,128)S(1)}, f32[68,128]{1,0:T(8,128)S(1)}, u32[]{:S(2)}, u32[]{:S(2)}) collective-permute-start(f32[68,128]{1,0:T(8,128)S(1)} %concatenate.3), channel_id=1, source_target_pairs={{0,24},{1,28},{2,26},{3,30},{4,25},{5,29},{6,27},{7,31},{8,0},{9,4... | collective-permute-start | bytes 104456 | tf_op jit(solution)/shard_map/ppermute | solution.py:269
  11.3 8.9 %collective-permute-start.2 = (f32[68,128]{1,0:T(8,128)S(1)}, f32[68,128]{1,0:T(8,128)S(1)}, u32[]{:S(2)}, u32[]{:S(2)}) collective-permute-start(f32[68,128]{1,0:T(8,128)S(1)} %concatenate.3), channel_id=1, source_target_pairs={{0,16},{1,20},{2,18},{3,22},{4,17},{5,21},{6,19},{7,23},{8,24},{9,... | collective-permute-start | bytes 104456 | tf_op jit(solution)/shard_map/ppermute | solution.py:269
  11.3 10.7 %collective-permute-start.3 = (f32[68,128]{1,0:T(8,128)S(1)}, f32[68,128]{1,0:T(8,128)S(1)}, u32[]{:S(2)}, u32[]{:S(2)}) collective-permute-start(f32[68,128]{1,0:T(8,128)S(1)} %concatenate.3), channel_id=1, source_target_pairs={{0,8},{1,12},{2,10},{3,14},{4,9},{5,13},{6,11},{7,15},{8,16},{9,20... | collective-permute-start | bytes 104456 | tf_op jit(solution)/shard_map/ppermute | solution.py:269
  14.3 8.4 %collective-permute-start.5 = (s16[256,256]{1,0:T(8,128)(2,1)S(1)}, s16[256,256]{1,0:T(8,128)(2,1)S(1)}, u32[]{:S(2)}, u32[]{:S(2)}) collective-permute-start(s16[256,256]{1,0:T(8,128)(2,1)S(1)} %sub.28), channel_id=1, source_target_pairs={{0,0},{1,4},{2,2},{3,6},{4,1},{5,5},{6,3},{7,7},{8,8},{9,12},{10,1... | collective-permute-start | bytes 393224 | tf_op jit(solution)/shard_map/ppermute | solution.py:272
  17.3 6.5 %collective-permute-start.6 = (s16[256,256]{1,0:T(8,128)(2,1)S(1)}, s16[256,256]{1,0:T(8,128)(2,1)S(1)}, u32[]{:S(2)}, u32[]{:S(2)}) collective-permute-start(s16[256,256]{1,0:T(8,128)(2,1)S(1)} %sub.28), channel_id=1, source_target_pairs={{0,24},{1,28},{2,26},{3,30},{4,25},{5,29},{6,27},{7,31},{8,0},{9,4... | collective-permute-start | bytes 393224 | tf_op jit(solution)/shard_map/ppermute | solution.py:272
  20.2 7.2 %collective-permute-start.7 = (s16[256,256]{1,0:T(8,128)(2,1)S(1)}, s16[256,256]{1,0:T(8,128)(2,1)S(1)}, u32[]{:S(2)}, u32[]{:S(2)}) collective-permute-start(s16[256,256]{1,0:T(8,128)(2,1)S(1)} %sub.28), channel_id=1, source_target_pairs={{0,16},{1,20},{2,18},{3,22},{4,17},{5,21},{6,19},{7,23},{8,24},{9,... | collective-permute-start | bytes 393224 | tf_op jit(solution)/shard_map/ppermute | solution.py:272
  22.0 7.1 %collective-permute-start.8 = (s16[256,256]{1,0:T(8,128)(2,1)S(1)}, s16[256,256]{1,0:T(8,128)(2,1)S(1)}, u32[]{:S(2)}, u32[]{:S(2)}) collective-permute-start(s16[256,256]{1,0:T(8,128)(2,1)S(1)} %sub.28), channel_id=1, source_target_pairs={{0,8},{1,12},{2,10},{3,14},{4,9},{5,13},{6,11},{7,15},{8,16},{9,20... | collective-permute-start | bytes 393224 | tf_op jit(solution)/shard_map/ppermute | solution.py:272
  22.0 7.1 %copy-start.1 = (f32[4,68,128]{2,1,0:T(8,128)}, f32[4,68,128]{2,1,0:T(8,128)S(1)}, u32[]{:S(2)}) copy-start(f32[4,68,128]{2,1,0:T(8,128)S(1)} %pad_maximum_fusion.prof_ref) | copy-start | bytes 417796
  22.6 6.4 %copy-start.2 = (s16[256,256]{1,0:T(8,128)(2,1)}, s16[256,256]{1,0:T(8,128)(2,1)S(1)}, u32[]{:S(2)}) copy-start(s16[256,256]{1,0:T(8,128)(2,1)S(1)} %collective-permute-done.5.rest_0_) | copy-start | bytes 393220
  23.9 5.2 %copy-start.3 = (s16[256,256]{1,0:T(8,128)(2,1)}, s16[256,256]{1,0:T(8,128)(2,1)S(1)}, u32[]{:S(2)}) copy-start(s16[256,256]{1,0:T(8,128)(2,1)S(1)} %collective-permute-done.6.rest_1_) | copy-start | bytes 393220
  27.4 1.7 copy-start.4
  29.1 0.7 copy-start.5
  29.7 245.5 %copy-start.8 = (s32[1,128]{1,0:T(1,128)S(1)}, s32[1,128]{1,0:T(1,128)}, u32[]{:S(2)}) copy-start(s32[1,128]{1,0:T(1,128)} %param.24) | copy-start | bytes 1540
  29.7 264.0 %copy-start.6 = (s32[1,128]{1,0:T(1,128)S(1)}, s32[1,128]{1,0:T(1,128)}, u32[]{:S(2)}) copy-start(s32[1,128]{1,0:T(1,128)} %param.22) | copy-start | bytes 1540
  29.7 264.0 %copy-start.7 = (s32[1,128,1]{1,2,0:T(1,128)S(1)}, s32[1,128,1]{1,2,0:T(1,128)}, u32[]{:S(2)}) copy-start(s32[1,128,1]{1,2,0:T(1,128)} %param.20) | copy-start | bytes 1540
  271.6 16.0 %all-to-all-start = ((bf16[16,32,512]{2,1,0:T(8,128)(2,1)}), bf16[16,32,512]{2,1,0:T(8,128)(2,1)S(1)}, u32[]{:S(2)}, u32[]{:S(2)}) async-start(bf16[16,32,512]{2,1,0:T(8,128)(2,1)} %bitcast.39), calls=%async_computation | async-start | bytes 1048576 | tf_op jit(solution)/shard_map/all_to_all | solution.py:326
  287.7 8.0 %collective-permute-start.9 = (f32[32,512]{1,0:T(8,128)S(1)}, f32[32,512]{1,0:T(8,128)S(1)}, u32[]{:S(2)}, u32[]{:S(2)}) collective-permute-start(f32[32,512]{1,0:T(8,128)S(1)} %convert_reduce_fusion), channel_id=1, source_target_pairs={{0,0},{1,4},{2,2},{3,6},{4,1},{5,5},{6,3},{7,7},{8,8},{9,12},{10,1... | collective-permute-start | bytes 196616 | tf_op jit(solution)/shard_map/ppermute | solution.py:328

commit v5 on v4

--- a/solution.py
+++ b/solution.py
@@ -96,7 +96,7 @@
 
         return found + hit.astype(jnp.int32)
 
-    found = lax.fori_loop(0, FT * FT, one_entry, 0, unroll=8)
+    found = lax.fori_loop(0, FT * FT, one_entry, 0, unroll=16)
 
     lane = lax.broadcasted_iota(jnp.int32, (16, LANES), 1)
     for part in range(2):
@@ -163,7 +163,7 @@
     factor = -math.log2(math.e) / kernel_width**2
     blank = jnp.zeros((LANES - 3 * SG, samples), bf16)
 
-    def one_sub(s):
+    def cut_out(s):
         r0 = r0_ref[q, s]
         code = c0_ref[q, s]
         mirrored = code >= 2 * FT * half_side
@@ -197,8 +197,10 @@
         half = half + pltpu.roll(half, 2 * SG, 1)
         half = half + pltpu.roll(half, SG, 1)
         low = half - half.astype(bf16).astype(f32)
-        cut = jnp.where(is_low, low, half).astype(bf16)
-
+        return jnp.where(is_low, low, half).astype(bf16)
+
+    def degrid(s, cut):
+        mirrored = c0_ref[q, s] >= 2 * FT * half_side
         base = jnp.where(mirrored, SG - 1.0, 0.0)
         way = jnp.where(mirrored, -1.0, 1.0)
         at = places * way + base
@@ -212,11 +214,12 @@
         inner = jnp.dot(cut, right, preferred_element_type=f32)
         re = jnp.sum(inner[:SG] * wu, axis=0, keepdims=True)
         im = jnp.sum(inner[SG:] * wu, axis=0, keepdims=True)
-        acc_ref[pl.ds(s, 1), :] = jnp.concatenate([re, im], axis=1)
+        return jnp.concatenate([re, im], axis=1)
 
     def some_subs(i, carry):
-        for u in range(unroll):
-            one_sub(i * unroll + u)
+        cuts = [cut_out(i * unroll + u) for u in range(unroll)]
+        rows = [degrid(i * unroll + u, cuts[u]) for u in range(unroll)]
+        acc_ref[pl.ds(pl.multiple_of(i * unroll, unroll), unroll), :] = jnp.concatenate(rows, axis=0)
         return carry
 
     subs = acc_ref.shape[0]
@@ -297,7 +300,7 @@
     fixed = [v_coarse, v_fine, u_coarse, u_fine, ea, eb, *offs]
     out_shape = (quads, 2, pairs, sub_dev, 2 * samples)
     partial = pl.pallas_call(
-        functools.partial(window_kernel, beams=beams, ffts=ffts, quads=quads, unroll=8),
+        functools.partial(window_kernel, beams=beams, ffts=ffts, quads=quads, unroll=16),
         out_shape=jax.ShapeDtypeStruct(out_shape, bf16),
         grid_spec=pltpu.PrefetchScalarGridSpec(
             num_scalar_prefetch=5, grid=(quads,),

time: 297 us -> 151 us (0.51)
  Pallas kernels: 242 us -> 95.4 us
    pallas_call x1, Pallas kernels: 242 us -> 95.4 us  [local(): pl.pallas_call(functools.partial(window_kernel, beams=beams, ffts=ffts, q...]
  transfers between devices with their start and end apart: 11 -> 11, of which waited for: 5 -> 5; matrix products, arithmetic and copies ran while one was open for 2% -> 3% of each run, Pallas kernels for 0% -> 0%
where the time goes in v5:
time: 151 us; the launch traced here: 150 us
  Pallas kernels  95.4 us (63%)
  starting transfers between devices  27.1 us (18%)
  waiting for transfers between devices  20.4 us (14%)
  other arithmetic  3.54 us (2%)
  local copies, waits for them, and re-layouts  2.58 us (2%)
    pallas_call x1, Pallas kernels, local(): pl.pallas_call(functools.partial(window_kernel, beams=beams, ffts=ffts, q...  95.4 us
    all_to_all x1, waiting for transfers between devices, local(): lax.all_to_all(parts, axes, 0, 0, tiled=True, axis_index_groups=groups)  12.2 us
    ppermute x4, starting transfers between devices, local(): lax.ppermute(small, axes, turn(t))  9.82 us
    ppermute x4, starting transfers between devices, local(): offs = [lax.ppermute(off_code, axes, turn(t)) for t in range(quads)]  7.66 us
    ppermute x4, waiting for transfers between devices, local(): offs = [lax.ppermute(off_code, axes, turn(t)) for t in range(quads)]  6.41 us
    ppermute x1, starting transfers between devices, local(): total = lax.ppermute(total, axes, turn(0)) * (1.0 / image_side)  5.98 us
    all_to_all x1, starting transfers between devices, local(): lax.all_to_all(parts, axes, 0, 0, tiled=True, axis_index_groups=groups)  3.57 us
  transfers between devices with their start and end apart: 11, of which 5 were waited for; matrix products, arithmetic and copies ran while one was open for 3% of the time, Pallas kernels for 0%

profile of v5, /device:TPU:1, one launch (start us, length us, event | category | flops | bytes accessed | tf_op | source)
XLA Modules:
  0.0 150.1 jit_solution(15532081698426925367)
XLA Ops:
  0.0 0.0 copy-start
  0.0 0.1 collective-permute-start.4
  0.7 0.7 sine_negate_fusion
  1.5 0.7 fusion.9
  2.2 0.9 constant_dynamic-slice_fusion.1
  3.1 4.5 %collective-permute-start = (f32[68,128]{1,0:T(8,128)S(1)}, f32[68,128]{1,0:T(8,128)S(1)}, u32[]{:S(2)}, u32[]{:S(2)}) collective-permute-start(f32[68,128]{1,0:T(8,128)S(1)} %concatenate.3), channel_id=1, source_target_pairs={{0,0},{1,4},{2,2},{3,6},{4,1},{5,5},{6,3},{7,7},{8,8},{9,12},{10,1... | collective-permute-start | bytes 104456 | tf_op jit(solution)/shard_map/ppermute | solution.py:272
  7.6 3.7 %collective-permute-start.1 = (f32[68,128]{1,0:T(8,128)S(1)}, f32[68,128]{1,0:T(8,128)S(1)}, u32[]{:S(2)}, u32[]{:S(2)}) collective-permute-start(f32[68,128]{1,0:T(8,128)S(1)} %concatenate.3), channel_id=1, source_target_pairs={{0,24},{1,28},{2,26},{3,30},{4,25},{5,29},{6,27},{7,31},{8,0},{9,4... | collective-permute-start | bytes 104456 | tf_op jit(solution)/shard_map/ppermute | solution.py:272
  11.3 0.0 collective-permute-start.2
  11.3 1.6 %collective-permute-start.3 = (f32[68,128]{1,0:T(8,128)S(1)}, f32[68,128]{1,0:T(8,128)S(1)}, u32[]{:S(2)}, u32[]{:S(2)}) collective-permute-start(f32[68,128]{1,0:T(8,128)S(1)} %concatenate.3), channel_id=1, source_target_pairs={{0,8},{1,12},{2,10},{3,14},{4,9},{5,13},{6,11},{7,15},{8,16},{9,20... | collective-permute-start | bytes 104456 | tf_op jit(solution)/shard_map/ppermute | solution.py:272
  12.9 1.3 add_convert_fusion
  14.2 0.1 sub.28
  14.3 0.0 collective-permute-done
  14.3 3.0 %collective-permute-start.5 = (s16[256,256]{1,0:T(8,128)(2,1)S(1)}, s16[256,256]{1,0:T(8,128)(2,1)S(1)}, u32[]{:S(2)}, u32[]{:S(2)}) collective-permute-start(s16[256,256]{1,0:T(8,128)(2,1)S(1)} %sub.28), channel_id=1, source_target_pairs={{0,0},{1,4},{2,2},{3,6},{4,1},{5,5},{6,3},{7,7},{8,8},{9,12},{10,1... | collective-permute-start | bytes 393224 | tf_op jit(solution)/shard_map/ppermute | solution.py:275
  17.3 0.0 collective-permute-done.1
  17.3 2.9 %collective-permute-start.6 = (s16[256,256]{1,0:T(8,128)(2,1)S(1)}, s16[256,256]{1,0:T(8,128)(2,1)S(1)}, u32[]{:S(2)}, u32[]{:S(2)}) collective-permute-start(s16[256,256]{1,0:T(8,128)(2,1)S(1)} %sub.28), channel_id=1, source_target_pairs={{0,24},{1,28},{2,26},{3,30},{4,25},{5,29},{6,27},{7,31},{8,0},{9,4... | collective-permute-start | bytes 393224 | tf_op jit(solution)/shard_map/ppermute | solution.py:275
  20.2 0.0 collective-permute-done.2
  20.2 1.7 %collective-permute-start.7 = (s16[256,256]{1,0:T(8,128)(2,1)S(1)}, s16[256,256]{1,0:T(8,128)(2,1)S(1)}, u32[]{:S(2)}, u32[]{:S(2)}) collective-permute-start(s16[256,256]{1,0:T(8,128)(2,1)S(1)} %sub.28), channel_id=1, source_target_pairs={{0,16},{1,20},{2,18},{3,22},{4,17},{5,21},{6,19},{7,23},{8,24},{9,... | collective-permute-start | bytes 393224 | tf_op jit(solution)/shard_map/ppermute | solution.py:275
  22.0 0.0 collective-permute-done.3
  22.0 0.0 collective-permute-start.8
  22.0 0.0 copy-start.1
  22.0 0.6 fusion.11
  22.6 0.0 collective-permute-done.5.rest_0_
  22.6 0.0 copy-start.2
  22.6 1.3 collective-permute-done.6.rest_1_
  23.9 0.0 copy-start.3
  23.9 3.5 %collective-permute-done.7.rest_2_ = s16[256,256]{1,0:T(8,128)(2,1)S(1)} collective-permute-done((s16[256,256]{1,0:T(8,128)(2,1)S(1)}, s16[256,256]{1,0:T(8,128)(2,1)S(1)}, u32[]{:S(2)}, u32[]{:S(2)}) %collective-permute-start.7) | collective-permute-done | bytes 131104 | tf_op jit(solution)/shard_map/ppermute | solution.py:275
  27.4 0.0 copy-start.4
  27.4 1.6 %collective-permute-done.8.rest_3_ = s16[256,256]{1,0:T(8,128)(2,1)S(1)} collective-permute-done((s16[256,256]{1,0:T(8,128)(2,1)S(1)}, s16[256,256]{1,0:T(8,128)(2,1)S(1)}, u32[]{:S(2)}, u32[]{:S(2)}) %collective-permute-start.8) | collective-permute-done | bytes 131104 | tf_op jit(solution)/shard_map/ppermute | solution.py:275
  29.1 0.0 copy-start.5
  29.1 0.0 collective-permute-done.4.oth_ref
  29.1 0.0 copy-done.1
  29.1 0.0 copy-done.2
  29.1 0.0 copy-done.3
  29.1 0.0 copy-done.4
  29.1 0.6 copy-done.5
  29.7 0.0 copy-start.8
  29.7 0.0 copy-start.6
  29.7 0.0 copy-start.7
  29.7 95.4 %windows.1 = bf16[4,2,2,32,512]{4,3,2,1,0:T(8,128)(2,1)} custom-call(s32[8,64]{1,0:T(8,128)} %lists_ref.1, s32[4,128]{1,0:T(4,128)} %bitcast.49, s32[4,128]{1,0:T(4,128)} %bitcast.48, f32[4,128]{1,0:T(4,128)} %bitcast.47, f32[4,128]{1,0:T(4,128)} %bitcast.46, bf16[16,128,512]{2,1,0:T(8,128)(2,1)} %own_ref.1, ...), custom_call_target="tpu_custom_call" | custom-call | tf_op jit(solution)/shard_map/windows/pallas_call | solution.py:302
  125.1 3.6 %all-to-all-start = ((bf16[16,32,512]{2,1,0:T(8,128)(2,1)}), bf16[16,32,512]{2,1,0:T(8,128)(2,1)S(1)}, u32[]{:S(2)}, u32[]{:S(2)}) async-start(bf16[16,32,512]{2,1,0:T(8,128)(2,1)} %bitcast.39), calls=%async_computation | async-start | bytes 1048576 | tf_op jit(solution)/shard_map/all_to_all | solution.py:329
  128.7 0.0 copy-done.8
  128.7 0.1 fusion.2
  128.8 0.0 copy-done
  128.8 0.2 fusion
  129.0 12.2 %all-to-all-done = bf16[16,32,512]{2,1,0:T(8,128)(2,1)S(1)} async-done(((bf16[16,32,512]{2,1,0:T(8,128)(2,1)}), bf16[16,32,512]{2,1,0:T(8,128)(2,1)S(1)}, u32[]{:S(2)}, u32[]{:S(2)}) %all-to-all-start) | async-done | bytes 524320 | tf_op jit(solution)/shard_map/all_to_all | solution.py:329
  141.2 0.1 convert_reduce_fusion
  141.3 6.0 %collective-permute-start.9 = (f32[32,512]{1,0:T(8,128)S(1)}, f32[32,512]{1,0:T(8,128)S(1)}, u32[]{:S(2)}, u32[]{:S(2)}) collective-permute-start(f32[32,512]{1,0:T(8,128)S(1)} %convert_reduce_fusion), channel_id=1, source_target_pairs={{0,0},{1,4},{2,2},{3,6},{4,1},{5,5},{6,3},{7,7},{8,8},{9,12},{10,1... | collective-permute-start | bytes 196616 | tf_op jit(solution)/shard_map/ppermute | solution.py:331
  147.3 0.0 copy-done.6
  147.3 0.0 copy-done.7
  147.3 0.1 dynamic_slice.12
  147.4 1.8 %collective-permute-done.9 = f32[32,512]{1,0:T(8,128)S(1)} collective-permute-done((f32[32,512]{1,0:T(8,128)S(1)}, f32[32,512]{1,0:T(8,128)S(1)}, u32[]{:S(2)}, u32[]{:S(2)}) %collective-permute-start.9) | collective-permute-done | bytes 65568 | tf_op jit(solution)/shard_map/ppermute | solution.py:331
  149.3 0.1 fusion.12
  149.3 0.1 multiply_subtract_fusion
  149.4 0.7 copy.20
  (8 shorter events, 0.2 us)
Async XLA Ops:
  0.0 128.8 %copy-start = (f32[2,630]{1,0:T(2,128)S(1)}, f32[2,630]{1,0:T(2,128)}, u32[]{:S(2)}) copy-start(f32[2,630]{1,0:T(2,128)} %param.25) | copy-start | bytes 15124
  0.0 29.1 %collective-permute-start.4 = (bf16[16,128,512]{2,1,0:T(8,128)(2,1)}, bf16[16,128,512]{2,1,0:T(8,128)(2,1)}, u32[]{:S(2)}, u32[]{:S(2)}) collective-permute-start(bf16[16,128,512]{2,1,0:T(8,128)(2,1)} %own_ref.1), channel_id=1, source_target_pairs={{0,1},{1,0},{2,3},{3,2},{4,5},{5,4},{6,7},{7,6},{8,9},{9,8},{10,11... | collective-permute-start | bytes 6291464 | tf_op jit(solution)/shard_map/ppermute | solution.py:258
  3.1 11.2 %collective-permute-start = (f32[68,128]{1,0:T(8,128)S(1)}, f32[68,128]{1,0:T(8,128)S(1)}, u32[]{:S(2)}, u32[]{:S(2)}) collective-permute-start(f32[68,128]{1,0:T(8,128)S(1)} %concatenate.3), channel_id=1, source_target_pairs={{0,0},{1,4},{2,2},{3,6},{4,1},{5,5},{6,3},{7,7},{8,8},{9,12},{10,1... | collective-permute-start | bytes 104456 | tf_op jit(solution)/shard_map/ppermute | solution.py:272
  7.6 9.7 %collective-permute-start.1 = (f32[68,128]{1,0:T(8,128)S(1)}, f32[68,128]{1,0:T(8,128)S(1)}, u32[]{:S(2)}, u32[]{:S(2)}) collective-permute-start(f32[68,128]{1,0:T(8,128)S(1)} %concatenate.3), channel_id=1, source_target_pairs={{0,24},{1,28},{2,26},{3,30},{4,25},{5,29},{6,27},{7,31},{8,0},{9,4... | collective-permute-start | bytes 104456 | tf_op jit(solution)/shard_map/ppermute | solution.py:272
  11.3 8.9 %collective-permute-start.2 = (f32[68,128]{1,0:T(8,128)S(1)}, f32[68,128]{1,0:T(8,128)S(1)}, u32[]{:S(2)}, u32[]{:S(2)}) collective-permute-start(f32[68,128]{1,0:T(8,128)S(1)} %concatenate.3), channel_id=1, source_target_pairs={{0,16},{1,20},{2,18},{3,22},{4,17},{5,21},{6,19},{7,23},{8,24},{9,... | collective-permute-start | bytes 104456 | tf_op jit(solution)/shard_map/ppermute | solution.py:272
  11.3 10.7 %collective-permute-start.3 = (f32[68,128]{1,0:T(8,128)S(1)}, f32[68,128]{1,0:T(8,128)S(1)}, u32[]{:S(2)}, u32[]{:S(2)}) collective-permute-start(f32[68,128]{1,0:T(8,128)S(1)} %concatenate.3), channel_id=1, source_target_pairs={{0,8},{1,12},{2,10},{3,14},{4,9},{5,13},{6,11},{7,15},{8,16},{9,20... | collective-permute-start | bytes 104456 | tf_op jit(solution)/shard_map/ppermute | solution.py:272
  14.3 8.4 %collective-permute-start.5 = (s16[256,256]{1,0:T(8,128)(2,1)S(1)}, s16[256,256]{1,0:T(8,128)(2,1)S(1)}, u32[]{:S(2)}, u32[]{:S(2)}) collective-permute-start(s16[256,256]{1,0:T(8,128)(2,1)S(1)} %sub.28), channel_id=1, source_target_pairs={{0,0},{1,4},{2,2},{3,6},{4,1},{5,5},{6,3},{7,7},{8,8},{9,12},{10,1... | collective-permute-start | bytes 393224 | tf_op jit(solution)/shard_map/ppermute | solution.py:275
  17.3 6.5 %collective-permute-start.6 = (s16[256,256]{1,0:T(8,128)(2,1)S(1)}, s16[256,256]{1,0:T(8,128)(2,1)S(1)}, u32[]{:S(2)}, u32[]{:S(2)}) collective-permute-start(s16[256,256]{1,0:T(8,128)(2,1)S(1)} %sub.28), channel_id=1, source_target_pairs={{0,24},{1,28},{2,26},{3,30},{4,25},{5,29},{6,27},{7,31},{8,0},{9,4... | collective-permute-start | bytes 393224 | tf_op jit(solution)/shard_map/ppermute | solution.py:275
  20.2 7.2 %collective-permute-start.7 = (s16[256,256]{1,0:T(8,128)(2,1)S(1)}, s16[256,256]{1,0:T(8,128)(2,1)S(1)}, u32[]{:S(2)}, u32[]{:S(2)}) collective-permute-start(s16[256,256]{1,0:T(8,128)(2,1)S(1)} %sub.28), channel_id=1, source_target_pairs={{0,16},{1,20},{2,18},{3,22},{4,17},{5,21},{6,19},{7,23},{8,24},{9,... | collective-permute-start | bytes 393224 | tf_op jit(solution)/shard_map/ppermute | solution.py:275
  22.0 7.1 %collective-permute-start.8 = (s16[256,256]{1,0:T(8,128)(2,1)S(1)}, s16[256,256]{1,0:T(8,128)(2,1)S(1)}, u32[]{:S(2)}, u32[]{:S(2)}) collective-permute-start(s16[256,256]{1,0:T(8,128)(2,1)S(1)} %sub.28), channel_id=1, source_target_pairs={{0,8},{1,12},{2,10},{3,14},{4,9},{5,13},{6,11},{7,15},{8,16},{9,20... | collective-permute-start | bytes 393224 | tf_op jit(solution)/shard_map/ppermute | solution.py:275
  22.0 7.1 %copy-start.1 = (f32[4,68,128]{2,1,0:T(8,128)}, f32[4,68,128]{2,1,0:T(8,128)S(1)}, u32[]{:S(2)}) copy-start(f32[4,68,128]{2,1,0:T(8,128)S(1)} %pad_maximum_fusion.prof_ref) | copy-start | bytes 417796
  22.6 6.4 %copy-start.2 = (s16[256,256]{1,0:T(8,128)(2,1)}, s16[256,256]{1,0:T(8,128)(2,1)S(1)}, u32[]{:S(2)}) copy-start(s16[256,256]{1,0:T(8,128)(2,1)S(1)} %collective-permute-done.5.rest_0_) | copy-start | bytes 393220
  23.9 5.2 %copy-start.3 = (s16[256,256]{1,0:T(8,128)(2,1)}, s16[256,256]{1,0:T(8,128)(2,1)S(1)}, u32[]{:S(2)}) copy-start(s16[256,256]{1,0:T(8,128)(2,1)S(1)} %collective-permute-done.6.rest_1_) | copy-start | bytes 393220
  27.4 1.7 %copy-start.4 = (s16[256,256]{1,0:T(8,128)(2,1)}, s16[256,256]{1,0:T(8,128)(2,1)S(1)}, u32[]{:S(2)}) copy-start(s16[256,256]{1,0:T(8,128)(2,1)S(1)} %collective-permute-done.7.rest_2_) | copy-start | bytes 393220
  29.1 0.7 copy-start.5
  29.7 99.0 %copy-start.8 = (s32[1,128]{1,0:T(1,128)S(1)}, s32[1,128]{1,0:T(1,128)}, u32[]{:S(2)}) copy-start(s32[1,128]{1,0:T(1,128)} %param.24) | copy-start | bytes 1540
  29.7 117.6 %copy-start.6 = (s32[1,128]{1,0:T(1,128)S(1)}, s32[1,128]{1,0:T(1,128)}, u32[]{:S(2)}) copy-start(s32[1,128]{1,0:T(1,128)} %param.22) | copy-start | bytes 1540
  29.7 117.6 %copy-start.7 = (s32[1,128,1]{1,2,0:T(1,128)S(1)}, s32[1,128,1]{1,2,0:T(1,128)}, u32[]{:S(2)}) copy-start(s32[1,128,1]{1,2,0:T(1,128)} %param.20) | copy-start | bytes 1540
  125.1 16.1 %all-to-all-start = ((bf16[16,32,512]{2,1,0:T(8,128)(2,1)}), bf16[16,32,512]{2,1,0:T(8,128)(2,1)S(1)}, u32[]{:S(2)}, u32[]{:S(2)}) async-start(bf16[16,32,512]{2,1,0:T(8,128)(2,1)} %bitcast.39), calls=%async_computation | async-start | bytes 1048576 | tf_op jit(solution)/shard_map/all_to_all | solution.py:329
  141.3 7.9 %collective-permute-start.9 = (f32[32,512]{1,0:T(8,128)S(1)}, f32[32,512]{1,0:T(8,128)S(1)}, u32[]{:S(2)}, u32[]{:S(2)}) collective-permute-start(f32[32,512]{1,0:T(8,128)S(1)} %convert_reduce_fusion), channel_id=1, source_target_pairs={{0,0},{1,4},{2,2},{3,6},{4,1},{5,5},{6,3},{7,7},{8,8},{9,12},{10,1... | collective-permute-start | bytes 196616 | tf_op jit(solution)/shard_map/ppermute | solution.py:331

commit v6 on v5

--- a/solution.py
+++ b/solution.py
@@ -14,6 +14,7 @@
 CAP = 8
 LANES = 128
 OFF_LEAST, OFF_MOST = 2.0, 29.0
+PROF_UNIT = 2.0**25
 OFF_STEP = (OFF_MOST - OFF_LEAST) / 65535.0
 
 kernel_width = 1.5
@@ -32,26 +33,27 @@
 
 
 def window_kernel(
-    lists_ref, r0_ref, c0_ref, wr_ref, wi_ref,
-    own_ref, oth_ref, prof_ref, v_coarse_ref, v_fine_ref, u_coarse_ref, u_fine_ref, ea_ref, eb_ref,
-    *rest, beams, ffts, quads, unroll,
+    tix_ref, ti_ref, tj_ref, valid_ref, r0_ref, c0_ref, wr_ref, wi_ref,
+    own_ref, oth_ref, v_coarse_ref, v_fine_ref, u_coarse_ref, u_fine_ref, ea_ref, eb_ref,
+    *rest, ffts, quads, unroll,
 ):
-    off_refs, rest = rest[:quads], rest[quads:]
-    (out_ref, rs_ref, low_ref, flip_ref, tcos_ref, tsin_ref, left_ref,
-     a_ref, b_ref, off_ref, acc_ref, slot_ref) = rest
+    small_refs, rest = rest[:quads], rest[quads:]
+    (out_ref, rs_ref, low_ref, flip_ref, prof_ref, off_ref, acc_ref,
+     tcos_ref, tsin_ref, left_ref, a_ref, b_ref) = rest
     q = pl.program_id(0)
     my_beam = lax.axis_index("beam")
     my_fft = lax.axis_index("fft")
     my_core = lax.rem(my_fft, 2)
     fft_ids = (my_fft, my_fft + 1 - 2 * my_core)
+    fine_v, fine_u = v_fine_ref.shape[1], u_fine_ref.shape[2]
     quad = lax.rem(my_beam // 2 + q, quads)
-    beam = 2 * quad + my_core
-    tiles_dev = own_ref.shape[0]
     half_side = own_ref.shape[2] // 2
     per_half = half_side // LANES
     per_tile = 2 * per_half
     first_v = FT * ffts
-    fine_v, fine_u = v_fine_ref.shape[1], u_fine_ref.shape[2]
+    subs = acc_ref.shape[0]
+    prof_rows = prof_ref.shape[0]
+    off_at = prof_rows + 4 * (subs // LANES)
 
     @pl.when(q == 0)
     def _():
@@ -79,25 +81,6 @@
 
         lax.fori_loop(0, v_coarse_ref.shape[1] // 3, some_rows, 0)
 
-    for k in range(CAP):
-        for n in range(3):
-            slot_ref[n, k] = 0
-
-    def one_entry(p, found):
-        tile = lists_ref[beam, p]
-        hit = (tile // tiles_dev) == my_beam
-
-        @pl.when(hit)
-        def _():
-            at = jnp.minimum(found, CAP - 1)
-            slot_ref[0, at] = lax.rem(tile, tiles_dev)
-            slot_ref[1, at] = p // FT
-            slot_ref[2, at] = lax.rem(p, FT)
-
-        return found + hit.astype(jnp.int32)
-
-    found = lax.fori_loop(0, FT * FT, one_entry, 0, unroll=16)
-
     lane = lax.broadcasted_iota(jnp.int32, (16, LANES), 1)
     for part in range(2):
         for half in range(2):
@@ -105,22 +88,26 @@
             for n in range(CAP // 2):
                 here = lane // SG == n
                 k = half * (CAP // 2) + n
-                a_rows = jnp.where(here, ea_ref[part, slot_ref[1, k]], a_rows)
-                b_rows = jnp.where(here[:8], eb_ref[part, slot_ref[2, k]], b_rows)
+                a_rows = jnp.where(here, ea_ref[part, ti_ref[q, k]], a_rows)
+                b_rows = jnp.where(here[:8], eb_ref[part, tj_ref[q, k]], b_rows)
             a_ref[part, half] = a_rows
             b_ref[part, half] = b_rows
 
     for t in range(quads):
         @pl.when(q == t)
         def _():
-            code = off_refs[t][...].astype(jnp.int32).astype(f32)
-            off_ref[...] = (code + 32768.0) * OFF_STEP + OFF_LEAST
+            prof_ref[...] = small_refs[t][:prof_rows].astype(f32) * (1.0 / PROF_UNIT)
+            for h in range(off_ref.shape[2] // LANES):
+                code = small_refs[t][off_at + h * subs:off_at + (h + 1) * subs]
+                pair = ((code & 65535).astype(f32), (code >> 16).astype(f32) + 32768.0)
+                for n in range(2):
+                    off_ref[n, :, h * LANES:(h + 1) * LANES] = pair[n] * OFF_STEP + OFF_LEAST
 
     def prof_row(at):
-        return prof_ref[0, pl.ds(at, 1), :]
+        return prof_ref[pl.ds(at, 1), :]
 
     low_prof = jnp.concatenate(
-        [prof_ref[0, pl.ds(first_v + p, FT, stride=per_tile), :] for p in range(per_half)], axis=1)
+        [prof_ref[pl.ds(first_v + p, FT, stride=per_tile), :] for p in range(per_half)], axis=1)
     low_ref[...] = jnp.dot(
         low_prof, flip_ref[...].astype(f32), precision=highest, preferred_element_type=f32)
 
@@ -128,8 +115,8 @@
         even, odd, row_scales = [], [], []
         for n in range(2):
             k = step * 2 + n
-            t, i, j = slot_ref[0, k], slot_ref[1, k], slot_ref[2, k]
-            valid = (k < found).astype(f32)
+            t, i, j = tix_ref[q, k], ti_ref[q, k], tj_ref[q, k]
+            valid = valid_ref[q, k].astype(f32)
             scale_hi = jnp.concatenate(
                 [prof_row(first_v + j * per_tile + p) for p in range(per_half, per_tile)], axis=1)
             scale_lo = low_ref[pl.ds(j, 1), :]
@@ -156,12 +143,11 @@
 
     lax.fori_loop(0, CAP // 2, some_tiles, 0)
 
-    samples = off_ref.shape[1]
+    samples = off_ref.shape[2]
     wide = lax.broadcasted_iota(jnp.int32, (2 * SG, LANES), 1)
     is_low = (wide // SG) == 1
     places = lax.broadcasted_iota(jnp.int32, (SG, samples), 0).astype(f32)
     factor = -math.log2(math.e) / kernel_width**2
-    blank = jnp.zeros((LANES - 3 * SG, samples), bf16)
 
     def cut_out(s):
         r0 = r0_ref[q, s]
@@ -204,14 +190,14 @@
         base = jnp.where(mirrored, SG - 1.0, 0.0)
         way = jnp.where(mirrored, -1.0, 1.0)
         at = places * way + base
-        tu = at - off_ref[pl.ds(2 * s, 1), :]
-        tv = at - off_ref[pl.ds(2 * s + 1, 1), :]
+        tu = at - off_ref[0, pl.ds(s, 1), :]
+        tv = at - off_ref[1, pl.ds(s, 1), :]
         wu = jnp.exp2(tu * tu * factor)
         wv = jnp.exp2(tv * tv * factor)
         wv_high = wv.astype(bf16)
         wv_low = (wv - wv_high.astype(f32)).astype(bf16)
-        right = jnp.concatenate([wv_high, wv_high, wv_low, blank], axis=0)
-        inner = jnp.dot(cut, right, preferred_element_type=f32)
+        right = jnp.concatenate([wv_high, wv_high, wv_low], axis=0)
+        inner = jnp.dot(cut[:, :3 * SG], right, preferred_element_type=f32)
         re = jnp.sum(inner[:SG] * wu, axis=0, keepdims=True)
         im = jnp.sum(inner[SG:] * wu, axis=0, keepdims=True)
         return jnp.concatenate([re, im], axis=1)
@@ -222,7 +208,6 @@
         acc_ref[pl.ds(pl.multiple_of(i * unroll, unroll), unroll), :] = jnp.concatenate(rows, axis=0)
         return carry
 
-    subs = acc_ref.shape[0]
     lax.fori_loop(0, subs // unroll, some_subs, 0)
     sub_dev = subs // ffts
     for f in range(ffts):
@@ -265,17 +250,35 @@
     middle = 2 * image_side
     angle = ((tile_side - 1) * c0_mine % middle).astype(f32) * (2.0 * math.pi / middle)
     code_mine = jnp.where(mirrored, c0_mine + image_side, c0_mine)
-    prof_u = jnp.pad(chosen[0].reshape(FT * ffts, tile_rows), ((0, 0), (0, LANES - tile_rows)))
-    per_sub = [r0_mine.astype(f32), code_mine.astype(f32), jnp.cos(angle), -jnp.sin(angle)]
+    unit = 2.0**30
+    per_sub = [r0_mine, code_mine] + [(x * unit).astype(jnp.int32) for x in (jnp.cos(angle), -jnp.sin(angle))]
+    prof_int = (chosen * PROF_UNIT).astype(jnp.int32)
+    prof_u = jnp.pad(prof_int[0].reshape(FT * ffts, tile_rows), ((0, 0), (0, LANES - tile_rows)))
+    off_code = jnp.round((offsets[0] - OFF_LEAST) * (1.0 / OFF_STEP)).astype(jnp.int32)
+    off_code = off_code[:, 0] + (off_code[:, 1] - 32768) * 65536
     small = jnp.concatenate(
-        [prof_u, chosen[1].reshape(-1, LANES)] + [x.reshape(-1, LANES) for x in per_sub])
-    smalls = jnp.stack([lax.ppermute(small, axes, turn(t)) for t in range(quads)])
-    off_code = jnp.round((offsets[0].reshape(2 * subs, samples) - OFF_LEAST) * (1.0 / OFF_STEP)) - 32768.0
-    off_code = off_code.astype(jnp.int16)
-    offs = [lax.ppermute(off_code, axes, turn(t)) for t in range(quads)]
-    sub_parts = smalls[:, FT * ffts + image_side // LANES:].reshape(quads, 4, subs)
-    r0_all, c0_all = sub_parts[:, 0].astype(jnp.int32), sub_parts[:, 1].astype(jnp.int32)
-    wr, wi = sub_parts[:, 2], sub_parts[:, 3]
+        [prof_u, prof_int[1].reshape(-1, LANES)] + [x.reshape(-1, LANES) for x in per_sub]
+        + [off_code[:, at:at + LANES] for at in range(0, samples, LANES)])
+    smalls = [lax.ppermute(small, axes, turn(t)) for t in range(quads)]
+    prof_rows = FT * ffts + image_side // LANES
+    sub_rows = subs // LANES
+    sub_parts = jnp.stack([x[prof_rows:prof_rows + 4 * sub_rows] for x in smalls]).reshape(quads, 4, subs)
+    r0_all, c0_all = sub_parts[:, 0], sub_parts[:, 1]
+    wr, wi = (sub_parts[:, n].astype(f32) * (1.0 / unit) for n in (2, 3))
+
+    my_beam = lax.axis_index("beam")
+    beam_ids = 2 * ((my_beam // 2 + jnp.arange(quads, dtype=jnp.int32)) % quads) + my_fft % 2
+    pick_beam = beam_ids[:, None, None] == jnp.arange(beams, dtype=jnp.int32)[None, :, None]
+    lists = jnp.sum(jnp.where(pick_beam, footprint[None], 0), axis=1)
+    hits = lists // tiles_dev == my_beam
+    entry = jnp.arange(FT * FT, dtype=jnp.int32)
+    earlier = entry[None, :] < entry[:, None]
+    order = jnp.sum(jnp.where(hits[:, None, :] & earlier[None], 1, 0), axis=2)
+    slots = hits[:, None, :] & (order[:, None, :] == jnp.arange(CAP, dtype=jnp.int32)[None, :, None])
+    in_slot = lambda values: jnp.sum(jnp.where(slots, values, 0), axis=2)
+    tix = in_slot((lists % tiles_dev)[:, None, :])
+    tile_i, tile_j = in_slot(entry // FT), in_slot(entry % FT)
+    valid = in_slot(1)
 
     side_half = tile_side // 2
     coarse, fine_v, fine_u = 129, image_side // 256, SG
@@ -296,33 +299,32 @@
         sky_model, oth_sky = jnp.pad(sky_model, pad_rows), jnp.pad(oth_sky, pad_rows)
 
     whole = lambda a: pl.BlockSpec(a.shape, lambda q, *_: (0,) * a.ndim, pipeline_mode=pl.Buffered(1))
-    per_beam = lambda a: pl.BlockSpec((1,) + a.shape[1:], lambda q, *_: (q,) + (0,) * (a.ndim - 1))
-    fixed = [v_coarse, v_fine, u_coarse, u_fine, ea, eb, *offs]
+    fixed = [sky_model, oth_sky, v_coarse, v_fine, u_coarse, u_fine, ea, eb, *smalls]
     out_shape = (quads, 2, pairs, sub_dev, 2 * samples)
     partial = pl.pallas_call(
-        functools.partial(window_kernel, beams=beams, ffts=ffts, quads=quads, unroll=16),
+        functools.partial(window_kernel, ffts=ffts, quads=quads, unroll=32),
         out_shape=jax.ShapeDtypeStruct(out_shape, bf16),
         grid_spec=pltpu.PrefetchScalarGridSpec(
-            num_scalar_prefetch=5, grid=(quads,),
-            in_specs=[whole(sky_model), whole(oth_sky), per_beam(smalls)] + [whole(x) for x in fixed],
+            num_scalar_prefetch=8, grid=(quads,),
+            in_specs=[whole(x) for x in fixed],
             out_specs=pl.BlockSpec(out_shape, lambda q, *_: (0,) * len(out_shape)),
             scratch_shapes=[
                 pltpu.VMEM((4, CAP, v_rows, LANES), f32),
                 pltpu.VMEM((FT, side_half), f32),
                 pltpu.VMEM((side_half, side_half), bf16),
+                pltpu.VMEM((prof_rows, LANES), f32),
+                pltpu.VMEM((2, subs, samples), f32),
+                pltpu.VMEM((subs, 2 * samples), f32),
                 pltpu.VMEM((v_rows, side_half), bf16),
                 pltpu.VMEM((v_rows, side_half), bf16),
                 pltpu.VMEM((4, u_rows, LANES), f32),
                 pltpu.VMEM((2, 2, 16, LANES), f32),
                 pltpu.VMEM((2, 2, 8, LANES), f32),
-                pltpu.VMEM((2 * subs, samples), f32),
-                pltpu.VMEM((subs, 2 * samples), f32),
-                pltpu.SMEM((3, CAP), jnp.int32),
             ],
         ),
         compiler_params=pltpu.CompilerParams(vmem_limit_bytes=63 << 20),
         name="windows",
-    )(footprint, r0_all, c0_all, wr, wi, sky_model, oth_sky, smalls, *fixed)
+    )(tix, tile_i, tile_j, valid, r0_all, c0_all, wr, wi, *fixed)
 
     groups = [[b * ffts + 2 * x + c for b in range(beams) for x in range(pairs)] for c in range(2)]
     parts = partial.reshape(beams * pairs, sub_dev, 2 * samples)

time: 151 us -> 142 us (0.940)
  Pallas kernels: 95.4 us -> 89.4 us
  waiting for transfers between devices: 20.4 us -> 17.5 us
  other arithmetic: 3.54 us -> 6.06 us
  starting transfers between devices: 27.1 us -> 24.8 us
    ppermute x8 -> x4, starting transfers between devices: 17.5 us -> 10.2 us  [local(): smalls = [lax.ppermute(small, axes, turn(t)) for t in range(quads)]]
    pallas_call x1, Pallas kernels: 95.4 us -> 89.4 us  [local(): pl.pallas_call(functools.partial(window_kernel, ffts=ffts, quads=quads, u...]
    all_to_all x1, starting transfers between devices: 3.57 us -> 7.13 us  [local(): lax.all_to_all(parts, axes, 0, 0, tiled=True, axis_index_groups=groups)]
    reduce_sum x0 -> x3, other arithmetic: none -> 1.88 us  [the longest x1 0.96 us: local(): in_slot = lambda values: jnp.sum(jnp.where(slots, values, 0), axis=2)]
    convert_element_type x1 -> x4, other arithmetic: 0.7 us -> 2.54 us  [the longest x1 0.99 us: local(): jnp.round((offsets[0] - OFF_LEAST) * (1.0 / OFF_STEP)).astype(jnp.int32)]
    ppermute x8 -> x4, waiting for transfers between devices: 6.42 us -> 4.76 us  [local(): smalls = [lax.ppermute(small, axes, turn(t)) for t in range(quads)]]
  transfers between devices with their start and end apart: 11 -> 7, of which waited for: 5 -> 4; matrix products, arithmetic and copies ran while one was open for 3% -> 3% of each run, Pallas kernels for 0% -> 0%
where the time goes in v6:
time: 142 us; the launch traced here: 141 us
  Pallas kernels  89.4 us (63%)
  starting transfers between devices  24.8 us (17%)
  waiting for transfers between devices  17.5 us (12%)
  other arithmetic  6.06 us (4%)
  local copies, waits for them, and re-layouts  2.24 us (2%)
    pallas_call x1, Pallas kernels, local(): pl.pallas_call(functools.partial(window_kernel, ffts=ffts, quads=quads, u...  89.4 us
    all_to_all x1, waiting for transfers between devices, local(): lax.all_to_all(parts, axes, 0, 0, tiled=True, axis_index_groups=groups)  10.9 us
    ppermute x4, starting transfers between devices, local(): smalls = [lax.ppermute(small, axes, turn(t)) for t in range(quads)]  10.2 us
    ppermute x1, starting transfers between devices, local(): total = lax.ppermute(total, axes, turn(0)) * (1.0 / image_side)  7.42 us
    all_to_all x1, starting transfers between devices, local(): lax.all_to_all(parts, axes, 0, 0, tiled=True, axis_index_groups=groups)  7.13 us
    ppermute x4, waiting for transfers between devices, local(): smalls = [lax.ppermute(small, axes, turn(t)) for t in range(quads)]  4.76 us
  transfers between devices with their start and end apart: 7, of which 4 were waited for; matrix products, arithmetic and copies ran while one was open for 3% of the time, Pallas kernels for 0%

profile of v6, /device:TPU:1, one launch (start us, length us, event | category | flops | bytes accessed | tf_op | source)
XLA Modules:
  0.0 141.0 jit_solution(2225222783805876577)
XLA Ops:
  0.0 0.0 copy-start
  0.7 0.8 multiply_convert_fusion
  1.5 1.0 fusion.3
  2.5 0.7 multiply_convert_fusion.1
  3.3 0.7 compare_select_fusion.6
  4.0 0.5 concatenate.3
  4.5 3.7 %collective-permute-start.3 = (s32[324,128]{1,0:T(8,128)S(1)}, s32[324,128]{1,0:T(8,128)S(1)}, u32[]{:S(2)}, u32[]{:S(2)}) collective-permute-start(s32[324,128]{1,0:T(8,128)S(1)} %concatenate.3), channel_id=1, source_target_pairs={{0,8},{1,12},{2,10},{3,14},{4,9},{5,13},{6,11},{7,15},{8,16},{9,20... | collective-permute-start | bytes 497672 | tf_op jit(solution)/shard_map/ppermute | solution.py:262
  8.2 2.0 %collective-permute-start.2 = (s32[324,128]{1,0:T(8,128)S(1)}, s32[324,128]{1,0:T(8,128)S(1)}, u32[]{:S(2)}, u32[]{:S(2)}) collective-permute-start(s32[324,128]{1,0:T(8,128)S(1)} %concatenate.3), channel_id=1, source_target_pairs={{0,16},{1,20},{2,18},{3,22},{4,17},{5,21},{6,19},{7,23},{8,24},{9,... | collective-permute-start | bytes 497672 | tf_op jit(solution)/shard_map/ppermute | solution.py:262
  10.2 2.6 %collective-permute-start.1 = (s32[324,128]{1,0:T(8,128)S(1)}, s32[324,128]{1,0:T(8,128)S(1)}, u32[]{:S(2)}, u32[]{:S(2)}) collective-permute-start(s32[324,128]{1,0:T(8,128)S(1)} %concatenate.3), channel_id=1, source_target_pairs={{0,24},{1,28},{2,26},{3,30},{4,25},{5,29},{6,27},{7,31},{8,0},{9,4... | collective-permute-start | bytes 497672 | tf_op jit(solution)/shard_map/ppermute | solution.py:262
  12.8 1.9 %collective-permute-start = (s32[324,128]{1,0:T(8,128)S(1)}, s32[324,128]{1,0:T(8,128)S(1)}, u32[]{:S(2)}, u32[]{:S(2)}) collective-permute-start(s32[324,128]{1,0:T(8,128)S(1)} %concatenate.3), channel_id=1, source_target_pairs={{0,0},{1,4},{2,2},{3,6},{4,1},{5,5},{6,3},{7,7},{8,8},{9,12},{10,1... | collective-permute-start | bytes 497672 | tf_op jit(solution)/shard_map/ppermute | solution.py:262
  14.7 0.1 collective-permute-start.4
  14.8 0.1 iota_compare_fusion.4
  14.9 0.8 select_reduce_fusion.5
  15.7 0.1 select_reduce_fusion
  15.9 1.0 select_reduce_fusion.1
  16.8 0.0 collective-permute-done.3.rest_3_
  16.8 0.0 copy-start.1
  16.8 4.7 %collective-permute-done.2.rest_2_ = s32[324,128]{1,0:T(8,128)S(1)} collective-permute-done((s32[324,128]{1,0:T(8,128)S(1)}, s32[324,128]{1,0:T(8,128)S(1)}, u32[]{:S(2)}, u32[]{:S(2)}) %collective-permute-start.2) | collective-permute-done | bytes 165920 | tf_op jit(solution)/shard_map/ppermute | solution.py:262
  21.5 0.0 copy-start.2
  21.5 0.0 collective-permute-done.1.rest_1_
  21.5 0.0 copy-start.3
  21.5 0.1 collective-permute-done.rest_0_
  21.6 0.0 copy-start.4
  21.6 0.7 fusion.26
  22.3 0.6 fusion.11
  23.0 0.0 collective-permute-done.4.oth_ref
  23.0 0.0 copy-done.1
  23.0 0.0 copy-done.2
  23.0 0.0 copy-done.3
  23.0 0.0 copy-done.4
  23.0 0.0 copy-start.7
  23.0 0.0 copy-start.5
  23.0 0.0 copy-start.6
  23.0 89.4 %windows.1 = bf16[4,2,2,32,512]{4,3,2,1,0:T(8,128)(2,1)} custom-call(s32[4,8]{1,0:T(4,128)} %get-tuple-element.8.tix_ref, s32[4,8]{1,0:T(4,128)} %get-tuple-element.7.ti_ref, s32[4,8]{1,0:T(4,128)} %get-tuple-element.6.tj_ref, s32[4,8]{1,0:T(4,128)} %get-tuple-element.5.valid_ref, s32[4,128]{1,0:T(4,128)} %bitcast.51, s32[4,128]{1,0:T(4,128)} %bitcast.50, ...), custom_call_target="tpu_custom_call" | custom-call | tf_op jit(solution)/shard_map/windows/pallas_call | solution.py:304
  112.4 7.1 %all-to-all-start = ((bf16[16,32,512]{2,1,0:T(8,128)(2,1)}), bf16[16,32,512]{2,1,0:T(8,128)(2,1)S(1)}, u32[]{:S(2)}, u32[]{:S(2)}) async-start(bf16[16,32,512]{2,1,0:T(8,128)(2,1)} %bitcast.47), calls=%async_computation | async-start | bytes 1048576 | tf_op jit(solution)/shard_map/all_to_all | solution.py:331
  119.5 0.0 copy-done.7
  119.5 0.1 dynamic-slice_bitcast_fusion
  119.6 0.0 copy-done
  119.6 0.2 fusion.7
  119.8 10.9 %all-to-all-done = bf16[16,32,512]{2,1,0:T(8,128)(2,1)S(1)} async-done(((bf16[16,32,512]{2,1,0:T(8,128)(2,1)}), bf16[16,32,512]{2,1,0:T(8,128)(2,1)S(1)}, u32[]{:S(2)}, u32[]{:S(2)}) %all-to-all-start) | async-done | bytes 524320 | tf_op jit(solution)/shard_map/all_to_all | solution.py:331
  130.7 0.1 convert_reduce_fusion
  130.8 7.4 %collective-permute-start.5 = (f32[32,512]{1,0:T(8,128)S(1)}, f32[32,512]{1,0:T(8,128)S(1)}, u32[]{:S(2)}, u32[]{:S(2)}) collective-permute-start(f32[32,512]{1,0:T(8,128)S(1)} %convert_reduce_fusion), channel_id=1, source_target_pairs={{0,0},{1,4},{2,2},{3,6},{4,1},{5,5},{6,3},{7,7},{8,8},{9,12},{10,1... | collective-permute-start | bytes 196616 | tf_op jit(solution)/shard_map/ppermute | solution.py:333
  138.2 0.0 copy-done.5
  138.2 0.0 copy-done.6
  138.2 0.1 dynamic_slice.12
  138.3 1.8 %collective-permute-done.5 = f32[32,512]{1,0:T(8,128)S(1)} collective-permute-done((f32[32,512]{1,0:T(8,128)S(1)}, f32[32,512]{1,0:T(8,128)S(1)}, u32[]{:S(2)}, u32[]{:S(2)}) %collective-permute-start.5) | collective-permute-done | bytes 65568 | tf_op jit(solution)/shard_map/ppermute | solution.py:333
  140.2 0.1 fusion.24
  140.2 0.1 multiply_subtract_fusion
  140.3 0.7 copy.24
  (19 shorter events, 0.2 us)
Async XLA Ops:
  0.0 119.6 %copy-start = (f32[2,630]{1,0:T(2,128)S(1)}, f32[2,630]{1,0:T(2,128)}, u32[]{:S(2)}) copy-start(f32[2,630]{1,0:T(2,128)} %param.25) | copy-start | bytes 15124
  4.5 12.3 %collective-permute-start.3 = (s32[324,128]{1,0:T(8,128)S(1)}, s32[324,128]{1,0:T(8,128)S(1)}, u32[]{:S(2)}, u32[]{:S(2)}) collective-permute-start(s32[324,128]{1,0:T(8,128)S(1)} %concatenate.3), channel_id=1, source_target_pairs={{0,8},{1,12},{2,10},{3,14},{4,9},{5,13},{6,11},{7,15},{8,16},{9,20... | collective-permute-start | bytes 497672 | tf_op jit(solution)/shard_map/ppermute | solution.py:262
  8.2 13.3 %collective-permute-start.2 = (s32[324,128]{1,0:T(8,128)S(1)}, s32[324,128]{1,0:T(8,128)S(1)}, u32[]{:S(2)}, u32[]{:S(2)}) collective-permute-start(s32[324,128]{1,0:T(8,128)S(1)} %concatenate.3), channel_id=1, source_target_pairs={{0,16},{1,20},{2,18},{3,22},{4,17},{5,21},{6,19},{7,23},{8,24},{9,... | collective-permute-start | bytes 497672 | tf_op jit(solution)/shard_map/ppermute | solution.py:262
  10.2 11.3 %collective-permute-start.1 = (s32[324,128]{1,0:T(8,128)S(1)}, s32[324,128]{1,0:T(8,128)S(1)}, u32[]{:S(2)}, u32[]{:S(2)}) collective-permute-start(s32[324,128]{1,0:T(8,128)S(1)} %concatenate.3), channel_id=1, source_target_pairs={{0,24},{1,28},{2,26},{3,30},{4,25},{5,29},{6,27},{7,31},{8,0},{9,4... | collective-permute-start | bytes 497672 | tf_op jit(solution)/shard_map/ppermute | solution.py:262
  12.8 8.8 %collective-permute-start = (s32[324,128]{1,0:T(8,128)S(1)}, s32[324,128]{1,0:T(8,128)S(1)}, u32[]{:S(2)}, u32[]{:S(2)}) collective-permute-start(s32[324,128]{1,0:T(8,128)S(1)} %concatenate.3), channel_id=1, source_target_pairs={{0,0},{1,4},{2,2},{3,6},{4,1},{5,5},{6,3},{7,7},{8,8},{9,12},{10,1... | collective-permute-start | bytes 497672 | tf_op jit(solution)/shard_map/ppermute | solution.py:262
  14.7 8.3 %collective-permute-start.4 = (bf16[16,128,512]{2,1,0:T(8,128)(2,1)}, bf16[16,128,512]{2,1,0:T(8,128)(2,1)}, u32[]{:S(2)}, u32[]{:S(2)}) collective-permute-start(bf16[16,128,512]{2,1,0:T(8,128)(2,1)} %own_ref.1), channel_id=1, source_target_pairs={{0,1},{1,0},{2,3},{3,2},{4,5},{5,4},{6,7},{7,6},{8,9},{9,8},{10,11... | collective-permute-start | bytes 6291464 | tf_op jit(solution)/shard_map/ppermute | solution.py:243
  16.8 6.1 %copy-start.1 = (s32[324,128]{1,0:T(8,128)}, s32[324,128]{1,0:T(8,128)S(1)}, u32[]{:S(2)}) copy-start(s32[324,128]{1,0:T(8,128)S(1)} %collective-permute-done.3.rest_3_) | copy-start | bytes 497668
  21.5 1.4 %copy-start.2 = (s32[324,128]{1,0:T(8,128)}, s32[324,128]{1,0:T(8,128)S(1)}, u32[]{:S(2)}) copy-start(s32[324,128]{1,0:T(8,128)S(1)} %collective-permute-done.2.rest_2_) | copy-start | bytes 497668
  21.5 1.4 %copy-start.3 = (s32[324,128]{1,0:T(8,128)}, s32[324,128]{1,0:T(8,128)S(1)}, u32[]{:S(2)}) copy-start(s32[324,128]{1,0:T(8,128)S(1)} %collective-permute-done.1.rest_1_) | copy-start | bytes 497668
  21.6 1.4 copy-start.4
  23.0 96.6 %copy-start.7 = (s32[1,128]{1,0:T(1,128)S(1)}, s32[1,128]{1,0:T(1,128)}, u32[]{:S(2)}) copy-start(s32[1,128]{1,0:T(1,128)} %param.24) | copy-start | bytes 1540
  23.0 115.2 %copy-start.5 = (s32[1,128]{1,0:T(1,128)S(1)}, s32[1,128]{1,0:T(1,128)}, u32[]{:S(2)}) copy-start(s32[1,128]{1,0:T(1,128)} %param.22) | copy-start | bytes 1540
  23.0 115.2 %copy-start.6 = (s32[1,128,1]{1,2,0:T(1,128)S(1)}, s32[1,128,1]{1,2,0:T(1,128)}, u32[]{:S(2)}) copy-start(s32[1,128,1]{1,2,0:T(1,128)} %param.20) | copy-start | bytes 1540
  112.4 18.3 %all-to-all-start = ((bf16[16,32,512]{2,1,0:T(8,128)(2,1)}), bf16[16,32,512]{2,1,0:T(8,128)(2,1)S(1)}, u32[]{:S(2)}, u32[]{:S(2)}) async-start(bf16[16,32,512]{2,1,0:T(8,128)(2,1)} %bitcast.47), calls=%async_computation | async-start | bytes 1048576 | tf_op jit(solution)/shard_map/all_to_all | solution.py:331
  130.8 9.4 %collective-permute-start.5 = (f32[32,512]{1,0:T(8,128)S(1)}, f32[32,512]{1,0:T(8,128)S(1)}, u32[]{:S(2)}, u32[]{:S(2)}) collective-permute-start(f32[32,512]{1,0:T(8,128)S(1)} %convert_reduce_fusion), channel_id=1, source_target_pairs={{0,0},{1,4},{2,2},{3,6},{4,1},{5,5},{6,3},{7,7},{8,8},{9,12},{10,1... | collective-permute-start | bytes 196616 | tf_op jit(solution)/shard_map/ppermute | solution.py:333

commit v7 on v6

--- a/solution.py
+++ b/solution.py
@@ -13,6 +13,7 @@
 SG = 32
 CAP = 8
 LANES = 128
+LAG = 12
 OFF_LEAST, OFF_MOST = 2.0, 29.0
 PROF_UNIT = 2.0**25
 OFF_STEP = (OFF_MOST - OFF_LEAST) / 65535.0
@@ -141,7 +142,8 @@
                     rs_ref[h * 2 + c, step * 2 + n] = got[:, at:at + LANES]
         return carry
 
-    lax.fori_loop(0, CAP // 2, some_tiles, 0)
+    for step in range(CAP // 2):
+        some_tiles(step, 0)
 
     samples = off_ref.shape[2]
     wide = lax.broadcasted_iota(jnp.int32, (2 * SG, LANES), 1)
@@ -203,8 +205,12 @@
         return jnp.concatenate([re, im], axis=1)
 
     def some_subs(i, carry):
-        cuts = [cut_out(i * unroll + u) for u in range(unroll)]
-        rows = [degrid(i * unroll + u, cuts[u]) for u in range(unroll)]
+        cuts, rows = [], []
+        for u in range(unroll + LAG):
+            if u < unroll:
+                cuts.append(cut_out(i * unroll + u))
+            if u >= LAG:
+                rows.append(degrid(i * unroll + u - LAG, cuts[u - LAG]))
         acc_ref[pl.ds(pl.multiple_of(i * unroll, unroll), unroll), :] = jnp.concatenate(rows, axis=0)
         return carry
 
@@ -302,7 +308,7 @@
     fixed = [sky_model, oth_sky, v_coarse, v_fine, u_coarse, u_fine, ea, eb, *smalls]
     out_shape = (quads, 2, pairs, sub_dev, 2 * samples)
     partial = pl.pallas_call(
-        functools.partial(window_kernel, ffts=ffts, quads=quads, unroll=32),
+        functools.partial(window_kernel, ffts=ffts, quads=quads, unroll=64),
         out_shape=jax.ShapeDtypeStruct(out_shape, bf16),
         grid_spec=pltpu.PrefetchScalarGridSpec(
             num_scalar_prefetch=8, grid=(quads,),

time: 142 us -> 131 us (0.923)
  Pallas kernels: 89.4 us -> 79.4 us
    pallas_call x1, Pallas kernels: 89.4 us -> 79.4 us  [local(): pl.pallas_call(functools.partial(window_kernel, ffts=ffts, quads=quads, u...]
where the time goes in v7:
time: 131 us
  Pallas kernels  79.4 us (61%)
  starting transfers between devices  24.7 us (19%)
  waiting for transfers between devices  17.5 us (13%)
  other arithmetic  6.06 us (5%)
  local copies, waits for them, and re-layouts  2.24 us (2%)
    pallas_call x1, Pallas kernels, local(): pl.pallas_call(functools.partial(window_kernel, ffts=ffts, quads=quads, u...  79.4 us
    all_to_all x1, waiting for transfers between devices, local(): lax.all_to_all(parts, axes, 0, 0, tiled=True, axis_index_groups=groups)  10.9 us
    ppermute x4, starting transfers between devices, local(): smalls = [lax.ppermute(small, axes, turn(t)) for t in range(quads)]  10.2 us
    ppermute x1, starting transfers between devices, local(): total = lax.ppermute(total, axes, turn(0)) * (1.0 / image_side)  7.37 us
    all_to_all x1, starting transfers between devices, local(): lax.all_to_all(parts, axes, 0, 0, tiled=True, axis_index_groups=groups)  7.13 us
    ppermute x4, waiting for transfers between devices, local(): smalls = [lax.ppermute(small, axes, turn(t)) for t in range(quads)]  4.76 us
  transfers between devices with their start and end apart: 7, of which 4 were waited for; matrix products, arithmetic and copies ran while one was open for 3% of the time, Pallas kernels for 0%

profile of v7, /device:TPU:1, one launch (start us, length us, event | category | flops | bytes accessed | tf_op | source)
XLA Modules:
  0.0 131.1 jit_solution(15740612166375510995)
XLA Ops:
  0.0 0.0 copy-start
  0.7 0.8 multiply_convert_fusion
  1.5 1.0 fusion.3
  2.5 0.7 multiply_convert_fusion.1
  3.3 0.7 compare_select_fusion.6
  4.0 0.5 concatenate.3
  4.5 3.7 %collective-permute-start.3 = (s32[324,128]{1,0:T(8,128)S(1)}, s32[324,128]{1,0:T(8,128)S(1)}, u32[]{:S(2)}, u32[]{:S(2)}) collective-permute-start(s32[324,128]{1,0:T(8,128)S(1)} %concatenate.3), channel_id=1, source_target_pairs={{0,8},{1,12},{2,10},{3,14},{4,9},{5,13},{6,11},{7,15},{8,16},{9,20... | collective-permute-start | bytes 497672 | tf_op jit(solution)/shard_map/ppermute | solution.py:268
  8.2 2.0 %collective-permute-start.2 = (s32[324,128]{1,0:T(8,128)S(1)}, s32[324,128]{1,0:T(8,128)S(1)}, u32[]{:S(2)}, u32[]{:S(2)}) collective-permute-start(s32[324,128]{1,0:T(8,128)S(1)} %concatenate.3), channel_id=1, source_target_pairs={{0,16},{1,20},{2,18},{3,22},{4,17},{5,21},{6,19},{7,23},{8,24},{9,... | collective-permute-start | bytes 497672 | tf_op jit(solution)/shard_map/ppermute | solution.py:268
  10.2 2.6 %collective-permute-start.1 = (s32[324,128]{1,0:T(8,128)S(1)}, s32[324,128]{1,0:T(8,128)S(1)}, u32[]{:S(2)}, u32[]{:S(2)}) collective-permute-start(s32[324,128]{1,0:T(8,128)S(1)} %concatenate.3), channel_id=1, source_target_pairs={{0,24},{1,28},{2,26},{3,30},{4,25},{5,29},{6,27},{7,31},{8,0},{9,4... | collective-permute-start | bytes 497672 | tf_op jit(solution)/shard_map/ppermute | solution.py:268
  12.8 1.9 %collective-permute-start = (s32[324,128]{1,0:T(8,128)S(1)}, s32[324,128]{1,0:T(8,128)S(1)}, u32[]{:S(2)}, u32[]{:S(2)}) collective-permute-start(s32[324,128]{1,0:T(8,128)S(1)} %concatenate.3), channel_id=1, source_target_pairs={{0,0},{1,4},{2,2},{3,6},{4,1},{5,5},{6,3},{7,7},{8,8},{9,12},{10,1... | collective-permute-start | bytes 497672 | tf_op jit(solution)/shard_map/ppermute | solution.py:268
  14.7 0.1 collective-permute-start.4
  14.8 0.1 iota_compare_fusion.4
  14.9 0.8 select_reduce_fusion.5
  15.7 0.1 select_reduce_fusion
  15.9 1.0 select_reduce_fusion.1
  16.8 0.0 collective-permute-done.3.rest_3_
  16.8 0.0 copy-start.1
  16.8 4.7 %collective-permute-done.2.rest_2_ = s32[324,128]{1,0:T(8,128)S(1)} collective-permute-done((s32[324,128]{1,0:T(8,128)S(1)}, s32[324,128]{1,0:T(8,128)S(1)}, u32[]{:S(2)}, u32[]{:S(2)}) %collective-permute-start.2) | collective-permute-done | bytes 165920 | tf_op jit(solution)/shard_map/ppermute | solution.py:268
  21.5 0.0 copy-start.2
  21.5 0.0 collective-permute-done.1.rest_1_
  21.5 0.0 copy-start.3
  21.5 0.1 collective-permute-done.rest_0_
  21.6 0.0 copy-start.4
  21.6 0.7 fusion.26
  22.3 0.6 fusion.11
  23.0 0.0 collective-permute-done.4.oth_ref
  23.0 0.0 copy-done.1
  23.0 0.0 copy-done.2
  23.0 0.0 copy-done.3
  23.0 0.0 copy-done.4
  23.0 0.0 copy-start.7
  23.0 0.0 copy-start.5
  23.0 0.0 copy-start.6
  23.0 79.4 %windows.1 = bf16[4,2,2,32,512]{4,3,2,1,0:T(8,128)(2,1)} custom-call(s32[4,8]{1,0:T(4,128)} %get-tuple-element.8.tix_ref, s32[4,8]{1,0:T(4,128)} %get-tuple-element.7.ti_ref, s32[4,8]{1,0:T(4,128)} %get-tuple-element.6.tj_ref, s32[4,8]{1,0:T(4,128)} %get-tuple-element.5.valid_ref, s32[4,128]{1,0:T(4,128)} %bitcast.51, s32[4,128]{1,0:T(4,128)} %bitcast.50, ...), custom_call_target="tpu_custom_call" | custom-call | tf_op jit(solution)/shard_map/windows/pallas_call | solution.py:310
  102.4 7.1 %all-to-all-start = ((bf16[16,32,512]{2,1,0:T(8,128)(2,1)}), bf16[16,32,512]{2,1,0:T(8,128)(2,1)S(1)}, u32[]{:S(2)}, u32[]{:S(2)}) async-start(bf16[16,32,512]{2,1,0:T(8,128)(2,1)} %bitcast.47), calls=%async_computation | async-start | bytes 1048576 | tf_op jit(solution)/shard_map/all_to_all | solution.py:337
  109.6 0.0 copy-done.7
  109.6 0.1 dynamic-slice_bitcast_fusion
  109.6 0.0 copy-done
  109.6 0.2 fusion.7
  109.8 10.9 %all-to-all-done = bf16[16,32,512]{2,1,0:T(8,128)(2,1)S(1)} async-done(((bf16[16,32,512]{2,1,0:T(8,128)(2,1)}), bf16[16,32,512]{2,1,0:T(8,128)(2,1)S(1)}, u32[]{:S(2)}, u32[]{:S(2)}) %all-to-all-start) | async-done | bytes 524320 | tf_op jit(solution)/shard_map/all_to_all | solution.py:337
  120.8 0.1 convert_reduce_fusion
  120.8 7.4 %collective-permute-start.5 = (f32[32,512]{1,0:T(8,128)S(1)}, f32[32,512]{1,0:T(8,128)S(1)}, u32[]{:S(2)}, u32[]{:S(2)}) collective-permute-start(f32[32,512]{1,0:T(8,128)S(1)} %convert_reduce_fusion), channel_id=1, source_target_pairs={{0,0},{1,4},{2,2},{3,6},{4,1},{5,5},{6,3},{7,7},{8,8},{9,12},{10,1... | collective-permute-start | bytes 196616 | tf_op jit(solution)/shard_map/ppermute | solution.py:339
  128.2 0.0 copy-done.5
  128.2 0.0 copy-done.6
  128.2 0.1 dynamic_slice.12
  128.3 1.8 %collective-permute-done.5 = f32[32,512]{1,0:T(8,128)S(1)} collective-permute-done((f32[32,512]{1,0:T(8,128)S(1)}, f32[32,512]{1,0:T(8,128)S(1)}, u32[]{:S(2)}, u32[]{:S(2)}) %collective-permute-start.5) | collective-permute-done | bytes 65568 | tf_op jit(solution)/shard_map/ppermute | solution.py:339
  130.2 0.1 fusion.24
  130.3 0.1 multiply_subtract_fusion
  130.4 0.7 copy.24
  (19 shorter events, 0.2 us)
Async XLA Ops:
  0.0 109.6 %copy-start = (f32[2,630]{1,0:T(2,128)S(1)}, f32[2,630]{1,0:T(2,128)}, u32[]{:S(2)}) copy-start(f32[2,630]{1,0:T(2,128)} %param.25) | copy-start | bytes 15124
  4.5 12.3 %collective-permute-start.3 = (s32[324,128]{1,0:T(8,128)S(1)}, s32[324,128]{1,0:T(8,128)S(1)}, u32[]{:S(2)}, u32[]{:S(2)}) collective-permute-start(s32[324,128]{1,0:T(8,128)S(1)} %concatenate.3), channel_id=1, source_target_pairs={{0,8},{1,12},{2,10},{3,14},{4,9},{5,13},{6,11},{7,15},{8,16},{9,20... | collective-permute-start | bytes 497672 | tf_op jit(solution)/shard_map/ppermute | solution.py:268
  8.2 13.3 %collective-permute-start.2 = (s32[324,128]{1,0:T(8,128)S(1)}, s32[324,128]{1,0:T(8,128)S(1)}, u32[]{:S(2)}, u32[]{:S(2)}) collective-permute-start(s32[324,128]{1,0:T(8,128)S(1)} %concatenate.3), channel_id=1, source_target_pairs={{0,16},{1,20},{2,18},{3,22},{4,17},{5,21},{6,19},{7,23},{8,24},{9,... | collective-permute-start | bytes 497672 | tf_op jit(solution)/shard_map/ppermute | solution.py:268
  10.2 11.3 %collective-permute-start.1 = (s32[324,128]{1,0:T(8,128)S(1)}, s32[324,128]{1,0:T(8,128)S(1)}, u32[]{:S(2)}, u32[]{:S(2)}) collective-permute-start(s32[324,128]{1,0:T(8,128)S(1)} %concatenate.3), channel_id=1, source_target_pairs={{0,24},{1,28},{2,26},{3,30},{4,25},{5,29},{6,27},{7,31},{8,0},{9,4... | collective-permute-start | bytes 497672 | tf_op jit(solution)/shard_map/ppermute | solution.py:268
  12.8 8.8 %collective-permute-start = (s32[324,128]{1,0:T(8,128)S(1)}, s32[324,128]{1,0:T(8,128)S(1)}, u32[]{:S(2)}, u32[]{:S(2)}) collective-permute-start(s32[324,128]{1,0:T(8,128)S(1)} %concatenate.3), channel_id=1, source_target_pairs={{0,0},{1,4},{2,2},{3,6},{4,1},{5,5},{6,3},{7,7},{8,8},{9,12},{10,1... | collective-permute-start | bytes 497672 | tf_op jit(solution)/shard_map/ppermute | solution.py:268
  14.7 8.3 %collective-permute-start.4 = (bf16[16,128,512]{2,1,0:T(8,128)(2,1)}, bf16[16,128,512]{2,1,0:T(8,128)(2,1)}, u32[]{:S(2)}, u32[]{:S(2)}) collective-permute-start(bf16[16,128,512]{2,1,0:T(8,128)(2,1)} %own_ref.1), channel_id=1, source_target_pairs={{0,1},{1,0},{2,3},{3,2},{4,5},{5,4},{6,7},{7,6},{8,9},{9,8},{10,11... | collective-permute-start | bytes 6291464 | tf_op jit(solution)/shard_map/ppermute | solution.py:249
  16.8 6.1 %copy-start.1 = (s32[324,128]{1,0:T(8,128)}, s32[324,128]{1,0:T(8,128)S(1)}, u32[]{:S(2)}) copy-start(s32[324,128]{1,0:T(8,128)S(1)} %collective-permute-done.3.rest_3_) | copy-start | bytes 497668
  21.5 1.4 %copy-start.2 = (s32[324,128]{1,0:T(8,128)}, s32[324,128]{1,0:T(8,128)S(1)}, u32[]{:S(2)}) copy-start(s32[324,128]{1,0:T(8,128)S(1)} %collective-permute-done.2.rest_2_) | copy-start | bytes 497668
  21.5 1.4 %copy-start.3 = (s32[324,128]{1,0:T(8,128)}, s32[324,128]{1,0:T(8,128)S(1)}, u32[]{:S(2)}) copy-start(s32[324,128]{1,0:T(8,128)S(1)} %collective-permute-done.1.rest_1_) | copy-start | bytes 497668
  21.6 1.4 %copy-start.4 = (s32[324,128]{1,0:T(8,128)}, s32[324,128]{1,0:T(8,128)S(1)}, u32[]{:S(2)}) copy-start(s32[324,128]{1,0:T(8,128)S(1)} %collective-permute-done.rest_0_) | copy-start | bytes 497668
  23.0 86.6 %copy-start.7 = (s32[1,128]{1,0:T(1,128)S(1)}, s32[1,128]{1,0:T(1,128)}, u32[]{:S(2)}) copy-start(s32[1,128]{1,0:T(1,128)} %param.24) | copy-start | bytes 1540
  23.0 105.2 %copy-start.5 = (s32[1,128]{1,0:T(1,128)S(1)}, s32[1,128]{1,0:T(1,128)}, u32[]{:S(2)}) copy-start(s32[1,128]{1,0:T(1,128)} %param.22) | copy-start | bytes 1540
  23.0 105.2 %copy-start.6 = (s32[1,128,1]{1,2,0:T(1,128)S(1)}, s32[1,128,1]{1,2,0:T(1,128)}, u32[]{:S(2)}) copy-start(s32[1,128,1]{1,2,0:T(1,128)} %param.20) | copy-start | bytes 1540
  102.4 18.3 %all-to-all-start = ((bf16[16,32,512]{2,1,0:T(8,128)(2,1)}), bf16[16,32,512]{2,1,0:T(8,128)(2,1)S(1)}, u32[]{:S(2)}, u32[]{:S(2)}) async-start(bf16[16,32,512]{2,1,0:T(8,128)(2,1)} %bitcast.47), calls=%async_computation | async-start | bytes 1048576 | tf_op jit(solution)/shard_map/all_to_all | solution.py:337
  120.8 9.3 %collective-permute-start.5 = (f32[32,512]{1,0:T(8,128)S(1)}, f32[32,512]{1,0:T(8,128)S(1)}, u32[]{:S(2)}, u32[]{:S(2)}) collective-permute-start(f32[32,512]{1,0:T(8,128)S(1)} %convert_reduce_fusion), channel_id=1, source_target_pairs={{0,0},{1,4},{2,2},{3,6},{4,1},{5,5},{6,3},{7,7},{8,8},{9,12},{10,1... | collective-permute-start | bytes 196616 | tf_op jit(solution)/shard_map/ppermute | solution.py:339

commit v8 on v7

--- a/solution.py
+++ b/solution.py
@@ -14,7 +14,9 @@
 CAP = 8
 LANES = 128
 LAG = 12
+TOGETHER = 4
 OFF_LEAST, OFF_MOST = 2.0, 29.0
+TURN_UNIT = 2.0**30
 PROF_UNIT = 2.0**25
 OFF_STEP = (OFF_MOST - OFF_LEAST) / 65535.0
 
@@ -34,7 +36,7 @@
 
 
 def window_kernel(
-    tix_ref, ti_ref, tj_ref, valid_ref, r0_ref, c0_ref, wr_ref, wi_ref,
+    tix_ref, ti_ref, tj_ref, valid_ref, sub_ref,
     own_ref, oth_ref, v_coarse_ref, v_fine_ref, u_coarse_ref, u_fine_ref, ea_ref, eb_ref,
     *rest, ffts, quads, unroll,
 ):
@@ -114,8 +116,8 @@
 
     def some_tiles(step, carry):
         even, odd, row_scales = [], [], []
-        for n in range(2):
-            k = step * 2 + n
+        for n in range(TOGETHER):
+            k = step * TOGETHER + n
             t, i, j = tix_ref[q, k], ti_ref[q, k], tj_ref[q, k]
             valid = valid_ref[q, k].astype(f32)
             scale_hi = jnp.concatenate(
@@ -136,13 +138,13 @@
                 table[...], jnp.concatenate(parts, axis=0), (((1,), (1,)), ((), ())),
                 preferred_element_type=f32,
             ) * row_scale
-            for n in range(2):
+            for n in range(TOGETHER):
                 for h in range(2):
                     at = (2 * n + h) * LANES
-                    rs_ref[h * 2 + c, step * 2 + n] = got[:, at:at + LANES]
+                    rs_ref[h * 2 + c, step * TOGETHER + n] = got[:, at:at + LANES]
         return carry
 
-    for step in range(CAP // 2):
+    for step in range(CAP // TOGETHER):
         some_tiles(step, 0)
 
     samples = off_ref.shape[2]
@@ -152,8 +154,8 @@
     factor = -math.log2(math.e) / kernel_width**2
 
     def cut_out(s):
-        r0 = r0_ref[q, s]
-        code = c0_ref[q, s]
+        r0 = sub_ref[q, 0, s]
+        code = sub_ref[q, 1, s]
         mirrored = code >= 2 * FT * half_side
         c0 = jnp.where(mirrored, code - 2 * FT * half_side, code)
         windows = jnp.concatenate([
@@ -173,7 +175,7 @@
         br, bi = (
             jnp.concatenate([b_ref[part, half, pl.ds(c8, 1), :] for half in range(2)], axis=1)
             for part in range(2))
-        br, bi = turn_by(br, bi, wr_ref[q, s], wi_ref[q, s])
+        br, bi = turn_by(br, bi, sub_ref[q, 2, s].astype(f32) * (1.0 / TURN_UNIT), sub_ref[q, 3, s].astype(f32) * (1.0 / TURN_UNIT))
         fr, fi = turn_by(ar, ai, br, bi)
         re_parts, im_parts = [], []
         for a in range(SG // 8):
@@ -188,7 +190,7 @@
         return jnp.where(is_low, low, half).astype(bf16)
 
     def degrid(s, cut):
-        mirrored = c0_ref[q, s] >= 2 * FT * half_side
+        mirrored = sub_ref[q, 1, s] >= 2 * FT * half_side
         base = jnp.where(mirrored, SG - 1.0, 0.0)
         way = jnp.where(mirrored, -1.0, 1.0)
         at = places * way + base
@@ -256,8 +258,7 @@
     middle = 2 * image_side
     angle = ((tile_side - 1) * c0_mine % middle).astype(f32) * (2.0 * math.pi / middle)
     code_mine = jnp.where(mirrored, c0_mine + image_side, c0_mine)
-    unit = 2.0**30
-    per_sub = [r0_mine, code_mine] + [(x * unit).astype(jnp.int32) for x in (jnp.cos(angle), -jnp.sin(angle))]
+    per_sub = [r0_mine, code_mine] + [(x * TURN_UNIT).astype(jnp.int32) for x in (jnp.cos(angle), -jnp.sin(angle))]
     prof_int = (chosen * PROF_UNIT).astype(jnp.int32)
     prof_u = jnp.pad(prof_int[0].reshape(FT * ffts, tile_rows), ((0, 0), (0, LANES - tile_rows)))
     off_code = jnp.round((offsets[0] - OFF_LEAST) * (1.0 / OFF_STEP)).astype(jnp.int32)
@@ -269,8 +270,6 @@
     prof_rows = FT * ffts + image_side // LANES
     sub_rows = subs // LANES
     sub_parts = jnp.stack([x[prof_rows:prof_rows + 4 * sub_rows] for x in smalls]).reshape(quads, 4, subs)
-    r0_all, c0_all = sub_parts[:, 0], sub_parts[:, 1]
-    wr, wi = (sub_parts[:, n].astype(f32) * (1.0 / unit) for n in (2, 3))
 
     my_beam = lax.axis_index("beam")
     beam_ids = 2 * ((my_beam // 2 + jnp.arange(quads, dtype=jnp.int32)) % quads) + my_fft % 2
@@ -311,7 +310,7 @@
         functools.partial(window_kernel, ffts=ffts, quads=quads, unroll=64),
         out_shape=jax.ShapeDtypeStruct(out_shape, bf16),
         grid_spec=pltpu.PrefetchScalarGridSpec(
-            num_scalar_prefetch=8, grid=(quads,),
+            num_scalar_prefetch=5, grid=(quads,),
             in_specs=[whole(x) for x in fixed],
             out_specs=pl.BlockSpec(out_shape, lambda q, *_: (0,) * len(out_shape)),
             scratch_shapes=[
@@ -330,7 +329,7 @@
         ),
         compiler_params=pltpu.CompilerParams(vmem_limit_bytes=63 << 20),
         name="windows",
-    )(tix, tile_i, tile_j, valid, r0_all, c0_all, wr, wi, *fixed)
+    )(tix, tile_i, tile_j, valid, sub_parts, *fixed)
 
     groups = [[b * ffts + 2 * x + c for b in range(beams) for x in range(pairs)] for c in range(2)]
     parts = partial.reshape(beams * pairs, sub_dev, 2 * samples)

time: 131 us -> 130 us (level)
  transfers between devices with their start and end apart: 7 -> 7, of which waited for: 4 -> 4; matrix products, arithmetic and copies ran while one was open for 3% -> 2% of each run, Pallas kernels for 0% -> 0%
where the time goes in v8:
time: 130 us
  Pallas kernels  78.6 us (60%)
  starting transfers between devices  24.6 us (19%)
  waiting for transfers between devices  17.8 us (14%)
  other arithmetic  6.13 us (5%)
  local copies, waits for them, and re-layouts  1.52 us (1%)
    pallas_call x1, Pallas kernels, local(): pl.pallas_call(functools.partial(window_kernel, ffts=ffts, quads=quads, u...  78.6 us
    all_to_all x1, waiting for transfers between devices, local(): lax.all_to_all(parts, axes, 0, 0, tiled=True, axis_index_groups=groups)  11.2 us
    ppermute x4, starting transfers between devices, local(): smalls = [lax.ppermute(small, axes, turn(t)) for t in range(quads)]  10.2 us
    all_to_all x1, starting transfers between devices, local(): lax.all_to_all(parts, axes, 0, 0, tiled=True, axis_index_groups=groups)  7.27 us
    ppermute x1, starting transfers between devices, local(): total = lax.ppermute(total, axes, turn(0)) * (1.0 / image_side)  7.08 us
    ppermute x4, waiting for transfers between devices, local(): smalls = [lax.ppermute(small, axes, turn(t)) for t in range(quads)]  4.75 us
  transfers between devices with their start and end apart: 7, of which 4 were waited for; matrix products, arithmetic and copies ran while one was open for 2% of the time, Pallas kernels for 0%

profile of v8, /device:TPU:1, one launch (start us, length us, event | category | flops | bytes accessed | tf_op | source)
XLA Modules:
  0.0 129.7 jit_solution(12531516937991761119)
XLA Ops:
  0.0 0.0 copy-start
  0.7 0.8 multiply_convert_fusion
  1.5 1.0 fusion.3
  2.5 0.7 multiply_convert_fusion.1
  3.3 0.7 compare_select_fusion.6
  4.0 0.5 concatenate.3
  4.5 3.7 %collective-permute-start.3 = (s32[324,128]{1,0:T(8,128)S(1)}, s32[324,128]{1,0:T(8,128)S(1)}, u32[]{:S(2)}, u32[]{:S(2)}) collective-permute-start(s32[324,128]{1,0:T(8,128)S(1)} %concatenate.3), channel_id=1, source_target_pairs={{0,8},{1,12},{2,10},{3,14},{4,9},{5,13},{6,11},{7,15},{8,16},{9,20... | collective-permute-start | bytes 497672 | tf_op jit(solution)/shard_map/ppermute | solution.py:269
  8.2 2.0 %collective-permute-start.2 = (s32[324,128]{1,0:T(8,128)S(1)}, s32[324,128]{1,0:T(8,128)S(1)}, u32[]{:S(2)}, u32[]{:S(2)}) collective-permute-start(s32[324,128]{1,0:T(8,128)S(1)} %concatenate.3), channel_id=1, source_target_pairs={{0,16},{1,20},{2,18},{3,22},{4,17},{5,21},{6,19},{7,23},{8,24},{9,... | collective-permute-start | bytes 497672 | tf_op jit(solution)/shard_map/ppermute | solution.py:269
  10.2 2.6 %collective-permute-start.1 = (s32[324,128]{1,0:T(8,128)S(1)}, s32[324,128]{1,0:T(8,128)S(1)}, u32[]{:S(2)}, u32[]{:S(2)}) collective-permute-start(s32[324,128]{1,0:T(8,128)S(1)} %concatenate.3), channel_id=1, source_target_pairs={{0,24},{1,28},{2,26},{3,30},{4,25},{5,29},{6,27},{7,31},{8,0},{9,4... | collective-permute-start | bytes 497672 | tf_op jit(solution)/shard_map/ppermute | solution.py:269
  12.8 1.9 %collective-permute-start = (s32[324,128]{1,0:T(8,128)S(1)}, s32[324,128]{1,0:T(8,128)S(1)}, u32[]{:S(2)}, u32[]{:S(2)}) collective-permute-start(s32[324,128]{1,0:T(8,128)S(1)} %concatenate.3), channel_id=1, source_target_pairs={{0,0},{1,4},{2,2},{3,6},{4,1},{5,5},{6,3},{7,7},{8,8},{9,12},{10,1... | collective-permute-start | bytes 497672 | tf_op jit(solution)/shard_map/ppermute | solution.py:269
  14.7 0.1 collective-permute-start.4
  14.8 0.1 iota_compare_fusion.4
  14.9 0.8 select_reduce_fusion.5
  15.7 0.2 select_reduce_fusion
  15.9 1.0 select_reduce_fusion.1
  16.8 0.0 collective-permute-done.3.rest_3_
  16.8 0.0 copy-start.1
  16.8 4.7 %collective-permute-done.2.rest_2_ = s32[324,128]{1,0:T(8,128)S(1)} collective-permute-done((s32[324,128]{1,0:T(8,128)S(1)}, s32[324,128]{1,0:T(8,128)S(1)}, u32[]{:S(2)}, u32[]{:S(2)}) %collective-permute-start.2) | collective-permute-done | bytes 165920 | tf_op jit(solution)/shard_map/ppermute | solution.py:269
  21.5 0.0 copy-start.2
  21.5 0.0 collective-permute-done.1.rest_1_
  21.5 0.0 copy-start.3
  21.5 0.1 collective-permute-done.rest_0_
  21.6 0.0 copy-start.4
  21.6 0.7 pad_add_fusion.sub_ref
  22.3 0.0 collective-permute-done.4.oth_ref
  22.3 0.0 copy-done.1
  22.3 0.0 copy-done.2
  22.3 0.0 copy-done.3
  22.3 0.0 copy-done.4
  22.3 0.0 copy-start.7
  22.3 0.0 copy-start.5
  22.4 0.0 copy-start.6
  22.4 78.6 %windows.1 = bf16[4,2,2,32,512]{4,3,2,1,0:T(8,128)(2,1)} custom-call(s32[4,8]{1,0:T(4,128)} %get-tuple-element.8.tix_ref, s32[4,8]{1,0:T(4,128)} %get-tuple-element.7.ti_ref, s32[4,8]{1,0:T(4,128)} %get-tuple-element.6.tj_ref, s32[4,8]{1,0:T(4,128)} %get-tuple-element.5.valid_ref, s32[4,4,128]{2,1,0:T(4,128)} %pad_add_fusion.sub_ref, ...), custom_call_target="tpu_custom_call" | custom-call | tf_op jit(solution)/shard_map/windows/pallas_call | solution.py:309
  101.0 7.3 %all-to-all-start = ((bf16[16,32,512]{2,1,0:T(8,128)(2,1)}), bf16[16,32,512]{2,1,0:T(8,128)(2,1)S(1)}, u32[]{:S(2)}, u32[]{:S(2)}) async-start(bf16[16,32,512]{2,1,0:T(8,128)(2,1)} %bitcast.43), calls=%async_computation | async-start | bytes 1048576 | tf_op jit(solution)/shard_map/all_to_all | solution.py:336
  108.2 0.0 copy-done.7
  108.2 0.1 dynamic-slice_bitcast_fusion
  108.3 0.0 copy-done
  108.3 0.2 fusion.7
  108.5 11.2 %all-to-all-done = bf16[16,32,512]{2,1,0:T(8,128)(2,1)S(1)} async-done(((bf16[16,32,512]{2,1,0:T(8,128)(2,1)}), bf16[16,32,512]{2,1,0:T(8,128)(2,1)S(1)}, u32[]{:S(2)}, u32[]{:S(2)}) %all-to-all-start) | async-done | bytes 524320 | tf_op jit(solution)/shard_map/all_to_all | solution.py:336
  119.7 0.1 convert_reduce_fusion
  119.8 7.1 %collective-permute-start.5 = (f32[32,512]{1,0:T(8,128)S(1)}, f32[32,512]{1,0:T(8,128)S(1)}, u32[]{:S(2)}, u32[]{:S(2)}) collective-permute-start(f32[32,512]{1,0:T(8,128)S(1)} %convert_reduce_fusion), channel_id=1, source_target_pairs={{0,0},{1,4},{2,2},{3,6},{4,1},{5,5},{6,3},{7,7},{8,8},{9,12},{10,1... | collective-permute-start | bytes 196616 | tf_op jit(solution)/shard_map/ppermute | solution.py:338
  126.9 0.0 copy-done.5
  126.9 0.0 copy-done.6
  126.9 0.1 dynamic_slice.12
  127.0 1.8 %collective-permute-done.5 = f32[32,512]{1,0:T(8,128)S(1)} collective-permute-done((f32[32,512]{1,0:T(8,128)S(1)}, f32[32,512]{1,0:T(8,128)S(1)}, u32[]{:S(2)}, u32[]{:S(2)}) %collective-permute-start.5) | collective-permute-done | bytes 65568 | tf_op jit(solution)/shard_map/ppermute | solution.py:338
  128.9 0.1 fusion.22
  128.9 0.1 multiply_subtract_fusion
  129.0 0.7 copy.24
  (18 shorter events, 0.2 us)
Async XLA Ops:
  0.0 108.3 %copy-start = (f32[2,630]{1,0:T(2,128)S(1)}, f32[2,630]{1,0:T(2,128)}, u32[]{:S(2)}) copy-start(f32[2,630]{1,0:T(2,128)} %param.25) | copy-start | bytes 15124
  4.5 12.3 %collective-permute-start.3 = (s32[324,128]{1,0:T(8,128)S(1)}, s32[324,128]{1,0:T(8,128)S(1)}, u32[]{:S(2)}, u32[]{:S(2)}) collective-permute-start(s32[324,128]{1,0:T(8,128)S(1)} %concatenate.3), channel_id=1, source_target_pairs={{0,8},{1,12},{2,10},{3,14},{4,9},{5,13},{6,11},{7,15},{8,16},{9,20... | collective-permute-start | bytes 497672 | tf_op jit(solution)/shard_map/ppermute | solution.py:269
  8.2 13.3 %collective-permute-start.2 = (s32[324,128]{1,0:T(8,128)S(1)}, s32[324,128]{1,0:T(8,128)S(1)}, u32[]{:S(2)}, u32[]{:S(2)}) collective-permute-start(s32[324,128]{1,0:T(8,128)S(1)} %concatenate.3), channel_id=1, source_target_pairs={{0,16},{1,20},{2,18},{3,22},{4,17},{5,21},{6,19},{7,23},{8,24},{9,... | collective-permute-start | bytes 497672 | tf_op jit(solution)/shard_map/ppermute | solution.py:269
  10.2 11.3 %collective-permute-start.1 = (s32[324,128]{1,0:T(8,128)S(1)}, s32[324,128]{1,0:T(8,128)S(1)}, u32[]{:S(2)}, u32[]{:S(2)}) collective-permute-start(s32[324,128]{1,0:T(8,128)S(1)} %concatenate.3), channel_id=1, source_target_pairs={{0,24},{1,28},{2,26},{3,30},{4,25},{5,29},{6,27},{7,31},{8,0},{9,4... | collective-permute-start | bytes 497672 | tf_op jit(solution)/shard_map/ppermute | solution.py:269
  12.8 8.8 %collective-permute-start = (s32[324,128]{1,0:T(8,128)S(1)}, s32[324,128]{1,0:T(8,128)S(1)}, u32[]{:S(2)}, u32[]{:S(2)}) collective-permute-start(s32[324,128]{1,0:T(8,128)S(1)} %concatenate.3), channel_id=1, source_target_pairs={{0,0},{1,4},{2,2},{3,6},{4,1},{5,5},{6,3},{7,7},{8,8},{9,12},{10,1... | collective-permute-start | bytes 497672 | tf_op jit(solution)/shard_map/ppermute | solution.py:269
  14.7 7.6 %collective-permute-start.4 = (bf16[16,128,512]{2,1,0:T(8,128)(2,1)}, bf16[16,128,512]{2,1,0:T(8,128)(2,1)}, u32[]{:S(2)}, u32[]{:S(2)}) collective-permute-start(bf16[16,128,512]{2,1,0:T(8,128)(2,1)} %own_ref.1), channel_id=1, source_target_pairs={{0,1},{1,0},{2,3},{3,2},{4,5},{5,4},{6,7},{7,6},{8,9},{9,8},{10,11... | collective-permute-start | bytes 6291464 | tf_op jit(solution)/shard_map/ppermute | solution.py:251
  16.8 5.5 %copy-start.1 = (s32[324,128]{1,0:T(8,128)}, s32[324,128]{1,0:T(8,128)S(1)}, u32[]{:S(2)}) copy-start(s32[324,128]{1,0:T(8,128)S(1)} %collective-permute-done.3.rest_3_) | copy-start | bytes 497668
  21.5 0.8 copy-start.2
  21.5 0.8 copy-start.3
  21.6 0.7 copy-start.4
  22.3 85.9 %copy-start.7 = (s32[1,128]{1,0:T(1,128)S(1)}, s32[1,128]{1,0:T(1,128)}, u32[]{:S(2)}) copy-start(s32[1,128]{1,0:T(1,128)} %param.24) | copy-start | bytes 1540
  22.3 104.5 %copy-start.5 = (s32[1,128]{1,0:T(1,128)S(1)}, s32[1,128]{1,0:T(1,128)}, u32[]{:S(2)}) copy-start(s32[1,128]{1,0:T(1,128)} %param.22) | copy-start | bytes 1540
  22.4 104.5 %copy-start.6 = (s32[1,128,1]{1,2,0:T(1,128)S(1)}, s32[1,128,1]{1,2,0:T(1,128)}, u32[]{:S(2)}) copy-start(s32[1,128,1]{1,2,0:T(1,128)} %param.20) | copy-start | bytes 1540
  101.0 18.8 %all-to-all-start = ((bf16[16,32,512]{2,1,0:T(8,128)(2,1)}), bf16[16,32,512]{2,1,0:T(8,128)(2,1)S(1)}, u32[]{:S(2)}, u32[]{:S(2)}) async-start(bf16[16,32,512]{2,1,0:T(8,128)(2,1)} %bitcast.43), calls=%async_computation | async-start | bytes 1048576 | tf_op jit(solution)/shard_map/all_to_all | solution.py:336
  119.8 9.0 %collective-permute-start.5 = (f32[32,512]{1,0:T(8,128)S(1)}, f32[32,512]{1,0:T(8,128)S(1)}, u32[]{:S(2)}, u32[]{:S(2)}) collective-permute-start(f32[32,512]{1,0:T(8,128)S(1)} %convert_reduce_fusion), channel_id=1, source_target_pairs={{0,0},{1,4},{2,2},{3,6},{4,1},{5,5},{6,3},{7,7},{8,8},{9,12},{10,1... | collective-permute-start | bytes 196616 | tf_op jit(solution)/shard_map/ppermute | solution.py:338
